TPU v7x, 32 devices: a whole 2x2x4 slice. The times are simulated.
32 devices in a mesh: view: 4 (over x, core), patch: 8 (over z, y).
Axes of the slice: x: 2, y: 2, z: 4, core: 2. Of those that a mesh axis runs over, the one named last changes fastest.
Arguments:
- queries: bfloat16 [4096, 768], P(('view', 'patch')), may hold values from -6 to 6
- key_rows: bfloat16 [4096, 768], P(('view', 'patch')), may hold values from -6 to 6
- value_rows: bfloat16 [4096, 768], P(('view', 'patch')), may hold values from -6 to 6
- step_rates: float32 [4096, 4], P(('view', 'patch')), may hold values from 0.5 to 18, as said below
- fast_init: float32 [192, 4608], replicated, may hold values from -2.598076 to 2.598076
- out_grad: bfloat16 [4096, 768], P(('view', 'patch')), may hold values from -6 to 6
Outputs:
- query_grad: bfloat16 [4096, 768], P(('view', 'patch'))
- key_grad: bfloat16 [4096, 768], P(('view', 'patch'))
- value_grad: bfloat16 [4096, 768], P(('view', 'patch'))
- rate_grad: float32 [4096, 4], P(('view', 'patch'))
- fast_grad: float32 [192, 4608], P(None, ('view', 'patch'))
Inputs may be any that keep to these rules, and one draw needn't show every extreme that they name: `step_rates`: positive learning rates.
All inputs are finite; a program needn't handle non-finite values.
Results may differ from a plain program's by a relative error of at most 0.0023.
Values sent between devices are 32-bit elements; how exact they have to be, the bound alone decides.
No kernel may reach another device: no remote copies, remote signals or barrier semaphores. Data moves between devices by JAX's collectives and lax.ppermute only.
A program may use at most 128 MiB of HBM per device.

v0:
```python
import functools
import math

import jax
import jax.numpy as jnp
from jax import lax
from jax.experimental import pallas as pl
from jax.experimental.pallas import tpu as pltpu
from jax.sharding import PartitionSpec as P


AXES = ("view", "patch")
step_size = 0.2
epsilon = 1e-06
F32, BF16 = jnp.float32, jnp.bfloat16
LANES, SUBLANES = 128, 8


class Layout:
    def __init__(self, views, patches, heads, hidden, head_dim):
        self.heads, self.head_dim, self.hidden = heads, head_dim, hidden
        self.cores = 2 if views % 2 == 0 else 1
        self.patches, self.devices = patches, views * patches
        self.sub = patches // heads
        self.plane = (views // self.cores) * self.sub
        self.half = hidden // self.cores
        self.slot = self.half // self.plane
        self.pow2 = self.plane & (self.plane - 1) == 0
        rows = 3 * self.slot
        self.packed = (
            head_dim == LANES + LANES // 2
            and rows % (2 * SUBLANES) == 0
            and (3 * self.half) % (4 * SUBLANES) == 0
            and self.pow2
            and self.plane > 1
        )

    def place(self, device):
        view, patch = divmod(device, self.patches)
        outer, core = divmod(view, self.cores)
        head, sub = divmod(patch, self.sub)
        return outer * self.sub + sub, core, head

    def device(self, member, core, head):
        outer, sub = divmod(member, self.sub)
        return (outer * self.cores + core) * self.patches + head * self.sub + sub

    def target(self, member, step):
        return member ^ step if self.pow2 else (member + step) % self.plane

    def origin(self, member, step):
        return member ^ step if self.pow2 else (member - step) % self.plane

    def perm(self, move):
        return [(i, self.device(*move(*self.place(i)))) for i in range(self.devices)]

    def core_perm(self):
        return self.perm(lambda j, c, h: (j, (c + 1) % self.cores, h))

    def head_perm(self, shift):
        return self.perm(lambda j, c, h: (j, c, (h + shift) % self.heads))

    def scatter_perm(self, step):
        return self.perm(lambda j, c, h: (self.target(j, step), c, h))

    def gather_perm(self, step):
        return self.perm(lambda j, c, h: (self.origin(j, step), c, h))

    def flip_perm(self, bit):
        return self.perm(lambda j, c, h: (j ^ bit, c, h))

    def owner_rounds(self):
        count = self.devices
        edges = []
        for i in range(count):
            j, c, h = self.place(i)
            for m in range(3):
                piece = (m * self.heads + h) * self.cores * self.plane + c * self.plane + j
                edges.append((i, piece // 3, m, piece % 3))
        left, rounds = list(edges), []
        for _ in range(3):
            out_edges = [[] for _ in range(count)]
            for edge in left:
                out_edges[edge[0]].append(edge)
            match = {}

            def place_one(i, seen):
                for edge in out_edges[i]:
                    if edge[1] in seen:
                        continue
                    seen.add(edge[1])
                    if edge[1] not in match or place_one(match[edge[1]][0], seen):
                        match[edge[1]] = edge
                        return True
                return False

            for i in range(count):
                place_one(i, set())
            chosen = sorted(match.values())
            rounds.append(chosen)
            left = [edge for edge in left if edge not in match.values()]
        return rounds


def split(lay, x):
    if not lay.packed:
        return (x,)
    high = x.astype(BF16)
    return high, (x - high.astype(F32)).astype(BF16)


def dot(a, b, dims, precision=None):
    return lax.dot_general(
        a, b, (dims, ((), ())), precision=precision, preferred_element_type=F32
    )


NN, NT = ((1,), (0,)), ((1,), (1,))


def dot_left(parts, exact, dims):
    if len(parts) == 1:
        return dot(parts[0], exact, dims, lax.Precision.HIGH)
    return dot(parts[0], exact, dims) + dot(parts[1], exact, dims)


def dot_both(a, b, dims):
    if len(a) == 1:
        return dot(a[0], b[0], dims, lax.Precision.HIGH)
    return dot(a[0], b[0], dims) + (dot(a[0], b[1], dims) + dot(a[1], b[0], dims))


def gates(act):
    sig = 1.0 / (1.0 + jnp.exp(-act))
    silu = act * sig
    rest = 1.0 - sig
    return sig, silu, rest, sig + silu * rest


def cat(parts, axis):
    return jnp.concatenate(parts, axis)


def pack(lay, body, extra):
    if not lay.packed:
        return cat([body, jnp.broadcast_to(extra, (SUBLANES, lay.head_dim))], 0)
    rows = body.shape[0]
    tail = body[:, LANES:]
    tail = cat([tail[: rows // 2], tail[rows // 2 :]], 1)
    return cat([body[:, :LANES], tail, jnp.broadcast_to(extra, (SUBLANES, LANES))], 0)


def unpack(lay, payload, rows=None):
    rows = 3 * lay.slot if rows is None else rows
    if not lay.packed:
        return payload[:rows], payload[rows : rows + 1, :1]
    tail = payload[rows : rows + rows // 2]
    half = LANES // 2
    tail = cat([tail[:, :half], tail[:, half:]], 0)
    return cat([payload[:rows], tail], 1), payload[rows + rows // 2 : rows + rows // 2 + 1, :1]


def pack_halves(lay, grads, extra):
    body = cat(grads, 0)
    rows = body.shape[0] // 2
    return [pack(lay, body[:rows], extra), pack(lay, body[rows:], extra)]


def unpack_halves(lay, first, first_in, second, second_in):
    rows = 3 * lay.half // 2
    top, extra = unpack(lay, first + first_in, rows)
    bottom, _ = unpack(lay, second + second_in, rows)
    return cat([top, bottom], 0), extra


def in_slots(lay, parts):
    slot = lay.slot
    return [cat([p[k * slot : (k + 1) * slot] for p in parts], 0) for k in range(lay.plane)]


def member_id(places):
    return places[0:1, 6:7]


def choose(pieces, index):
    result = pieces[0]
    for i in range(1, len(pieces)):
        result = jnp.where(index == i, pieces[i], result)
    return result


def in_three(lay, body):
    return [body[m * lay.half : (m + 1) * lay.half] for m in range(3)]


def pack_all(lay, grads, extra):
    outs = []
    for step in range(lay.plane):
        take = slice(step * lay.slot, (step + 1) * lay.slot)
        outs.append(pack(lay, cat([g[take] for g in grads], 0), extra))
    return outs


def unpack_all(lay, payloads):
    bodies = [unpack(lay, p)[0] for p in payloads]
    slot = lay.slot
    return [cat([b[m * slot : (m + 1) * slot] for b in bodies], 0) for m in range(3)]


def select_heads(lay, pieces, head_ids, shift):
    wanted = lax.rem(head_ids[0:1, :] + shift, lay.heads)
    result = pieces[0]
    for h in range(1, lay.heads):
        result = jnp.where(wanted == h, pieces[h], result)
    return result


def spread_rows(lay, with_rates, first, second, *rest):
    dim = lay.head_dim
    head_ids = rest[-1]
    turned = [x.astype(F32).T for x in (first, second)]
    pieces = [[t[h * dim : (h + 1) * dim] for h in range(lay.heads)] for t in turned]
    if with_rates:
        rates = rest[0]
        rows = rates.shape[1]
        pieces.append(
            [jnp.broadcast_to(rates[h : h + 1], (SUBLANES, rows)) for h in range(lay.heads)]
        )
    return [
        cat([select_heads(lay, p, head_ids, shift) for p in pieces], 0)
        for shift in range(lay.heads)
    ]


def join_rows(lay, slabs):
    dim = lay.head_dim
    kind = BF16 if lay.packed else F32
    first = cat([s[:dim] for s in slabs], 1).astype(kind)
    second = cat([s[dim : 2 * dim] for s in slabs], 1).astype(kind)
    return first, second


def join_rates(lay, slabs):
    dim = lay.head_dim
    return cat([s[2 * dim : 2 * dim + 1] for s in slabs], 1)


def update_math(lay, slabs, weights):
    keys, values = join_rows(lay, slabs)
    rates = join_rates(lay, slabs)
    gate, up, down = (split(lay, w) for w in in_three(lay, weights))
    a = dot_left(gate, keys, NN)
    b = dot_left(up, keys, NN)
    u = dot_left(down, values, NN)
    _, silu, _, slope = gates(a)
    mu = -rates * u
    d_gate = dot_left(split(lay, mu * b * slope), keys, NT)
    d_up = dot_left(split(lay, mu * silu), keys, NT)
    d_down = dot_left(split(lay, -rates * (silu * b)), values, NT)
    return [d_gate, d_up, d_down], jnp.sum(rates, 1, keepdims=True)


def update_fn(lay, weights, *slabs):
    grads, total = update_math(lay, slabs, weights)
    return pack_all(lay, grads, total)


def update_near_fn(lay, weights, *slabs):
    grads, total = update_math(lay, slabs, weights)
    return [cat(grads, 0), jnp.broadcast_to(total, (SUBLANES, LANES))]


def update_rest_fn(lay, weights, before, total_before, *slabs):
    grads, total = update_math(lay, slabs, weights)
    grads = [g + b for g, b in zip(grads, in_three(lay, before))]
    return pack_halves(lay, grads, total + total_before[0:1, 0:1])


def norms(initial, moved):
    norm = jnp.sqrt(jnp.sum(initial * initial, 1, keepdims=True) + epsilon)
    inverse = lax.rsqrt(jnp.sum(moved * moved, 1, keepdims=True) + epsilon)
    return norm, inverse


def renormed(coefficient, body, total, initial):
    grad = body * (coefficient / total)
    moved = initial - grad
    norm, inverse = norms(initial, moved)
    return moved * (norm * inverse), grad, moved


def renorm_fn(lay, coefficient, *args):
    payloads, initial = args[:-1], args[-1]
    body, total = unpack(lay, functools.reduce(jnp.add, payloads))
    new, grad, moved = renormed(coefficient, body, total, initial)
    return [pack(lay, new, total), grad, moved]


def renorm_all_fn(lay, coefficient, *args):
    body, total = unpack_halves(lay, *args[:4])
    new, grad, moved = renormed(coefficient, body, total, args[4])
    return [new, grad, moved, jnp.broadcast_to(total, (SUBLANES, LANES))]


def apply_fn(lay, *args):
    if lay.packed:
        weights, slabs = in_three(lay, args[0]), args[1:]
    else:
        weights, slabs = unpack_all(lay, args[: lay.plane]), args[lay.plane :]
    queries, cotangents = join_rows(lay, slabs)
    gate, up, down = (split(lay, w) for w in weights)
    a = dot_left(gate, queries, NN)
    b = dot_left(up, queries, NN)
    u = dot_left(down, cotangents, NN)
    _, silu, _, slope = gates(a)
    da = split(lay, u * b * slope)
    db = split(lay, u * silu)
    h = split(lay, silu * b)
    d_gate = dot_left(da, queries, NT)
    d_up = dot_left(db, queries, NT)
    d_down = dot_left(h, cotangents, NT)
    outs = (pack_halves if lay.packed else pack_all)(
        lay, (d_gate, d_up, d_down), jnp.zeros((1, 1), F32)
    )
    turned = split(lay, cat([weights[0], weights[1]], 0).T)
    both = tuple(cat([x, y], 0) for x, y in zip(da, db))
    d_query = dot_both(turned, both, NN)
    rows = slabs[0].shape[1]
    cut = [d_query[:, i * rows : (i + 1) * rows] for i in range(len(slabs))]
    heads = lay.heads
    return outs + cut[:heads] + ([stack(cut[heads:])] if lay.cores > 1 else [])


def stack(parts):
    return cat([p[None] for p in parts], 0)


def renormed_back(coefficient, d_new, total, initial, grad, moved):
    norm, inverse = norms(initial, moved)
    dots = jnp.sum(d_new * moved, 1, keepdims=True)
    d_moved = d_new * (norm * inverse) - moved * (dots * norm * inverse * inverse * inverse)
    direct = d_moved + initial * (dots * inverse / norm)
    d_update = -d_moved
    part = jnp.sum(jnp.sum(d_update * grad, 1, keepdims=True), 0, keepdims=True)
    return d_update * (coefficient / total), -part / total, direct


def renorm_back_fn(lay, coefficient, *args):
    payloads = args[: lay.plane]
    total_payload, initial, grad, moved = args[lay.plane :]
    d_new, _ = unpack(lay, functools.reduce(jnp.add, payloads))
    _, total = unpack(lay, total_payload)
    move, d_total, direct = renormed_back(coefficient, d_new, total, initial, grad, moved)
    return [pack(lay, move, d_total), direct]


def renorm_back_all_fn(lay, coefficient, *args):
    d_new, _ = unpack_halves(lay, *args[:4])
    initial, grad, moved, total, places = args[4:]
    move, d_total, direct = renormed_back(
        coefficient, d_new, total[0:1, 0:1], initial, grad, moved
    )
    own = choose(in_slots(lay, in_three(lay, direct)), member_id(places))
    return [move, jnp.broadcast_to(d_total, (SUBLANES, LANES)), own]


def pull_math(lay, slabs, weights, moves, d_total):
    keys, values = join_rows(lay, slabs)
    rates = join_rates(lay, slabs)
    gate, up, down = (split(lay, w) for w in weights)
    gate_move, up_move, down_move = (split(lay, w) for w in moves)
    a = dot_left(gate, keys, NN)
    b = dot_left(up, keys, NN)
    u = dot_left(down, values, NN)
    ta = dot_left(gate_move, keys, NN)
    tb = dot_left(up_move, keys, NN)
    w = dot_left(down_move, values, NN)
    sig, silu, rest, slope = gates(a)
    bend = sig * rest * (2.0 + a * (rest - sig))
    hidden = silu * b
    hidden_dot = slope * ta * b + silu * tb
    rate_part = -jnp.sum(w * hidden + u * hidden_dot, 0, keepdims=True) + d_total
    mu = -rates
    wm, um = mu * w, mu * u
    ga = split(lay, wm * b * slope + um * (bend * ta * b + slope * tb))
    gb = split(lay, wm * silu + um * slope * ta)
    gta = split(lay, um * slope * b)
    gtb = split(lay, um * silu)
    mh = split(lay, mu * hidden)
    md = split(lay, mu * hidden_dot)
    grads = [dot_left(ga, keys, NT), dot_left(gb, keys, NT), dot_left(md, values, NT)]
    turned = split(lay, cat([weights[0], weights[1], moves[0], moves[1]], 0).T)
    d_key = dot_both(turned, tuple(cat(x, 0) for x in zip(ga, gb, gta, gtb)), NN)
    turned = split(lay, cat([moves[2], weights[2]], 0).T)
    d_value = dot_both(turned, tuple(cat(x, 0) for x in zip(mh, md)), NN)
    rows = slabs[0].shape[1]
    parts = []
    for i in range(len(slabs)):
        take = slice(i * rows, (i + 1) * rows)
        rate_rows = jnp.broadcast_to(rate_part[:, take], (SUBLANES, rows))
        parts.append(cat([d_key[:, take], d_value[:, take], rate_rows], 0))
    return grads, parts


def pull_fn(lay, *args):
    payloads, slabs, weights = args[: lay.plane], args[lay.plane : -1], args[-1]
    d_total = functools.reduce(jnp.add, [unpack(lay, p)[1] for p in payloads])
    grads, parts = pull_math(
        lay, slabs, in_three(lay, weights), unpack_all(lay, payloads), d_total
    )
    outs = pack_all(lay, grads, jnp.zeros((1, 1), F32))
    heads = lay.heads
    return outs + parts[:heads] + ([stack(parts[heads:])] if lay.cores > 1 else [])


def pull_other_fn(lay, *args):
    moves, d_total, weights, slabs = args[0], args[1], args[2], args[3:]
    grads, parts = pull_math(
        lay, slabs, in_three(lay, weights), in_three(lay, moves), d_total[0:1, 0:1]
    )
    return [stack(parts), cat(grads, 0)]


def pull_own_fn(lay, *args):
    moves, d_total, weights, before, places, slabs = *args[:5], args[5:]
    grads, parts = pull_math(
        lay, slabs, in_three(lay, weights), in_three(lay, moves), d_total[0:1, 0:1]
    )
    grads = [g + b for g, b in zip(grads, in_three(lay, before))]
    slots, member = in_slots(lay, grads), member_id(places)
    zero = jnp.zeros((1, 1), F32)
    return [pack(lay, choose(slots, member ^ r), zero) for r in range(lay.plane)] + parts


def add_two_fn(first, first_in, second, second_in):
    return [first + first_in, second + second_in]


def finish_fn(lay, count, *args):
    slabs, head_ids = args[:-1], args[-1]
    dim = lay.head_dim
    outs = []
    for n in range(count):
        pieces = [s[n * dim : (n + 1) * dim] for s in slabs]
        ordered = [
            select_heads(lay, pieces, lay.heads - head_ids, h) for h in range(lay.heads)
        ]
        outs.append(cat(ordered, 0).T.astype(BF16))
    if slabs[0].shape[0] > count * dim:
        pieces = [s[count * dim : count * dim + 1] for s in slabs]
        rows = [select_heads(lay, pieces, lay.heads - head_ids, h) for h in range(lay.heads)]
        outs.append(cat(rows, 0))
    return outs


def add_fn(*args):
    return [part + args[-1][i] for i, part in enumerate(args[:-1])]


def total_fn(lay, scale, *args):
    payloads, direct, places = args[: lay.plane], args[-2], args[-1]
    body, _ = unpack(lay, functools.reduce(jnp.add, payloads))
    final = (body + direct) / scale
    pieces = [final[m * lay.slot : (m + 1) * lay.slot] for m in range(3)]
    return [choose(pieces, places[0:1, t : t + 1]) for t in range(3)]


def place_fn(*args):
    pieces, places = args[:3], args[3]
    return [cat([choose(pieces, places[0:1, 3 + q : 4 + q]) for q in range(3)], 0)]


VMEM_LIMIT = 24 * 1024 * 1024


def run(lay, fn, args, always=False, deps=()):
    if not (lay.packed or always):
        return fn(*args)
    shapes = jax.eval_shape(fn, *args)
    deps = [x[: min(SUBLANES, x.shape[0])] for x in deps]
    count = len(args)

    def kernel(*refs):
        ins, outs = refs[:count], refs[count + len(deps) :]
        for ref, value in zip(outs, fn(*[r[...] for r in ins])):
            ref[...] = value

    vmem = pl.BlockSpec(memory_space=pltpu.VMEM)
    return pl.pallas_call(
        kernel,
        out_shape=[jax.ShapeDtypeStruct(s.shape, s.dtype) for s in shapes],
        in_specs=[vmem] * (count + len(deps)),
        out_specs=[vmem] * len(shapes),
        compiler_params=pltpu.CompilerParams(vmem_limit_bytes=VMEM_LIMIT),
    )(*args, *deps)


def tie(lay, arrays, deps):
    if not lay.packed:
        return arrays
    deps = [x[:SUBLANES] for x in deps]
    vmem = pl.BlockSpec(memory_space=pltpu.VMEM)
    return list(
        pl.pallas_call(
            lambda *refs: None,
            out_shape=[jax.ShapeDtypeStruct(a.shape, a.dtype) for a in arrays],
            in_specs=[vmem] * (len(arrays) + len(deps)),
            out_specs=[vmem] * len(arrays),
            input_output_aliases={i: i for i in range(len(arrays))},
            compiler_params=pltpu.CompilerParams(vmem_limit_bytes=VMEM_LIMIT),
        )(*arrays, *deps)
    )


def on_device(lay, queries, key_rows, value_rows, step_rates, fast_init, out_grad):
    head_dim, _ = fast_init.shape
    heads, slot, plane = lay.heads, lay.slot, lay.plane
    coefficient = step_size * math.sqrt(queries.shape[0] * lay.devices)
    view, patch = lax.axis_index("view"), lax.axis_index("patch")
    core = lax.rem(view, lay.cores)
    head = patch // lay.sub
    member = view // lay.cores * lay.sub + lax.rem(patch, lay.sub)
    me = view * lay.patches + patch
    head_ids = jnp.full((SUBLANES, LANES), head, jnp.int32)

    def send(x, perm):
        return lax.ppermute(x, AXES, perm)

    def over_heads(slabs):
        return [slabs[0]] + [send(slabs[t], lay.head_perm(t)) for t in range(1, heads)]

    def over_cores(slabs):
        return [send(x, lay.core_perm()) for x in slabs] if lay.cores > 1 else []

    def total_rows(parts):
        if lay.cores == 1:
            return parts
        return run(lay, add_fn, (*parts[:heads], send(parts[heads], lay.core_perm())))

    def back_home(slabs):
        return [slabs[0]] + [send(slabs[t], lay.head_perm(heads - t)) for t in range(1, heads)]

    def scatter(payloads):
        moved = [send(payloads[r], lay.scatter_perm(r)) for r in range(1, plane)]
        return [payloads[0]] + moved

    def gather(payload):
        return [payload] + [send(payload, lay.gather_perm(r)) for r in range(1, plane)]

    fn = functools.partial
    scale = math.sqrt(queries.shape[0] * lay.devices)
    kv = over_heads(
        run(
            lay,
            fn(spread_rows, lay, True),
            (key_rows, value_rows, step_rates.T, head_ids),
            always=True,
        )
    )
    qg = run(
        lay, fn(spread_rows, lay, False), (queries, out_grad, head_ids), always=True, deps=(kv[1],)
    )
    qg = over_heads(qg)
    kv = kv + over_cores(kv)

    owner_perms, table = owner_plan(lay)
    places = lax.dynamic_slice_in_dim(jnp.array(table, jnp.int32), me, 1, 0)
    first = head * lay.hidden + core * lay.half
    turned = []
    for m in range(3):
        part = lax.dynamic_slice_in_dim(fast_init, m * heads * lay.hidden + first, lay.half, 1)
        turned.append(part.T)
    if not lay.packed:
        order = jnp.stack([lay.target(member, r) for r in range(plane)])
        turned = [
            t.reshape(plane, slot, head_dim)[order].reshape(lay.half, head_dim) for t in turned
        ]
    weights = jnp.concatenate(turned, 0)

    def exchange(first, second):
        bits = [1 << i for i in range(plane.bit_length() - 1)]
        turned_bits = bits[1:] + bits[:1]
        for i, (one, two) in enumerate(zip(bits, turned_bits)):
            if i:
                first, second = run(lay, add_two_fn, (first, first_in, second, second_in))
            first_in = send(first, lay.flip_perm(one))
            second_in = send(second, lay.flip_perm(two))
        return first, first_in, second, second_in

    if lay.packed:
        near = (heads + 1) // 2
        before = run(lay, fn(update_near_fn, lay), (weights, *kv[:near]), deps=(places,))
        rest = run(lay, fn(update_rest_fn, lay), (weights, *before, *kv[near:]))
        sums = exchange(*rest)
        qg = tie(lay, qg, (sums[0],))
        qg = qg + over_cores(qg)
        renewed, grad, moved, total = run(
            lay, fn(renorm_all_fn, lay, coefficient), (*sums, weights)
        )
        applied = run(lay, fn(apply_fn, lay), (renewed, *qg))
        query_home = total_rows(applied[2:])
        sums = exchange(*applied[:2])
        move, d_total, direct = run(
            lay,
            fn(renorm_back_all_fn, lay, coefficient),
            (*sums, weights, grad, moved, total, places),
        )
        query_home = back_home(query_home)
        if lay.cores > 1:
            other, before = run(lay, fn(pull_other_fn, lay), (move, d_total, weights, *kv[heads:]))
        else:
            other, before = None, jnp.zeros_like(weights)
        pulled = run(
            lay, fn(pull_own_fn, lay), (move, d_total, weights, before, places, *kv[:heads])
        )
        pulled = [*pulled, other]
    else:
        own = jnp.concatenate([t[:slot] for t in turned], 0)
        sums = scatter(run(lay, fn(update_fn, lay), (weights, *kv)))
        payload, grad, moved = run(lay, fn(renorm_fn, lay, coefficient), (*sums, own))
        qg = qg + over_cores(qg)
        applied = run(lay, fn(apply_fn, lay), (*gather(payload), *qg))
        sums = scatter(applied[:plane])
        query_home = back_home(total_rows(applied[plane:]))
        d_payload, direct = run(
            lay, fn(renorm_back_fn, lay, coefficient), (*sums, payload, own, grad, moved)
        )
        pulled = run(lay, fn(pull_fn, lay), (*gather(d_payload), *kv, weights))
    key_home = total_rows(pulled[plane:])
    sums = scatter(pulled[:plane])
    pieces = run(lay, fn(total_fn, lay, scale), (*sums, direct, places), deps=tuple(key_home))
    key_home = back_home(key_home)
    (query_grad,) = run(
        lay, fn(finish_fn, lay, 1), (*query_home, head_ids), always=True, deps=tuple(pulled[:1])
    )
    arrived = [send(x, perm) for x, perm in zip(pieces, owner_perms)]
    (fast_grad,) = run(lay, place_fn, (*arrived, places))
    key_grad, value_grad, rate_grad = run(
        lay, fn(finish_fn, lay, 2), (*key_home, head_ids), always=True
    )
    return query_grad, key_grad, value_grad, rate_grad.T, fast_grad.T


def owner_plan(lay):
    rounds = lay.owner_rounds()
    table = [[0] * LANES for _ in range(lay.devices)]
    for t, chosen in enumerate(rounds):
        for source, owner, m, spot in chosen:
            table[source][t] = m
            table[owner][3 + spot] = t
            table[source][6] = lay.place(source)[0]
    return [[(i, o) for i, o, _, _ in chosen] for chosen in rounds], table


def solution(mesh):
    rows = P(AXES, None)

    def whole(queries, key_rows, value_rows, step_rates, fast_init, out_grad):
        heads = step_rates.shape[1]
        head_dim, columns = fast_init.shape
        lay = Layout(
            mesh.shape["view"], mesh.shape["patch"], heads, columns // (3 * heads), head_dim
        )

        def body(*args):
            return on_device(lay, *args)

        return jax.shard_map(
            body,
            mesh=mesh,
            in_specs=(rows, rows, rows, rows, P(), rows),
            out_specs=(rows, rows, rows, rows, P(None, AXES)),
            check_vma=False,
        )(queries, key_rows, value_rows, step_rates, fast_init, out_grad)

    return whole
```

profile of v0, /device:TPU:0, one launch (start us, length us, event | category | flops | bytes accessed | tf_op | source)
XLA Modules:
  0.0 129.0 jit_solution(3963196233040293191)
XLA Ops:
  0.7 0.9 copy-done
  1.6 0.9 copy-done.1
  2.5 0.7 copy-done.4
  3.4 3.1 %collective-permute-start = (f32[392,128]{1,0:T(8,128)S(1)}, f32[392,128]{1,0:T(8,128)S(1)}, u32[]{:S(2)}, u32[]{:S(2)}) collective-permute-start(f32[392,128]{1,0:T(8,128)S(1)} %get-tuple-element.64), channel_id=1, source_target_pairs={{0,2},{1,3},{2,4},{3,5},{4,6},{5,7},{6,0},{7,1},{8,10},{9,11},{10,... | collective-permute-start | bytes 602120 | tf_op jit(solution)/shard_map/ppermute | solution.py:527
  6.5 2.6 %collective-permute-start.1 = (f32[392,128]{1,0:T(8,128)S(1)}, f32[392,128]{1,0:T(8,128)S(1)}, u32[]{:S(2)}, u32[]{:S(2)}) collective-permute-start(f32[392,128]{1,0:T(8,128)S(1)} %get-tuple-element.67), channel_id=1, source_target_pairs={{0,4},{1,5},{2,6},{3,7},{4,0},{5,1},{6,2},{7,3},{8,12},{9,13},{10,... | collective-permute-start | bytes 602120 | tf_op jit(solution)/shard_map/ppermute | solution.py:527
  9.1 1.3 %collective-permute-start.2 = (f32[392,128]{1,0:T(8,128)S(1)}, f32[392,128]{1,0:T(8,128)S(1)}, u32[]{:S(2)}, u32[]{:S(2)}) collective-permute-start(f32[392,128]{1,0:T(8,128)S(1)} %get-tuple-element.68), channel_id=1, source_target_pairs={{0,6},{1,7},{2,0},{3,1},{4,2},{5,3},{6,4},{7,5},{8,14},{9,15},{10,... | collective-permute-start | bytes 602120 | tf_op jit(solution)/shard_map/ppermute | solution.py:527
  10.4 1.4 %constant_dynamic-slice_fusion.3 = (f32[192,192]{1,0:T(8,128)S(1)}, f32[192,192]{1,0:T(8,128)S(1)}, f32[192,192]{1,0:T(8,128)S(1)}) fusion(f32[192,4608]{1,0:T(8,128)} %param.11, s32[]{:T(128)S(6)} %select_n.18, s32[]{:T(128)S(6)} %select_n.19, s32[]{:T(128)S(6)} %select_n.20), kind=kLoop, calls=%fused_computation.4 | loop fusion | bytes 884748 | tf_op jit(solution)/shard_map/dynamic_slice | solution.py:571
  12.2 2.3 %collective-permute-done.refs_2_.refs_6_ = f32[392,128]{1,0:T(8,128)S(1)} collective-permute-done((f32[392,128]{1,0:T(8,128)S(1)}, f32[392,128]{1,0:T(8,128)S(1)}, u32[]{:S(2)}, u32[]{:S(2)}) %collective-permute-start) | collective-permute-done | bytes 200736 | tf_op jit(solution)/shard_map/ppermute | solution.py:527
  14.5 7.7 %collective-permute-done.1.refs_3_.refs_7_ = f32[392,128]{1,0:T(8,128)S(1)} collective-permute-done((f32[392,128]{1,0:T(8,128)S(1)}, f32[392,128]{1,0:T(8,128)S(1)}, u32[]{:S(2)}, u32[]{:S(2)}) %collective-permute-start.1) | collective-permute-done | bytes 200736 | tf_op jit(solution)/shard_map/ppermute | solution.py:527
  22.8 0.7 constant_dynamic-slice_fusion.refs_3_.refs_8_.refs_4_.refs_5_
  23.5 0.7 shard_map.111
  24.2 1.6 %shard_map.112 = (f32[440,128]{1,0:T(8,128)S(1)}, f32[440,128]{1,0:T(8,128)S(1)}) custom-call(f32[576,192]{1,0:T(8,128)S(1)} %pad_maximum_fusion.refs_0_.refs_4_.refs_2_, f32[576,192]{1,0:T(8,128)S(1)} %get-tuple-element.65.refs_1_, f32[8,128]{1,0:T(8,128)S(1)} %get-tuple-element.66.refs_2_, f32[392,128]{1,0:T(8,128)S(1)} %collective-permute-done.1.refs_3_.refs_7_, ...), custom_call_target="tpu_custom_call" | custom-call | tf_op jit(solution)/shard_map/pallas_call | solution.py:489
  25.9 1.6 %collective-permute-start.7 = (f32[440,128]{1,0:T(8,128)S(1)}, f32[440,128]{1,0:T(8,128)S(1)}, u32[]{:S(2)}, u32[]{:S(2)}) collective-permute-start(f32[440,128]{1,0:T(8,128)S(1)} %get-tuple-element.69.refs_0_), channel_id=1, source_target_pairs={{0,1},{1,0},{2,3},{3,2},{4,5},{5,4},{6,7},{7,6},{8,9},{9,8},{10,11... | collective-permute-start | bytes 675848 | tf_op jit(solution)/shard_map/ppermute | solution.py:527
  27.4 1.5 %collective-permute-start.8 = (f32[440,128]{1,0:T(8,128)S(1)}, f32[440,128]{1,0:T(8,128)S(1)}, u32[]{:S(2)}, u32[]{:S(2)}) collective-permute-start(f32[440,128]{1,0:T(8,128)S(1)} %get-tuple-element.70.refs_2_), channel_id=1, source_target_pairs={{0,16},{1,17},{2,18},{3,19},{4,20},{5,21},{6,22},{7,23},{8,24},{9,... | collective-permute-start | bytes 675848 | tf_op jit(solution)/shard_map/ppermute | solution.py:527
  28.9 4.4 %collective-permute-done.7.refs_1_ = f32[440,128]{1,0:T(8,128)S(1)} collective-permute-done((f32[440,128]{1,0:T(8,128)S(1)}, f32[440,128]{1,0:T(8,128)S(1)}, u32[]{:S(2)}, u32[]{:S(2)}) %collective-permute-start.7) | collective-permute-done | bytes 225312 | tf_op jit(solution)/shard_map/ppermute | solution.py:527
  33.4 1.2 collective-permute-done.8.refs_3_
  34.6 0.6 collective-permute-start.10
  35.5 4.8 %collective-permute-start.11 = (f32[384,128]{1,0:T(8,128)S(1)}, f32[384,128]{1,0:T(8,128)S(1)}, u32[]{:S(2)}, u32[]{:S(2)}) collective-permute-start(f32[384,128]{1,0:T(8,128)S(1)} %get-tuple-element.75), channel_id=1, source_target_pairs={{0,2},{1,3},{2,4},{3,5},{4,6},{5,7},{6,0},{7,1},{8,10},{9,11},{10,... | collective-permute-start | bytes 589832 | tf_op jit(solution)/shard_map/ppermute | solution.py:527
  40.3 1.6 %collective-permute-start.12 = (f32[384,128]{1,0:T(8,128)S(1)}, f32[384,128]{1,0:T(8,128)S(1)}, u32[]{:S(2)}, u32[]{:S(2)}) collective-permute-start(f32[384,128]{1,0:T(8,128)S(1)} %get-tuple-element.76), channel_id=1, source_target_pairs={{0,4},{1,5},{2,6},{3,7},{4,0},{5,1},{6,2},{7,3},{8,12},{9,13},{10,... | collective-permute-start | bytes 589832 | tf_op jit(solution)/shard_map/ppermute | solution.py:527
  41.9 0.8 collective-permute-start.13
  42.7 1.5 %collective-permute-start.9 = (f32[440,128]{1,0:T(8,128)S(1)}, f32[440,128]{1,0:T(8,128)S(1)}, u32[]{:S(2)}, u32[]{:S(2)}) collective-permute-start(f32[440,128]{1,0:T(8,128)S(1)} %get-tuple-element.71.refs_0_), channel_id=1, source_target_pairs={{0,16},{1,17},{2,18},{3,19},{4,20},{5,21},{6,22},{7,23},{8,24},{9,... | collective-permute-start | bytes 675848 | tf_op jit(solution)/shard_map/ppermute | solution.py:527
  44.2 3.0 %collective-permute-done.11.refs_1_ = f32[384,128]{1,0:T(8,128)S(1)} collective-permute-done((f32[384,128]{1,0:T(8,128)S(1)}, f32[384,128]{1,0:T(8,128)S(1)}, u32[]{:S(2)}, u32[]{:S(2)}) %collective-permute-start.11) | collective-permute-done | bytes 196640 | tf_op jit(solution)/shard_map/ppermute | solution.py:527
  47.2 6.4 %collective-permute-done.12.refs_2_ = f32[384,128]{1,0:T(8,128)S(1)} collective-permute-done((f32[384,128]{1,0:T(8,128)S(1)}, f32[384,128]{1,0:T(8,128)S(1)}, u32[]{:S(2)}, u32[]{:S(2)}) %collective-permute-start.12) | collective-permute-done | bytes 196640 | tf_op jit(solution)/shard_map/ppermute | solution.py:527
  55.8 2.9 %shard_map.117 = (f32[440,128]{1,0:T(8,128)S(1)}, f32[440,128]{1,0:T(8,128)S(1)}, f32[192,128]{1,0:T(8,128)S(1)}, f32[192,128]{1,0:T(8,128)S(1)}, f32[192,128]{1...) custom-call(f32[576,192]{1,0:T(8,128)S(1)} %get-tuple-element.73.refs_0_, ...), custom_call_target="tpu_custom_call" | custom-call | tf_op jit(solution)/shard_map/pallas_call | solution.py:489
  58.7 1.5 %collective-permute-start.22 = (f32[440,128]{1,0:T(8,128)S(1)}, f32[440,128]{1,0:T(8,128)S(1)}, u32[]{:S(2)}, u32[]{:S(2)}) collective-permute-start(f32[440,128]{1,0:T(8,128)S(1)} %get-tuple-element.91.refs_0_), channel_id=1, source_target_pairs={{0,1},{1,0},{2,3},{3,2},{4,5},{5,4},{6,7},{7,6},{8,9},{9,8},{10,11... | collective-permute-start | bytes 675848 | tf_op jit(solution)/shard_map/ppermute | solution.py:527
  60.3 1.5 %collective-permute-start.23 = (f32[440,128]{1,0:T(8,128)S(1)}, f32[440,128]{1,0:T(8,128)S(1)}, u32[]{:S(2)}, u32[]{:S(2)}) collective-permute-start(f32[440,128]{1,0:T(8,128)S(1)} %get-tuple-element.92.refs_2_), channel_id=1, source_target_pairs={{0,16},{1,17},{2,18},{3,19},{4,20},{5,21},{6,22},{7,23},{8,24},{9,... | collective-permute-start | bytes 675848 | tf_op jit(solution)/shard_map/ppermute | solution.py:527
  61.8 4.7 %collective-permute-done.22.refs_1_ = f32[440,128]{1,0:T(8,128)S(1)} collective-permute-done((f32[440,128]{1,0:T(8,128)S(1)}, f32[440,128]{1,0:T(8,128)S(1)}, u32[]{:S(2)}, u32[]{:S(2)}) %collective-permute-start.22) | collective-permute-done | bytes 225312 | tf_op jit(solution)/shard_map/ppermute | solution.py:527
  66.4 1.2 collective-permute-done.23.refs_3_
  67.7 1.6 %collective-permute-start.24 = (f32[440,128]{1,0:T(8,128)S(1)}, f32[440,128]{1,0:T(8,128)S(1)}, u32[]{:S(2)}, u32[]{:S(2)}) collective-permute-start(f32[440,128]{1,0:T(8,128)S(1)} %get-tuple-element.93.refs_0_), channel_id=1, source_target_pairs={{0,16},{1,17},{2,18},{3,19},{4,20},{5,21},{6,22},{7,23},{8,24},{9,... | collective-permute-start | bytes 675848 | tf_op jit(solution)/shard_map/ppermute | solution.py:527
  69.2 0.6 collective-permute-start.25
  69.8 4.5 %collective-permute-done.24.refs_1_ = f32[440,128]{1,0:T(8,128)S(1)} collective-permute-done((f32[440,128]{1,0:T(8,128)S(1)}, f32[440,128]{1,0:T(8,128)S(1)}, u32[]{:S(2)}, u32[]{:S(2)}) %collective-permute-start.24) | collective-permute-done | bytes 225312 | tf_op jit(solution)/shard_map/ppermute | solution.py:527
  74.3 1.2 collective-permute-done.25.refs_3_
  75.5 0.8 shard_map.120
  76.3 2.4 %shard_map.121 = (f32[4,392,128]{2,1,0:T(8,128)S(1)}, f32[576,192]{1,0:T(8,128)S(1)}) custom-call(f32[576,192]{1,0:T(8,128)S(1)} %get-tuple-element.98.refs_0_, f32[8,128]{1,0:T(8,128)S(1)} %get-tuple-element.99.refs_1_, f32[576,192]{1,0:T(8,128)S(1)} %pad_maximum_fusion.refs_0_.refs_4_.refs_2_, f32[392,128]{1,0:T(8,128)S(1)} %collective-permute-done.3.refs_5_.refs_3_, ...), custom_call_target="tpu_custom_call" | custom-call | tf_op jit(solution)/shard_map/pallas_call | solution.py:489
  79.3 2.4 %shard_map.122 = (f32[224,128]{1,0:T(8,128)S(1)}, f32[224,128]{1,0:T(8,128)S(1)}, f32[224,128]{1,0:T(8,128)S(1)}, f32[224,128]{1,0:T(8,128)S(1)}, f32[392,128]{1...) custom-call(f32[576,192]{1,0:T(8,128)S(1)} %get-tuple-element.98.refs_0_, ...), custom_call_target="tpu_custom_call" | custom-call | tf_op jit(solution)/shard_map/pallas_call | solution.py:489
  81.7 0.6 collective-permute-start.30
  82.4 6.0 %collective-permute-start.19 = (f32[192,128]{1,0:T(8,128)S(1)}, f32[192,128]{1,0:T(8,128)S(1)}, u32[]{:S(2)}, u32[]{:S(2)}) collective-permute-start(f32[192,128]{1,0:T(8,128)S(1)} %get-tuple-element.88), channel_id=1, source_target_pairs={{0,6},{1,7},{2,0},{3,1},{4,2},{5,3},{6,4},{7,5},{8,14},{9,15},{10,... | collective-permute-start | bytes 294920 | tf_op jit(solution)/shard_map/ppermute | solution.py:527
  88.9 2.4 %collective-permute-start.32 = (f32[224,128]{1,0:T(8,128)S(1)}, f32[224,128]{1,0:T(8,128)S(1)}, u32[]{:S(2)}, u32[]{:S(2)}) collective-permute-start(f32[224,128]{1,0:T(8,128)S(1)} %get-tuple-element.116), channel_id=1, source_target_pairs={{0,17},{1,16},{2,19},{3,18},{4,21},{5,20},{6,23},{7,22},{8,25},{9,... | collective-permute-start | bytes 344072 | tf_op jit(solution)/shard_map/ppermute | solution.py:527
  91.8 3.6 %collective-permute-start.29 = (f32[392,128]{1,0:T(8,128)S(1)}, f32[392,128]{1,0:T(8,128)S(1)}, u32[]{:S(2)}, u32[]{:S(2)}) collective-permute-start(f32[392,128]{1,0:T(8,128)S(1)} %get-tuple-element.110), channel_id=1, source_target_pairs={{0,2},{1,3},{2,4},{3,5},{4,6},{5,7},{6,0},{7,1},{8,10},{9,11},{10,... | collective-permute-start | bytes 602120 | tf_op jit(solution)/shard_map/ppermute | solution.py:527
  95.3 1.1 collective-permute-start.20
  96.6 18.5 %collective-permute-done.20.refs_2_ = f32[192,128]{1,0:T(8,128)S(1)} collective-permute-done((f32[192,128]{1,0:T(8,128)S(1)}, f32[192,128]{1,0:T(8,128)S(1)}, u32[]{:S(2)}, u32[]{:S(2)}) %collective-permute-start.20) | collective-permute-done | bytes 98336 | tf_op jit(solution)/shard_map/ppermute | solution.py:527
  115.1 0.7 collective-permute-start.33
  115.8 2.7 %collective-permute-start.34 = (f32[48,192]{1,0:T(8,128)S(1)}, f32[48,192]{1,0:T(8,128)S(1)}, u32[]{:S(2)}, u32[]{:S(2)}) collective-permute-start(f32[48,192]{1,0:T(8,128)S(1)} %get-tuple-element.119), channel_id=1, source_target_pairs={{0,10},{1,0},{2,24},{3,13},{4,26},{5,16},{6,29},{7,19},{8,1},{9,23... | collective-permute-start | bytes 110600 | tf_op jit(solution)/shard_map/ppermute | solution.py:527
  118.5 7.1 %collective-permute-start.35 = (f32[48,192]{1,0:T(8,128)S(1)}, f32[48,192]{1,0:T(8,128)S(1)}, u32[]{:S(2)}, u32[]{:S(2)}) collective-permute-start(f32[48,192]{1,0:T(8,128)S(1)} %get-tuple-element.120), channel_id=1, source_target_pairs={{0,21},{1,11},{2,2},{3,24},{4,16},{5,5},{6,8},{7,29},{8,12},{9,1},... | collective-permute-start | bytes 110600 | tf_op jit(solution)/shard_map/ppermute | solution.py:527
  125.6 0.8 shard_map.123
  126.4 0.9 collective-permute-done.35.refs_2_
  127.3 0.7 shard_map.127
  128.1 0.9 shard_map.125
  (66 shorter events, 5.6 us)
Async XLA Ops:
  0.7 0.9 copy-start
  1.6 0.9 copy-start.1
  2.5 0.7 copy-start.4
  3.4 11.1 %collective-permute-start = (f32[392,128]{1,0:T(8,128)S(1)}, f32[392,128]{1,0:T(8,128)S(1)}, u32[]{:S(2)}, u32[]{:S(2)}) collective-permute-start(f32[392,128]{1,0:T(8,128)S(1)} %get-tuple-element.64), channel_id=1, source_target_pairs={{0,2},{1,3},{2,4},{3,5},{4,6},{5,7},{6,0},{7,1},{8,10},{9,11},{10,... | collective-permute-start | bytes 602120 | tf_op jit(solution)/shard_map/ppermute | solution.py:527
  6.5 15.7 %collective-permute-start.1 = (f32[392,128]{1,0:T(8,128)S(1)}, f32[392,128]{1,0:T(8,128)S(1)}, u32[]{:S(2)}, u32[]{:S(2)}) collective-permute-start(f32[392,128]{1,0:T(8,128)S(1)} %get-tuple-element.67), channel_id=1, source_target_pairs={{0,4},{1,5},{2,6},{3,7},{4,0},{5,1},{6,2},{7,3},{8,12},{9,13},{10,... | collective-permute-start | bytes 602120 | tf_op jit(solution)/shard_map/ppermute | solution.py:527
  9.1 13.2 %collective-permute-start.2 = (f32[392,128]{1,0:T(8,128)S(1)}, f32[392,128]{1,0:T(8,128)S(1)}, u32[]{:S(2)}, u32[]{:S(2)}) collective-permute-start(f32[392,128]{1,0:T(8,128)S(1)} %get-tuple-element.68), channel_id=1, source_target_pairs={{0,6},{1,7},{2,0},{3,1},{4,2},{5,3},{6,4},{7,5},{8,14},{9,15},{10,... | collective-permute-start | bytes 602120 | tf_op jit(solution)/shard_map/ppermute | solution.py:527
  10.4 13.7 %collective-permute-start.3 = (f32[392,128]{1,0:T(8,128)S(1)}, f32[392,128]{1,0:T(8,128)S(1)}, u32[]{:S(2)}, u32[]{:S(2)}) collective-permute-start(f32[392,128]{1,0:T(8,128)S(1)} %get-tuple-element.63.refs_1_.refs_5_), channel_id=1, source_target_pairs={{0,8},{1,9},{2,10},{3,11},{4,12},{5,13},{6,14},{7,15},{8,0},{9,1},... | collective-permute-start | bytes 602120 | tf_op jit(solution)/shard_map/ppermute | solution.py:527
  11.8 23.4 %copy-start.2 = (bf16[128,768]{1,0:T(8,128)(2,1)S(1)}, bf16[128,768]{1,0:T(8,128)(2,1)}, u32[]{:S(2)}) copy-start(bf16[128,768]{1,0:T(8,128)(2,1)} %refs_0_.3) | copy-start | bytes 589828
  11.8 23.4 %copy-start.3 = (bf16[128,768]{1,0:T(8,128)(2,1)S(1)}, bf16[128,768]{1,0:T(8,128)(2,1)}, u32[]{:S(2)}) copy-start(bf16[128,768]{1,0:T(8,128)(2,1)} %refs_1_.3) | copy-start | bytes 589828
  14.5 9.7 %collective-permute-start.4 = (f32[392,128]{1,0:T(8,128)S(1)}, f32[392,128]{1,0:T(8,128)S(1)}, u32[]{:S(2)}, u32[]{:S(2)}) collective-permute-start(f32[392,128]{1,0:T(8,128)S(1)} %collective-permute-done.refs_2_.refs_6_), channel_id=1, source_target_pairs={{0,8},{1,9},{2,10},{3,11},{4,12},{5,13},{6,14},{7,15},{8,0},{9,1},... | collective-permute-start | bytes 602120 | tf_op jit(solution)/shard_map/ppermute | solution.py:527
  22.3 2.0 %collective-permute-start.5 = (f32[392,128]{1,0:T(8,128)S(1)}, f32[392,128]{1,0:T(8,128)S(1)}, u32[]{:S(2)}, u32[]{:S(2)}) collective-permute-start(f32[392,128]{1,0:T(8,128)S(1)} %collective-permute-done.1.refs_3_.refs_7_), channel_id=1, source_target_pairs={{0,8},{1,9},{2,10},{3,11},{4,12},{5,13},{6,14},{7,15},{8,0},{9,1},... | collective-permute-start | bytes 602120 | tf_op jit(solution)/shard_map/ppermute | solution.py:527
  22.3 2.0 %collective-permute-start.6 = (f32[392,128]{1,0:T(8,128)S(1)}, f32[392,128]{1,0:T(8,128)S(1)}, u32[]{:S(2)}, u32[]{:S(2)}) collective-permute-start(f32[392,128]{1,0:T(8,128)S(1)} %collective-permute-done.2.refs_4_.refs_8_), channel_id=1, source_target_pairs={{0,8},{1,9},{2,10},{3,11},{4,12},{5,13},{6,14},{7,15},{8,0},{9,1},... | collective-permute-start | bytes 602120 | tf_op jit(solution)/shard_map/ppermute | solution.py:527
  25.9 7.5 %collective-permute-start.7 = (f32[440,128]{1,0:T(8,128)S(1)}, f32[440,128]{1,0:T(8,128)S(1)}, u32[]{:S(2)}, u32[]{:S(2)}) collective-permute-start(f32[440,128]{1,0:T(8,128)S(1)} %get-tuple-element.69.refs_0_), channel_id=1, source_target_pairs={{0,1},{1,0},{2,3},{3,2},{4,5},{5,4},{6,7},{7,6},{8,9},{9,8},{10,11... | collective-permute-start | bytes 675848 | tf_op jit(solution)/shard_map/ppermute | solution.py:527
  27.4 7.1 %collective-permute-start.8 = (f32[440,128]{1,0:T(8,128)S(1)}, f32[440,128]{1,0:T(8,128)S(1)}, u32[]{:S(2)}, u32[]{:S(2)}) collective-permute-start(f32[440,128]{1,0:T(8,128)S(1)} %get-tuple-element.70.refs_2_), channel_id=1, source_target_pairs={{0,16},{1,17},{2,18},{3,19},{4,20},{5,21},{6,22},{7,23},{8,24},{9,... | collective-permute-start | bytes 675848 | tf_op jit(solution)/shard_map/ppermute | solution.py:527
  34.6 19.5 %collective-permute-start.10 = (f32[440,128]{1,0:T(8,128)S(1)}, f32[440,128]{1,0:T(8,128)S(1)}, u32[]{:S(2)}, u32[]{:S(2)}) collective-permute-start(f32[440,128]{1,0:T(8,128)S(1)} %get-tuple-element.72.refs_2_), channel_id=1, source_target_pairs={{0,1},{1,0},{2,3},{3,2},{4,5},{5,4},{6,7},{7,6},{8,9},{9,8},{10,11... | collective-permute-start | bytes 675848 | tf_op jit(solution)/shard_map/ppermute | solution.py:527
  35.5 11.7 %collective-permute-start.11 = (f32[384,128]{1,0:T(8,128)S(1)}, f32[384,128]{1,0:T(8,128)S(1)}, u32[]{:S(2)}, u32[]{:S(2)}) collective-permute-start(f32[384,128]{1,0:T(8,128)S(1)} %get-tuple-element.75), channel_id=1, source_target_pairs={{0,2},{1,3},{2,4},{3,5},{4,6},{5,7},{6,0},{7,1},{8,10},{9,11},{10,... | collective-permute-start | bytes 589832 | tf_op jit(solution)/shard_map/ppermute | solution.py:527
  40.3 13.3 %collective-permute-start.12 = (f32[384,128]{1,0:T(8,128)S(1)}, f32[384,128]{1,0:T(8,128)S(1)}, u32[]{:S(2)}, u32[]{:S(2)}) collective-permute-start(f32[384,128]{1,0:T(8,128)S(1)} %get-tuple-element.76), channel_id=1, source_target_pairs={{0,4},{1,5},{2,6},{3,7},{4,0},{5,1},{6,2},{7,3},{8,12},{9,13},{10,... | collective-permute-start | bytes 589832 | tf_op jit(solution)/shard_map/ppermute | solution.py:527
  41.9 11.7 %collective-permute-start.13 = (f32[384,128]{1,0:T(8,128)S(1)}, f32[384,128]{1,0:T(8,128)S(1)}, u32[]{:S(2)}, u32[]{:S(2)}) collective-permute-start(f32[384,128]{1,0:T(8,128)S(1)} %get-tuple-element.77), channel_id=1, source_target_pairs={{0,6},{1,7},{2,0},{3,1},{4,2},{5,3},{6,4},{7,5},{8,14},{9,15},{10,... | collective-permute-start | bytes 589832 | tf_op jit(solution)/shard_map/ppermute | solution.py:527
  42.7 11.9 %collective-permute-start.9 = (f32[440,128]{1,0:T(8,128)S(1)}, f32[440,128]{1,0:T(8,128)S(1)}, u32[]{:S(2)}, u32[]{:S(2)}) collective-permute-start(f32[440,128]{1,0:T(8,128)S(1)} %get-tuple-element.71.refs_0_), channel_id=1, source_target_pairs={{0,16},{1,17},{2,18},{3,19},{4,20},{5,21},{6,22},{7,23},{8,24},{9,... | collective-permute-start | bytes 675848 | tf_op jit(solution)/shard_map/ppermute | solution.py:527
  53.5 1.5 %collective-permute-start.14 = (f32[384,128]{1,0:T(8,128)S(1)}, f32[384,128]{1,0:T(8,128)S(1)}, u32[]{:S(2)}, u32[]{:S(2)}) collective-permute-start(f32[384,128]{1,0:T(8,128)S(1)} %get-tuple-element.78.refs_1_), channel_id=1, source_target_pairs={{0,8},{1,9},{2,10},{3,11},{4,12},{5,13},{6,14},{7,15},{8,0},{9,1},... | collective-permute-start | bytes 589832 | tf_op jit(solution)/shard_map/ppermute | solution.py:527
  53.5 1.7 %collective-permute-start.15 = (f32[384,128]{1,0:T(8,128)S(1)}, f32[384,128]{1,0:T(8,128)S(1)}, u32[]{:S(2)}, u32[]{:S(2)}) collective-permute-start(f32[384,128]{1,0:T(8,128)S(1)} %get-tuple-element.79.refs_2_), channel_id=1, source_target_pairs={{0,8},{1,9},{2,10},{3,11},{4,12},{5,13},{6,14},{7,15},{8,0},{9,1},... | collective-permute-start | bytes 589832 | tf_op jit(solution)/shard_map/ppermute | solution.py:527
  54.1 1.5 %collective-permute-start.16 = (f32[384,128]{1,0:T(8,128)S(1)}, f32[384,128]{1,0:T(8,128)S(1)}, u32[]{:S(2)}, u32[]{:S(2)}) collective-permute-start(f32[384,128]{1,0:T(8,128)S(1)} %get-tuple-element.80.refs_3_), channel_id=1, source_target_pairs={{0,8},{1,9},{2,10},{3,11},{4,12},{5,13},{6,14},{7,15},{8,0},{9,1},... | collective-permute-start | bytes 589832 | tf_op jit(solution)/shard_map/ppermute | solution.py:527
  54.1 1.7 %collective-permute-start.17 = (f32[384,128]{1,0:T(8,128)S(1)}, f32[384,128]{1,0:T(8,128)S(1)}, u32[]{:S(2)}, u32[]{:S(2)}) collective-permute-start(f32[384,128]{1,0:T(8,128)S(1)} %get-tuple-element.81.refs_4_), channel_id=1, source_target_pairs={{0,8},{1,9},{2,10},{3,11},{4,12},{5,13},{6,14},{7,15},{8,0},{9,1},... | collective-permute-start | bytes 589832 | tf_op jit(solution)/shard_map/ppermute | solution.py:527
  58.7 7.7 %collective-permute-start.22 = (f32[440,128]{1,0:T(8,128)S(1)}, f32[440,128]{1,0:T(8,128)S(1)}, u32[]{:S(2)}, u32[]{:S(2)}) collective-permute-start(f32[440,128]{1,0:T(8,128)S(1)} %get-tuple-element.91.refs_0_), channel_id=1, source_target_pairs={{0,1},{1,0},{2,3},{3,2},{4,5},{5,4},{6,7},{7,6},{8,9},{9,8},{10,11... | collective-permute-start | bytes 675848 | tf_op jit(solution)/shard_map/ppermute | solution.py:527
  60.3 7.4 %collective-permute-start.23 = (f32[440,128]{1,0:T(8,128)S(1)}, f32[440,128]{1,0:T(8,128)S(1)}, u32[]{:S(2)}, u32[]{:S(2)}) collective-permute-start(f32[440,128]{1,0:T(8,128)S(1)} %get-tuple-element.92.refs_2_), channel_id=1, source_target_pairs={{0,16},{1,17},{2,18},{3,19},{4,20},{5,21},{6,22},{7,23},{8,24},{9,... | collective-permute-start | bytes 675848 | tf_op jit(solution)/shard_map/ppermute | solution.py:527
  67.7 6.6 %collective-permute-start.24 = (f32[440,128]{1,0:T(8,128)S(1)}, f32[440,128]{1,0:T(8,128)S(1)}, u32[]{:S(2)}, u32[]{:S(2)}) collective-permute-start(f32[440,128]{1,0:T(8,128)S(1)} %get-tuple-element.93.refs_0_), channel_id=1, source_target_pairs={{0,16},{1,17},{2,18},{3,19},{4,20},{5,21},{6,22},{7,23},{8,24},{9,... | collective-permute-start | bytes 675848 | tf_op jit(solution)/shard_map/ppermute | solution.py:527
  69.2 6.2 %collective-permute-start.25 = (f32[440,128]{1,0:T(8,128)S(1)}, f32[440,128]{1,0:T(8,128)S(1)}, u32[]{:S(2)}, u32[]{:S(2)}) collective-permute-start(f32[440,128]{1,0:T(8,128)S(1)} %get-tuple-element.94.refs_2_), channel_id=1, source_target_pairs={{0,1},{1,0},{2,3},{3,2},{4,5},{5,4},{6,7},{7,6},{8,9},{9,8},{10,11... | collective-permute-start | bytes 675848 | tf_op jit(solution)/shard_map/ppermute | solution.py:527
  78.7 12.6 %collective-permute-start.26 = (f32[4,392,128]{2,1,0:T(8,128)S(1)}, f32[4,392,128]{2,1,0:T(8,128)S(1)}, u32[]{:S(2)}, u32[]{:S(2)}) collective-permute-start(f32[4,392,128]{2,1,0:T(8,128)S(1)} %get-tuple-element.106), channel_id=1, source_target_pairs={{0,8},{1,9},{2,10},{3,11},{4,12},{5,13},{6,14},{7,15},{8,0},{9,1},... | collective-permute-start | bytes 2408456 | tf_op jit(solution)/shard_map/ppermute | solution.py:527
  78.8 3.6 %collective-permute-start.18 = (f32[4,192,128]{2,1,0:T(8,128)S(1)}, f32[4,192,128]{2,1,0:T(8,128)S(1)}, u32[]{:S(2)}, u32[]{:S(2)}) collective-permute-start(f32[4,192,128]{2,1,0:T(8,128)S(1)} %get-tuple-element.86), channel_id=1, source_target_pairs={{0,8},{1,9},{2,10},{3,11},{4,12},{5,13},{6,14},{7,15},{8,0},{9,1},... | collective-permute-start | bytes 1179656 | tf_op jit(solution)/shard_map/ppermute | solution.py:527
  81.7 10.1 %collective-permute-start.30 = (f32[224,128]{1,0:T(8,128)S(1)}, f32[224,128]{1,0:T(8,128)S(1)}, u32[]{:S(2)}, u32[]{:S(2)}) collective-permute-start(f32[224,128]{1,0:T(8,128)S(1)} %get-tuple-element.114), channel_id=1, source_target_pairs={{0,1},{1,0},{2,3},{3,2},{4,5},{5,4},{6,7},{7,6},{8,9},{9,8},{10,11... | collective-permute-start | bytes 344072 | tf_op jit(solution)/shard_map/ppermute | solution.py:527
  82.4 9.1 %collective-permute-start.19 = (f32[192,128]{1,0:T(8,128)S(1)}, f32[192,128]{1,0:T(8,128)S(1)}, u32[]{:S(2)}, u32[]{:S(2)}) collective-permute-start(f32[192,128]{1,0:T(8,128)S(1)} %get-tuple-element.88), channel_id=1, source_target_pairs={{0,6},{1,7},{2,0},{3,1},{4,2},{5,3},{6,4},{7,5},{8,14},{9,15},{10,... | collective-permute-start | bytes 294920 | tf_op jit(solution)/shard_map/ppermute | solution.py:527
  88.3 7.0 %collective-permute-start.31 = (f32[224,128]{1,0:T(8,128)S(1)}, f32[224,128]{1,0:T(8,128)S(1)}, u32[]{:S(2)}, u32[]{:S(2)}) collective-permute-start(f32[224,128]{1,0:T(8,128)S(1)} %get-tuple-element.115), channel_id=1, source_target_pairs={{0,16},{1,17},{2,18},{3,19},{4,20},{5,21},{6,22},{7,23},{8,24},{9,... | collective-permute-start | bytes 344072 | tf_op jit(solution)/shard_map/ppermute | solution.py:527
  88.9 7.5 %collective-permute-start.32 = (f32[224,128]{1,0:T(8,128)S(1)}, f32[224,128]{1,0:T(8,128)S(1)}, u32[]{:S(2)}, u32[]{:S(2)}) collective-permute-start(f32[224,128]{1,0:T(8,128)S(1)} %get-tuple-element.116), channel_id=1, source_target_pairs={{0,17},{1,16},{2,19},{3,18},{4,21},{5,20},{6,23},{7,22},{8,25},{9,... | collective-permute-start | bytes 344072 | tf_op jit(solution)/shard_map/ppermute | solution.py:527
  91.4 36.6 %collective-permute-start.27 = (f32[392,128]{1,0:T(8,128)S(1)}, f32[392,128]{1,0:T(8,128)S(1)}, u32[]{:S(2)}, u32[]{:S(2)}) collective-permute-start(f32[392,128]{1,0:T(8,128)S(1)} %get-tuple-element.108), channel_id=1, source_target_pairs={{0,6},{1,7},{2,0},{3,1},{4,2},{5,3},{6,4},{7,5},{8,14},{9,15},{10,... | collective-permute-start | bytes 602120 | tf_op jit(solution)/shard_map/ppermute | solution.py:527
  91.5 36.5 %collective-permute-start.28 = (f32[392,128]{1,0:T(8,128)S(1)}, f32[392,128]{1,0:T(8,128)S(1)}, u32[]{:S(2)}, u32[]{:S(2)}) collective-permute-start(f32[392,128]{1,0:T(8,128)S(1)} %get-tuple-element.109), channel_id=1, source_target_pairs={{0,4},{1,5},{2,6},{3,7},{4,0},{5,1},{6,2},{7,3},{8,12},{9,13},{10,... | collective-permute-start | bytes 602120 | tf_op jit(solution)/shard_map/ppermute | solution.py:527
  91.8 36.3 %collective-permute-start.29 = (f32[392,128]{1,0:T(8,128)S(1)}, f32[392,128]{1,0:T(8,128)S(1)}, u32[]{:S(2)}, u32[]{:S(2)}) collective-permute-start(f32[392,128]{1,0:T(8,128)S(1)} %get-tuple-element.110), channel_id=1, source_target_pairs={{0,2},{1,3},{2,4},{3,5},{4,6},{5,7},{6,0},{7,1},{8,10},{9,11},{10,... | collective-permute-start | bytes 602120 | tf_op jit(solution)/shard_map/ppermute | solution.py:527
  95.3 19.8 %collective-permute-start.20 = (f32[192,128]{1,0:T(8,128)S(1)}, f32[192,128]{1,0:T(8,128)S(1)}, u32[]{:S(2)}, u32[]{:S(2)}) collective-permute-start(f32[192,128]{1,0:T(8,128)S(1)} %get-tuple-element.89), channel_id=1, source_target_pairs={{0,4},{1,5},{2,6},{3,7},{4,0},{5,1},{6,2},{7,3},{8,12},{9,13},{10,... | collective-permute-start | bytes 294920 | tf_op jit(solution)/shard_map/ppermute | solution.py:527
  96.4 19.3 %collective-permute-start.21 = (f32[192,128]{1,0:T(8,128)S(1)}, f32[192,128]{1,0:T(8,128)S(1)}, u32[]{:S(2)}, u32[]{:S(2)}) collective-permute-start(f32[192,128]{1,0:T(8,128)S(1)} %get-tuple-element.90), channel_id=1, source_target_pairs={{0,2},{1,3},{2,4},{3,5},{4,6},{5,7},{6,0},{7,1},{8,10},{9,11},{10,... | collective-permute-start | bytes 294920 | tf_op jit(solution)/shard_map/ppermute | solution.py:527
  115.1 3.4 %collective-permute-start.33 = (f32[48,192]{1,0:T(8,128)S(1)}, f32[48,192]{1,0:T(8,128)S(1)}, u32[]{:S(2)}, u32[]{:S(2)}) collective-permute-start(f32[48,192]{1,0:T(8,128)S(1)} %get-tuple-element.118), channel_id=1, source_target_pairs={{0,0},{1,21},{2,13},{3,3},{4,5},{5,27},{6,18},{7,8},{8,22},{9,12},... | collective-permute-start | bytes 110600 | tf_op jit(solution)/shard_map/ppermute | solution.py:527
  115.8 10.6 %collective-permute-start.34 = (f32[48,192]{1,0:T(8,128)S(1)}, f32[48,192]{1,0:T(8,128)S(1)}, u32[]{:S(2)}, u32[]{:S(2)}) collective-permute-start(f32[48,192]{1,0:T(8,128)S(1)} %get-tuple-element.119), channel_id=1, source_target_pairs={{0,10},{1,0},{2,24},{3,13},{4,26},{5,16},{6,29},{7,19},{8,1},{9,23... | collective-permute-start | bytes 110600 | tf_op jit(solution)/shard_map/ppermute | solution.py:527
  118.5 8.8 %collective-permute-start.35 = (f32[48,192]{1,0:T(8,128)S(1)}, f32[48,192]{1,0:T(8,128)S(1)}, u32[]{:S(2)}, u32[]{:S(2)}) collective-permute-start(f32[48,192]{1,0:T(8,128)S(1)} %get-tuple-element.120), channel_id=1, source_target_pairs={{0,21},{1,11},{2,2},{3,24},{4,16},{5,5},{6,8},{7,29},{8,12},{9,1},... | collective-permute-start | bytes 110600 | tf_op jit(solution)/shard_map/ppermute | solution.py:527
where the time goes:
time: 131 us; the launch traced here: 129 us
  waiting for transfers between devices  56.8 us (43%)
  starting transfers between devices  51.7 us (39%)
  Pallas kernels  14.6 us (11%)
  local copies, waits for them, and re-layouts  4.94 us (4%)
    ppermute x36, waiting for transfers between devices, send(): return lax.ppermute(x, AXES, perm)  56.8 us
    ppermute x36, starting transfers between devices, send(): return lax.ppermute(x, AXES, perm)  51.7 us
    pallas_call x17, Pallas kernels, run(): pl.pallas_call(kernel, out_shape=[jax.ShapeDtypeStruct(s.shape, s.dtype)...  14.6 us
    unnamed x13, local copies, waits for them, and re-layouts  2.88 us
  transfers between devices with their start and end apart: 36, of which 15 were waited for; matrix products, arithmetic and copies ran while one was open for 2% of the time, Pallas kernels for 4%

commit v1 on v0

--- a/solution.py
+++ b/solution.py
@@ -57,8 +57,11 @@
     def core_perm(self):
         return self.perm(lambda j, c, h: (j, (c + 1) % self.cores, h))
 
-    def head_perm(self, shift):
-        return self.perm(lambda j, c, h: (j, c, (h + shift) % self.heads))
+    def other_head(self, head, step):
+        return head ^ step if self.heads & (self.heads - 1) == 0 else (step - head) % self.heads
+
+    def head_perm(self, step):
+        return self.perm(lambda j, c, h: (j, c, self.other_head(h, step)))
 
     def scatter_perm(self, step):
         return self.perm(lambda j, c, h: (self.target(j, step), c, h))
@@ -124,10 +127,21 @@
     return dot(parts[0], exact, dims) + dot(parts[1], exact, dims)
 
 
+def dots_left(lefts, exact, dims):
+    if len(lefts[0]) == 1:
+        return [dot_left(left, exact, dims) for left in lefts]
+    rows = lefts[0][0].shape[0]
+    flat = dot(cat([part for left in lefts for part in left], 0), exact, dims)
+    cuts = [flat[i * rows : (i + 1) * rows] for i in range(2 * len(lefts))]
+    return [cuts[2 * i] + cuts[2 * i + 1] for i in range(len(lefts))]
+
+
 def dot_both(a, b, dims):
     if len(a) == 1:
         return dot(a[0], b[0], dims, lax.Precision.HIGH)
-    return dot(a[0], b[0], dims) + (dot(a[0], b[1], dims) + dot(a[1], b[0], dims))
+    rows = a[0].shape[0]
+    both = dot(cat(a, 0), b[0], dims)
+    return both[:rows] + (dot(a[0], b[1], dims) + both[rows:])
 
 
 def gates(act):
@@ -207,11 +221,19 @@
     return [cat([b[m * slot : (m + 1) * slot] for b in bodies], 0) for m in range(3)]
 
 
-def select_heads(lay, pieces, head_ids, shift):
-    wanted = lax.rem(head_ids[0:1, :] + shift, lay.heads)
+def select_heads(lay, pieces, head_ids, step):
+    own = head_ids[0:1, :]
     result = pieces[0]
-    for h in range(1, lay.heads):
-        result = jnp.where(wanted == h, pieces[h], result)
+    for i in range(1, lay.heads):
+        result = jnp.where(own == lay.other_head(i, step), pieces[i], result)
+    return result
+
+
+def select_steps(lay, pieces, head_ids, head):
+    own = head_ids[0:1, :]
+    result = pieces[0]
+    for step in range(1, lay.heads):
+        result = jnp.where(own == lay.other_head(head, step), pieces[step], result)
     return result
 
 
@@ -249,14 +271,14 @@
     keys, values = join_rows(lay, slabs)
     rates = join_rates(lay, slabs)
     gate, up, down = (split(lay, w) for w in in_three(lay, weights))
-    a = dot_left(gate, keys, NN)
-    b = dot_left(up, keys, NN)
-    u = dot_left(down, values, NN)
+    a, b = dots_left((gate, up), keys, NN)
+    (u,) = dots_left((down,), values, NN)
     _, silu, _, slope = gates(a)
     mu = -rates * u
-    d_gate = dot_left(split(lay, mu * b * slope), keys, NT)
-    d_up = dot_left(split(lay, mu * silu), keys, NT)
-    d_down = dot_left(split(lay, -rates * (silu * b)), values, NT)
+    d_gate, d_up = dots_left(
+        (split(lay, mu * b * slope), split(lay, mu * silu)), keys, NT
+    )
+    (d_down,) = dots_left((split(lay, -rates * (silu * b)),), values, NT)
     return [d_gate, d_up, d_down], jnp.sum(rates, 1, keepdims=True)
 
 
@@ -309,16 +331,14 @@
         weights, slabs = unpack_all(lay, args[: lay.plane]), args[lay.plane :]
     queries, cotangents = join_rows(lay, slabs)
     gate, up, down = (split(lay, w) for w in weights)
-    a = dot_left(gate, queries, NN)
-    b = dot_left(up, queries, NN)
-    u = dot_left(down, cotangents, NN)
+    a, b = dots_left((gate, up), queries, NN)
+    (u,) = dots_left((down,), cotangents, NN)
     _, silu, _, slope = gates(a)
     da = split(lay, u * b * slope)
     db = split(lay, u * silu)
     h = split(lay, silu * b)
-    d_gate = dot_left(da, queries, NT)
-    d_up = dot_left(db, queries, NT)
-    d_down = dot_left(h, cotangents, NT)
+    d_gate, d_up = dots_left((da, db), queries, NT)
+    (d_down,) = dots_left((h,), cotangents, NT)
     outs = (pack_halves if lay.packed else pack_all)(
         lay, (d_gate, d_up, d_down), jnp.zeros((1, 1), F32)
     )
@@ -369,12 +389,8 @@
     rates = join_rates(lay, slabs)
     gate, up, down = (split(lay, w) for w in weights)
     gate_move, up_move, down_move = (split(lay, w) for w in moves)
-    a = dot_left(gate, keys, NN)
-    b = dot_left(up, keys, NN)
-    u = dot_left(down, values, NN)
-    ta = dot_left(gate_move, keys, NN)
-    tb = dot_left(up_move, keys, NN)
-    w = dot_left(down_move, values, NN)
+    a, b, ta, tb = dots_left((gate, up, gate_move, up_move), keys, NN)
+    u, w = dots_left((down, down_move), values, NN)
     sig, silu, rest, slope = gates(a)
     bend = sig * rest * (2.0 + a * (rest - sig))
     hidden = silu * b
@@ -388,7 +404,7 @@
     gtb = split(lay, um * silu)
     mh = split(lay, mu * hidden)
     md = split(lay, mu * hidden_dot)
-    grads = [dot_left(ga, keys, NT), dot_left(gb, keys, NT), dot_left(md, values, NT)]
+    grads = dots_left((ga, gb), keys, NT) + dots_left((md,), values, NT)
     turned = split(lay, cat([weights[0], weights[1], moves[0], moves[1]], 0).T)
     d_key = dot_both(turned, tuple(cat(x, 0) for x in zip(ga, gb, gta, gtb)), NN)
     turned = split(lay, cat([moves[2], weights[2]], 0).T)
@@ -443,12 +459,12 @@
     for n in range(count):
         pieces = [s[n * dim : (n + 1) * dim] for s in slabs]
         ordered = [
-            select_heads(lay, pieces, lay.heads - head_ids, h) for h in range(lay.heads)
+            select_steps(lay, pieces, head_ids, h) for h in range(lay.heads)
         ]
         outs.append(cat(ordered, 0).T.astype(BF16))
     if slabs[0].shape[0] > count * dim:
         pieces = [s[count * dim : count * dim + 1] for s in slabs]
-        rows = [select_heads(lay, pieces, lay.heads - head_ids, h) for h in range(lay.heads)]
+        rows = [select_steps(lay, pieces, head_ids, h) for h in range(lay.heads)]
         outs.append(cat(rows, 0))
     return outs
 
@@ -526,8 +542,13 @@
     def send(x, perm):
         return lax.ppermute(x, AXES, perm)
 
-    def over_heads(slabs):
-        return [slabs[0]] + [send(slabs[t], lay.head_perm(t)) for t in range(1, heads)]
+    def over_heads(slabs, hold=()):
+        close = [send(slabs[t], lay.head_perm(t)) for t in range(1, min(2, heads))]
+        away = slabs[2:]
+        if hold:
+            away = tie(lay, away, hold)
+        away = [send(x, lay.head_perm(t)) for t, x in enumerate(away, 2)]
+        return [slabs[0]] + close + away
 
     def over_cores(slabs):
         return [send(x, lay.core_perm()) for x in slabs] if lay.cores > 1 else []
@@ -538,7 +559,7 @@
         return run(lay, add_fn, (*parts[:heads], send(parts[heads], lay.core_perm())))
 
     def back_home(slabs):
-        return [slabs[0]] + [send(slabs[t], lay.head_perm(heads - t)) for t in range(1, heads)]
+        return [slabs[0]] + [send(slabs[t], lay.head_perm(t)) for t in range(1, heads)]
 
     def scatter(payloads):
         moved = [send(payloads[r], lay.scatter_perm(r)) for r in range(1, plane)]
@@ -549,18 +570,14 @@
 
     fn = functools.partial
     scale = math.sqrt(queries.shape[0] * lay.devices)
-    kv = over_heads(
-        run(
-            lay,
-            fn(spread_rows, lay, True),
-            (key_rows, value_rows, step_rates.T, head_ids),
-            always=True,
-        )
-    )
+    kv = run(
+        lay, fn(spread_rows, lay, True), (key_rows, value_rows, step_rates.T, head_ids), always=True
+    )
+    kv = over_heads(kv)
     qg = run(
         lay, fn(spread_rows, lay, False), (queries, out_grad, head_ids), always=True, deps=(kv[1],)
     )
-    qg = over_heads(qg)
+    qg = over_heads(qg, tuple(kv[2:]))
     kv = kv + over_cores(kv)
 
     owner_perms, table = owner_plan(lay)

time: 131 us -> 134 us (1.023)
  waiting for transfers between devices: 56.8 us -> 65.1 us
  starting transfers between devices: 51.7 us -> 47.9 us
  Pallas kernels: 14.6 us -> 13 us
    ppermute x36, waiting for transfers between devices: 56.8 us -> 65.1 us  [send(): return lax.ppermute(x, AXES, perm)]
    ppermute x36, starting transfers between devices: 51.7 us -> 47.9 us  [send(): return lax.ppermute(x, AXES, perm)]
    pallas_call x17, Pallas kernels: 14.6 us -> 13 us  [run(): pl.pallas_call(kernel, out_shape=[jax.ShapeDtypeStruct(s.shape, s.dtype)...]
  transfers between devices with their start and end apart: 36 -> 36, of which waited for: 15 -> 16; matrix products, arithmetic and copies ran while one was open for 2% -> 2% of each run, Pallas kernels for 4% -> 4%
where the time goes in v1:
time: 134 us; the launch traced here: 132 us
  waiting for transfers between devices  65.1 us (49%)
  starting transfers between devices  47.9 us (36%)
  Pallas kernels  13 us (10%)
  local copies, waits for them, and re-layouts  4.95 us (4%)
    ppermute x36, waiting for transfers between devices, send(): return lax.ppermute(x, AXES, perm)  65.1 us
    ppermute x36, starting transfers between devices, send(): return lax.ppermute(x, AXES, perm)  47.9 us
    pallas_call x17, Pallas kernels, run(): pl.pallas_call(kernel, out_shape=[jax.ShapeDtypeStruct(s.shape, s.dtype)...  13 us
    unnamed x13, local copies, waits for them, and re-layouts  2.88 us
  transfers between devices with their start and end apart: 36, of which 16 were waited for; matrix products, arithmetic and copies ran while one was open for 2% of the time, Pallas kernels for 4%

profile of v1, /device:TPU:0, one launch (start us, length us, event | category | flops | bytes accessed | tf_op | source)
XLA Modules:
  0.0 131.9 jit_solution(7069708519410821310)
XLA Ops:
  0.7 0.9 copy-done
  1.6 0.9 copy-done.1
  2.5 0.7 copy-done.4
  3.4 3.1 %collective-permute-start = (f32[392,128]{1,0:T(8,128)S(1)}, f32[392,128]{1,0:T(8,128)S(1)}, u32[]{:S(2)}, u32[]{:S(2)}) collective-permute-start(f32[392,128]{1,0:T(8,128)S(1)} %get-tuple-element.66), channel_id=1, source_target_pairs={{0,2},{1,3},{2,0},{3,1},{4,6},{5,7},{6,4},{7,5},{8,10},{9,11},{10,... | collective-permute-start | bytes 602120 | tf_op jit(solution)/shard_map/ppermute | solution.py:543
  6.5 2.6 %collective-permute-start.1 = (f32[392,128]{1,0:T(8,128)S(1)}, f32[392,128]{1,0:T(8,128)S(1)}, u32[]{:S(2)}, u32[]{:S(2)}) collective-permute-start(f32[392,128]{1,0:T(8,128)S(1)} %get-tuple-element.69), channel_id=1, source_target_pairs={{0,4},{1,5},{2,6},{3,7},{4,0},{5,1},{6,2},{7,3},{8,12},{9,13},{10,... | collective-permute-start | bytes 602120 | tf_op jit(solution)/shard_map/ppermute | solution.py:543
  9.1 1.4 %constant_dynamic-slice_fusion.3 = (f32[192,192]{1,0:T(8,128)S(1)}, f32[192,192]{1,0:T(8,128)S(1)}, f32[192,192]{1,0:T(8,128)S(1)}) fusion(f32[192,4608]{1,0:T(8,128)} %param.11, s32[]{:T(128)S(6)} %select_n.18, s32[]{:T(128)S(6)} %select_n.19, s32[]{:T(128)S(6)} %select_n.20), kind=kLoop, calls=%fused_computation.4 | loop fusion | bytes 884748 | tf_op jit(solution)/shard_map/dynamic_slice | solution.py:588
  10.9 4.2 %collective-permute-done.refs_2_.refs_6_ = f32[392,128]{1,0:T(8,128)S(1)} collective-permute-done((f32[392,128]{1,0:T(8,128)S(1)}, f32[392,128]{1,0:T(8,128)S(1)}, u32[]{:S(2)}, u32[]{:S(2)}) %collective-permute-start) | collective-permute-done | bytes 200736 | tf_op jit(solution)/shard_map/ppermute | solution.py:543
  15.1 8.8 %collective-permute-done.1.refs_3_.refs_7_ = f32[392,128]{1,0:T(8,128)S(1)} collective-permute-done((f32[392,128]{1,0:T(8,128)S(1)}, f32[392,128]{1,0:T(8,128)S(1)}, u32[]{:S(2)}, u32[]{:S(2)}) %collective-permute-start.1) | collective-permute-done | bytes 200736 | tf_op jit(solution)/shard_map/ppermute | solution.py:543
  24.4 0.7 constant_dynamic-slice_fusion.refs_3_.refs_8_.refs_4_.refs_5_
  25.1 0.7 shard_map.111
  25.9 1.2 shard_map.112
  27.1 1.6 %collective-permute-start.7 = (f32[440,128]{1,0:T(8,128)S(1)}, f32[440,128]{1,0:T(8,128)S(1)}, u32[]{:S(2)}, u32[]{:S(2)}) collective-permute-start(f32[440,128]{1,0:T(8,128)S(1)} %get-tuple-element.71.refs_0_), channel_id=1, source_target_pairs={{0,1},{1,0},{2,3},{3,2},{4,5},{5,4},{6,7},{7,6},{8,9},{9,8},{10,11... | collective-permute-start | bytes 675848 | tf_op jit(solution)/shard_map/ppermute | solution.py:543
  28.6 1.5 %collective-permute-start.8 = (f32[440,128]{1,0:T(8,128)S(1)}, f32[440,128]{1,0:T(8,128)S(1)}, u32[]{:S(2)}, u32[]{:S(2)}) collective-permute-start(f32[440,128]{1,0:T(8,128)S(1)} %get-tuple-element.72.refs_2_), channel_id=1, source_target_pairs={{0,16},{1,17},{2,18},{3,19},{4,20},{5,21},{6,22},{7,23},{8,24},{9,... | collective-permute-start | bytes 675848 | tf_op jit(solution)/shard_map/ppermute | solution.py:543
  30.1 4.4 %collective-permute-done.7.refs_1_ = f32[440,128]{1,0:T(8,128)S(1)} collective-permute-done((f32[440,128]{1,0:T(8,128)S(1)}, f32[440,128]{1,0:T(8,128)S(1)}, u32[]{:S(2)}, u32[]{:S(2)}) %collective-permute-start.7) | collective-permute-done | bytes 225312 | tf_op jit(solution)/shard_map/ppermute | solution.py:543
  34.5 1.2 collective-permute-done.8.refs_3_
  35.8 0.6 collective-permute-start.10
  36.6 3.6 %collective-permute-start.11 = (f32[384,128]{1,0:T(8,128)S(1)}, f32[384,128]{1,0:T(8,128)S(1)}, u32[]{:S(2)}, u32[]{:S(2)}) collective-permute-start(f32[384,128]{1,0:T(8,128)S(1)} %get-tuple-element.77), channel_id=1, source_target_pairs={{0,2},{1,3},{2,0},{3,1},{4,6},{5,7},{6,4},{7,5},{8,10},{9,11},{10,... | collective-permute-start | bytes 589832 | tf_op jit(solution)/shard_map/ppermute | solution.py:543
  40.2 1.1 collective-permute-start.12
  41.3 1.4 %collective-permute-start.13 = (f32[384,128]{1,0:T(8,128)S(1)}, f32[384,128]{1,0:T(8,128)S(1)}, u32[]{:S(2)}, u32[]{:S(2)}) collective-permute-start(f32[384,128]{1,0:T(8,128)S(1)} %get-tuple-element.81), channel_id=1, source_target_pairs={{0,6},{1,7},{2,4},{3,5},{4,2},{5,3},{6,0},{7,1},{8,14},{9,15},{10,... | collective-permute-start | bytes 589832 | tf_op jit(solution)/shard_map/ppermute | solution.py:543
  42.7 1.5 %collective-permute-start.9 = (f32[440,128]{1,0:T(8,128)S(1)}, f32[440,128]{1,0:T(8,128)S(1)}, u32[]{:S(2)}, u32[]{:S(2)}) collective-permute-start(f32[440,128]{1,0:T(8,128)S(1)} %get-tuple-element.73.refs_0_), channel_id=1, source_target_pairs={{0,16},{1,17},{2,18},{3,19},{4,20},{5,21},{6,22},{7,23},{8,24},{9,... | collective-permute-start | bytes 675848 | tf_op jit(solution)/shard_map/ppermute | solution.py:543
  44.2 2.9 %collective-permute-done.11.refs_1_ = f32[384,128]{1,0:T(8,128)S(1)} collective-permute-done((f32[384,128]{1,0:T(8,128)S(1)}, f32[384,128]{1,0:T(8,128)S(1)}, u32[]{:S(2)}, u32[]{:S(2)}) %collective-permute-start.11) | collective-permute-done | bytes 196640 | tf_op jit(solution)/shard_map/ppermute | solution.py:543
  47.2 10.1 %collective-permute-done.12.refs_2_ = f32[384,128]{1,0:T(8,128)S(1)} collective-permute-done((f32[384,128]{1,0:T(8,128)S(1)}, f32[384,128]{1,0:T(8,128)S(1)}, u32[]{:S(2)}, u32[]{:S(2)}) %collective-permute-start.12) | collective-permute-done | bytes 196640 | tf_op jit(solution)/shard_map/ppermute | solution.py:543
  59.6 2.1 %shard_map.118 = (f32[440,128]{1,0:T(8,128)S(1)}, f32[440,128]{1,0:T(8,128)S(1)}, f32[192,128]{1,0:T(8,128)S(1)}, f32[192,128]{1,0:T(8,128)S(1)}, f32[192,128]{1...) custom-call(f32[576,192]{1,0:T(8,128)S(1)} %get-tuple-element.75.refs_0_, ...), custom_call_target="tpu_custom_call" | custom-call | tf_op jit(solution)/shard_map/pallas_call | solution.py:505
  61.7 1.6 %collective-permute-start.22 = (f32[440,128]{1,0:T(8,128)S(1)}, f32[440,128]{1,0:T(8,128)S(1)}, u32[]{:S(2)}, u32[]{:S(2)}) collective-permute-start(f32[440,128]{1,0:T(8,128)S(1)} %get-tuple-element.95.refs_0_), channel_id=1, source_target_pairs={{0,1},{1,0},{2,3},{3,2},{4,5},{5,4},{6,7},{7,6},{8,9},{9,8},{10,11... | collective-permute-start | bytes 675848 | tf_op jit(solution)/shard_map/ppermute | solution.py:543
  63.3 1.5 %collective-permute-start.23 = (f32[440,128]{1,0:T(8,128)S(1)}, f32[440,128]{1,0:T(8,128)S(1)}, u32[]{:S(2)}, u32[]{:S(2)}) collective-permute-start(f32[440,128]{1,0:T(8,128)S(1)} %get-tuple-element.96.refs_2_), channel_id=1, source_target_pairs={{0,16},{1,17},{2,18},{3,19},{4,20},{5,21},{6,22},{7,23},{8,24},{9,... | collective-permute-start | bytes 675848 | tf_op jit(solution)/shard_map/ppermute | solution.py:543
  64.8 4.7 %collective-permute-done.22.refs_1_ = f32[440,128]{1,0:T(8,128)S(1)} collective-permute-done((f32[440,128]{1,0:T(8,128)S(1)}, f32[440,128]{1,0:T(8,128)S(1)}, u32[]{:S(2)}, u32[]{:S(2)}) %collective-permute-start.22) | collective-permute-done | bytes 225312 | tf_op jit(solution)/shard_map/ppermute | solution.py:543
  69.4 1.2 collective-permute-done.23.refs_3_
  70.7 1.5 %collective-permute-start.24 = (f32[440,128]{1,0:T(8,128)S(1)}, f32[440,128]{1,0:T(8,128)S(1)}, u32[]{:S(2)}, u32[]{:S(2)}) collective-permute-start(f32[440,128]{1,0:T(8,128)S(1)} %get-tuple-element.97.refs_0_), channel_id=1, source_target_pairs={{0,16},{1,17},{2,18},{3,19},{4,20},{5,21},{6,22},{7,23},{8,24},{9,... | collective-permute-start | bytes 675848 | tf_op jit(solution)/shard_map/ppermute | solution.py:543
  72.8 4.5 %collective-permute-done.24.refs_1_ = f32[440,128]{1,0:T(8,128)S(1)} collective-permute-done((f32[440,128]{1,0:T(8,128)S(1)}, f32[440,128]{1,0:T(8,128)S(1)}, u32[]{:S(2)}, u32[]{:S(2)}) %collective-permute-start.24) | collective-permute-done | bytes 225312 | tf_op jit(solution)/shard_map/ppermute | solution.py:543
  77.3 1.2 collective-permute-done.25.refs_3_
  78.4 0.8 shard_map.121
  79.3 2.2 %shard_map.122 = (f32[4,392,128]{2,1,0:T(8,128)S(1)}, f32[576,192]{1,0:T(8,128)S(1)}) custom-call(f32[576,192]{1,0:T(8,128)S(1)} %get-tuple-element.102.refs_0_, f32[8,128]{1,0:T(8,128)S(1)} %get-tuple-element.103.refs_1_, f32[576,192]{1,0:T(8,128)S(1)} %pad_maximum_fusion.refs_0_.refs_4_.refs_2_, f32[392,128]{1,0:T(8,128)S(1)} %collective-permute-done.3.refs_5_.refs_3_, ...), custom_call_target="tpu_custom_call" | custom-call | tf_op jit(solution)/shard_map/pallas_call | solution.py:505
  82.0 2.3 %shard_map.123 = (f32[224,128]{1,0:T(8,128)S(1)}, f32[224,128]{1,0:T(8,128)S(1)}, f32[224,128]{1,0:T(8,128)S(1)}, f32[224,128]{1,0:T(8,128)S(1)}, f32[392,128]{1...) custom-call(f32[576,192]{1,0:T(8,128)S(1)} %get-tuple-element.102.refs_0_, ...), custom_call_target="tpu_custom_call" | custom-call | tf_op jit(solution)/shard_map/pallas_call | solution.py:505
  84.4 0.6 collective-permute-start.30
  85.0 2.8 %collective-permute-start.19 = (f32[192,128]{1,0:T(8,128)S(1)}, f32[192,128]{1,0:T(8,128)S(1)}, u32[]{:S(2)}, u32[]{:S(2)}) collective-permute-start(f32[192,128]{1,0:T(8,128)S(1)} %get-tuple-element.92), channel_id=1, source_target_pairs={{0,2},{1,3},{2,0},{3,1},{4,6},{5,7},{6,4},{7,5},{8,10},{9,11},{10,... | collective-permute-start | bytes 294920 | tf_op jit(solution)/shard_map/ppermute | solution.py:543
  87.8 0.5 collective-permute-start.31
  88.3 2.4 %collective-permute-start.32 = (f32[224,128]{1,0:T(8,128)S(1)}, f32[224,128]{1,0:T(8,128)S(1)}, u32[]{:S(2)}, u32[]{:S(2)}) collective-permute-start(f32[224,128]{1,0:T(8,128)S(1)} %get-tuple-element.120), channel_id=1, source_target_pairs={{0,17},{1,16},{2,19},{3,18},{4,21},{5,20},{6,23},{7,22},{8,25},{9,... | collective-permute-start | bytes 344072 | tf_op jit(solution)/shard_map/ppermute | solution.py:543
  91.0 2.9 %collective-permute-start.28 = (f32[392,128]{1,0:T(8,128)S(1)}, f32[392,128]{1,0:T(8,128)S(1)}, u32[]{:S(2)}, u32[]{:S(2)}) collective-permute-start(f32[392,128]{1,0:T(8,128)S(1)} %get-tuple-element.113), channel_id=1, source_target_pairs={{0,4},{1,5},{2,6},{3,7},{4,0},{5,1},{6,2},{7,3},{8,12},{9,13},{10,... | collective-permute-start | bytes 602120 | tf_op jit(solution)/shard_map/ppermute | solution.py:543
  93.9 1.4 %collective-permute-start.29 = (f32[392,128]{1,0:T(8,128)S(1)}, f32[392,128]{1,0:T(8,128)S(1)}, u32[]{:S(2)}, u32[]{:S(2)}) collective-permute-start(f32[392,128]{1,0:T(8,128)S(1)} %get-tuple-element.114), channel_id=1, source_target_pairs={{0,6},{1,7},{2,4},{3,5},{4,2},{5,3},{6,0},{7,1},{8,14},{9,15},{10,... | collective-permute-start | bytes 602120 | tf_op jit(solution)/shard_map/ppermute | solution.py:543
  95.7 2.4 %collective-permute-start.21 = (f32[192,128]{1,0:T(8,128)S(1)}, f32[192,128]{1,0:T(8,128)S(1)}, u32[]{:S(2)}, u32[]{:S(2)}) collective-permute-start(f32[192,128]{1,0:T(8,128)S(1)} %get-tuple-element.94), channel_id=1, source_target_pairs={{0,6},{1,7},{2,4},{3,5},{4,2},{5,3},{6,0},{7,1},{8,14},{9,15},{10,... | collective-permute-start | bytes 294920 | tf_op jit(solution)/shard_map/ppermute | solution.py:543
  98.3 19.8 %collective-permute-done.20.refs_2_ = f32[192,128]{1,0:T(8,128)S(1)} collective-permute-done((f32[192,128]{1,0:T(8,128)S(1)}, f32[192,128]{1,0:T(8,128)S(1)}, u32[]{:S(2)}, u32[]{:S(2)}) %collective-permute-start.20) | collective-permute-done | bytes 98336 | tf_op jit(solution)/shard_map/ppermute | solution.py:543
  118.1 0.7 collective-permute-start.33
  118.8 0.8 collective-permute-start.34
  119.5 9.0 %collective-permute-start.35 = (f32[48,192]{1,0:T(8,128)S(1)}, f32[48,192]{1,0:T(8,128)S(1)}, u32[]{:S(2)}, u32[]{:S(2)}) collective-permute-start(f32[48,192]{1,0:T(8,128)S(1)} %get-tuple-element.124), channel_id=1, source_target_pairs={{0,21},{1,11},{2,2},{3,24},{4,16},{5,5},{6,8},{7,29},{8,12},{9,1},... | collective-permute-start | bytes 110600 | tf_op jit(solution)/shard_map/ppermute | solution.py:543
  128.5 0.8 shard_map.124
  129.3 0.9 collective-permute-done.35.refs_2_
  130.2 0.7 shard_map.128
  131.0 0.9 shard_map.126
  (69 shorter events, 5.7 us)
Async XLA Ops:
  0.7 0.9 copy-start
  1.6 0.9 copy-start.1
  2.5 0.7 copy-start.4
  3.4 11.7 %collective-permute-start = (f32[392,128]{1,0:T(8,128)S(1)}, f32[392,128]{1,0:T(8,128)S(1)}, u32[]{:S(2)}, u32[]{:S(2)}) collective-permute-start(f32[392,128]{1,0:T(8,128)S(1)} %get-tuple-element.66), channel_id=1, source_target_pairs={{0,2},{1,3},{2,0},{3,1},{4,6},{5,7},{6,4},{7,5},{8,10},{9,11},{10,... | collective-permute-start | bytes 602120 | tf_op jit(solution)/shard_map/ppermute | solution.py:543
  6.5 17.4 %collective-permute-start.1 = (f32[392,128]{1,0:T(8,128)S(1)}, f32[392,128]{1,0:T(8,128)S(1)}, u32[]{:S(2)}, u32[]{:S(2)}) collective-permute-start(f32[392,128]{1,0:T(8,128)S(1)} %get-tuple-element.69), channel_id=1, source_target_pairs={{0,4},{1,5},{2,6},{3,7},{4,0},{5,1},{6,2},{7,3},{8,12},{9,13},{10,... | collective-permute-start | bytes 602120 | tf_op jit(solution)/shard_map/ppermute | solution.py:543
  9.1 14.8 %collective-permute-start.2 = (f32[392,128]{1,0:T(8,128)S(1)}, f32[392,128]{1,0:T(8,128)S(1)}, u32[]{:S(2)}, u32[]{:S(2)}) collective-permute-start(f32[392,128]{1,0:T(8,128)S(1)} %get-tuple-element.70), channel_id=1, source_target_pairs={{0,6},{1,7},{2,4},{3,5},{4,2},{5,3},{6,0},{7,1},{8,14},{9,15},{10,... | collective-permute-start | bytes 602120 | tf_op jit(solution)/shard_map/ppermute | solution.py:543
  9.1 16.7 %collective-permute-start.3 = (f32[392,128]{1,0:T(8,128)S(1)}, f32[392,128]{1,0:T(8,128)S(1)}, u32[]{:S(2)}, u32[]{:S(2)}) collective-permute-start(f32[392,128]{1,0:T(8,128)S(1)} %get-tuple-element.65.refs_1_.refs_5_), channel_id=1, source_target_pairs={{0,8},{1,9},{2,10},{3,11},{4,12},{5,13},{6,14},{7,15},{8,0},{9,1},... | collective-permute-start | bytes 602120 | tf_op jit(solution)/shard_map/ppermute | solution.py:543
  10.5 25.9 %copy-start.2 = (bf16[128,768]{1,0:T(8,128)(2,1)S(1)}, bf16[128,768]{1,0:T(8,128)(2,1)}, u32[]{:S(2)}) copy-start(bf16[128,768]{1,0:T(8,128)(2,1)} %refs_0_.3) | copy-start | bytes 589828
  10.5 25.9 %copy-start.3 = (bf16[128,768]{1,0:T(8,128)(2,1)S(1)}, bf16[128,768]{1,0:T(8,128)(2,1)}, u32[]{:S(2)}) copy-start(bf16[128,768]{1,0:T(8,128)(2,1)} %refs_1_.3) | copy-start | bytes 589828
  15.1 10.8 %collective-permute-start.4 = (f32[392,128]{1,0:T(8,128)S(1)}, f32[392,128]{1,0:T(8,128)S(1)}, u32[]{:S(2)}, u32[]{:S(2)}) collective-permute-start(f32[392,128]{1,0:T(8,128)S(1)} %collective-permute-done.refs_2_.refs_6_), channel_id=1, source_target_pairs={{0,8},{1,9},{2,10},{3,11},{4,12},{5,13},{6,14},{7,15},{8,0},{9,1},... | collective-permute-start | bytes 602120 | tf_op jit(solution)/shard_map/ppermute | solution.py:543
  23.9 2.0 %collective-permute-start.5 = (f32[392,128]{1,0:T(8,128)S(1)}, f32[392,128]{1,0:T(8,128)S(1)}, u32[]{:S(2)}, u32[]{:S(2)}) collective-permute-start(f32[392,128]{1,0:T(8,128)S(1)} %collective-permute-done.1.refs_3_.refs_7_), channel_id=1, source_target_pairs={{0,8},{1,9},{2,10},{3,11},{4,12},{5,13},{6,14},{7,15},{8,0},{9,1},... | collective-permute-start | bytes 602120 | tf_op jit(solution)/shard_map/ppermute | solution.py:543
  23.9 2.0 %collective-permute-start.6 = (f32[392,128]{1,0:T(8,128)S(1)}, f32[392,128]{1,0:T(8,128)S(1)}, u32[]{:S(2)}, u32[]{:S(2)}) collective-permute-start(f32[392,128]{1,0:T(8,128)S(1)} %collective-permute-done.2.refs_4_.refs_8_), channel_id=1, source_target_pairs={{0,8},{1,9},{2,10},{3,11},{4,12},{5,13},{6,14},{7,15},{8,0},{9,1},... | collective-permute-start | bytes 602120 | tf_op jit(solution)/shard_map/ppermute | solution.py:543
  27.1 7.5 %collective-permute-start.7 = (f32[440,128]{1,0:T(8,128)S(1)}, f32[440,128]{1,0:T(8,128)S(1)}, u32[]{:S(2)}, u32[]{:S(2)}) collective-permute-start(f32[440,128]{1,0:T(8,128)S(1)} %get-tuple-element.71.refs_0_), channel_id=1, source_target_pairs={{0,1},{1,0},{2,3},{3,2},{4,5},{5,4},{6,7},{7,6},{8,9},{9,8},{10,11... | collective-permute-start | bytes 675848 | tf_op jit(solution)/shard_map/ppermute | solution.py:543
  28.6 7.1 %collective-permute-start.8 = (f32[440,128]{1,0:T(8,128)S(1)}, f32[440,128]{1,0:T(8,128)S(1)}, u32[]{:S(2)}, u32[]{:S(2)}) collective-permute-start(f32[440,128]{1,0:T(8,128)S(1)} %get-tuple-element.72.refs_2_), channel_id=1, source_target_pairs={{0,16},{1,17},{2,18},{3,19},{4,20},{5,21},{6,22},{7,23},{8,24},{9,... | collective-permute-start | bytes 675848 | tf_op jit(solution)/shard_map/ppermute | solution.py:543
  35.8 22.0 %collective-permute-start.10 = (f32[440,128]{1,0:T(8,128)S(1)}, f32[440,128]{1,0:T(8,128)S(1)}, u32[]{:S(2)}, u32[]{:S(2)}) collective-permute-start(f32[440,128]{1,0:T(8,128)S(1)} %get-tuple-element.74.refs_2_), channel_id=1, source_target_pairs={{0,1},{1,0},{2,3},{3,2},{4,5},{5,4},{6,7},{7,6},{8,9},{9,8},{10,11... | collective-permute-start | bytes 675848 | tf_op jit(solution)/shard_map/ppermute | solution.py:543
  36.6 10.5 %collective-permute-start.11 = (f32[384,128]{1,0:T(8,128)S(1)}, f32[384,128]{1,0:T(8,128)S(1)}, u32[]{:S(2)}, u32[]{:S(2)}) collective-permute-start(f32[384,128]{1,0:T(8,128)S(1)} %get-tuple-element.77), channel_id=1, source_target_pairs={{0,2},{1,3},{2,0},{3,1},{4,6},{5,7},{6,4},{7,5},{8,10},{9,11},{10,... | collective-permute-start | bytes 589832 | tf_op jit(solution)/shard_map/ppermute | solution.py:543
  40.2 17.1 %collective-permute-start.12 = (f32[384,128]{1,0:T(8,128)S(1)}, f32[384,128]{1,0:T(8,128)S(1)}, u32[]{:S(2)}, u32[]{:S(2)}) collective-permute-start(f32[384,128]{1,0:T(8,128)S(1)} %get-tuple-element.80), channel_id=1, source_target_pairs={{0,4},{1,5},{2,6},{3,7},{4,0},{5,1},{6,2},{7,3},{8,12},{9,13},{10,... | collective-permute-start | bytes 589832 | tf_op jit(solution)/shard_map/ppermute | solution.py:543
  41.3 16.0 %collective-permute-start.13 = (f32[384,128]{1,0:T(8,128)S(1)}, f32[384,128]{1,0:T(8,128)S(1)}, u32[]{:S(2)}, u32[]{:S(2)}) collective-permute-start(f32[384,128]{1,0:T(8,128)S(1)} %get-tuple-element.81), channel_id=1, source_target_pairs={{0,6},{1,7},{2,4},{3,5},{4,2},{5,3},{6,0},{7,1},{8,14},{9,15},{10,... | collective-permute-start | bytes 589832 | tf_op jit(solution)/shard_map/ppermute | solution.py:543
  42.7 15.6 %collective-permute-start.9 = (f32[440,128]{1,0:T(8,128)S(1)}, f32[440,128]{1,0:T(8,128)S(1)}, u32[]{:S(2)}, u32[]{:S(2)}) collective-permute-start(f32[440,128]{1,0:T(8,128)S(1)} %get-tuple-element.73.refs_0_), channel_id=1, source_target_pairs={{0,16},{1,17},{2,18},{3,19},{4,20},{5,21},{6,22},{7,23},{8,24},{9,... | collective-permute-start | bytes 675848 | tf_op jit(solution)/shard_map/ppermute | solution.py:543
  57.3 1.5 %collective-permute-start.14 = (f32[384,128]{1,0:T(8,128)S(1)}, f32[384,128]{1,0:T(8,128)S(1)}, u32[]{:S(2)}, u32[]{:S(2)}) collective-permute-start(f32[384,128]{1,0:T(8,128)S(1)} %get-tuple-element.82.refs_1_), channel_id=1, source_target_pairs={{0,8},{1,9},{2,10},{3,11},{4,12},{5,13},{6,14},{7,15},{8,0},{9,1},... | collective-permute-start | bytes 589832 | tf_op jit(solution)/shard_map/ppermute | solution.py:543
  57.3 1.7 %collective-permute-start.15 = (f32[384,128]{1,0:T(8,128)S(1)}, f32[384,128]{1,0:T(8,128)S(1)}, u32[]{:S(2)}, u32[]{:S(2)}) collective-permute-start(f32[384,128]{1,0:T(8,128)S(1)} %get-tuple-element.83.refs_2_), channel_id=1, source_target_pairs={{0,8},{1,9},{2,10},{3,11},{4,12},{5,13},{6,14},{7,15},{8,0},{9,1},... | collective-permute-start | bytes 589832 | tf_op jit(solution)/shard_map/ppermute | solution.py:543
  57.8 1.5 %collective-permute-start.16 = (f32[384,128]{1,0:T(8,128)S(1)}, f32[384,128]{1,0:T(8,128)S(1)}, u32[]{:S(2)}, u32[]{:S(2)}) collective-permute-start(f32[384,128]{1,0:T(8,128)S(1)} %get-tuple-element.84.refs_3_), channel_id=1, source_target_pairs={{0,8},{1,9},{2,10},{3,11},{4,12},{5,13},{6,14},{7,15},{8,0},{9,1},... | collective-permute-start | bytes 589832 | tf_op jit(solution)/shard_map/ppermute | solution.py:543
  57.9 1.7 %collective-permute-start.17 = (f32[384,128]{1,0:T(8,128)S(1)}, f32[384,128]{1,0:T(8,128)S(1)}, u32[]{:S(2)}, u32[]{:S(2)}) collective-permute-start(f32[384,128]{1,0:T(8,128)S(1)} %get-tuple-element.85.refs_4_), channel_id=1, source_target_pairs={{0,8},{1,9},{2,10},{3,11},{4,12},{5,13},{6,14},{7,15},{8,0},{9,1},... | collective-permute-start | bytes 589832 | tf_op jit(solution)/shard_map/ppermute | solution.py:543
  61.7 7.7 %collective-permute-start.22 = (f32[440,128]{1,0:T(8,128)S(1)}, f32[440,128]{1,0:T(8,128)S(1)}, u32[]{:S(2)}, u32[]{:S(2)}) collective-permute-start(f32[440,128]{1,0:T(8,128)S(1)} %get-tuple-element.95.refs_0_), channel_id=1, source_target_pairs={{0,1},{1,0},{2,3},{3,2},{4,5},{5,4},{6,7},{7,6},{8,9},{9,8},{10,11... | collective-permute-start | bytes 675848 | tf_op jit(solution)/shard_map/ppermute | solution.py:543
  63.3 7.4 %collective-permute-start.23 = (f32[440,128]{1,0:T(8,128)S(1)}, f32[440,128]{1,0:T(8,128)S(1)}, u32[]{:S(2)}, u32[]{:S(2)}) collective-permute-start(f32[440,128]{1,0:T(8,128)S(1)} %get-tuple-element.96.refs_2_), channel_id=1, source_target_pairs={{0,16},{1,17},{2,18},{3,19},{4,20},{5,21},{6,22},{7,23},{8,24},{9,... | collective-permute-start | bytes 675848 | tf_op jit(solution)/shard_map/ppermute | solution.py:543
  70.7 6.6 %collective-permute-start.24 = (f32[440,128]{1,0:T(8,128)S(1)}, f32[440,128]{1,0:T(8,128)S(1)}, u32[]{:S(2)}, u32[]{:S(2)}) collective-permute-start(f32[440,128]{1,0:T(8,128)S(1)} %get-tuple-element.97.refs_0_), channel_id=1, source_target_pairs={{0,16},{1,17},{2,18},{3,19},{4,20},{5,21},{6,22},{7,23},{8,24},{9,... | collective-permute-start | bytes 675848 | tf_op jit(solution)/shard_map/ppermute | solution.py:543
  72.2 6.2 %collective-permute-start.25 = (f32[440,128]{1,0:T(8,128)S(1)}, f32[440,128]{1,0:T(8,128)S(1)}, u32[]{:S(2)}, u32[]{:S(2)}) collective-permute-start(f32[440,128]{1,0:T(8,128)S(1)} %get-tuple-element.98.refs_2_), channel_id=1, source_target_pairs={{0,1},{1,0},{2,3},{3,2},{4,5},{5,4},{6,7},{7,6},{8,9},{9,8},{10,11... | collective-permute-start | bytes 675848 | tf_op jit(solution)/shard_map/ppermute | solution.py:543
  81.5 9.3 %collective-permute-start.26 = (f32[4,392,128]{2,1,0:T(8,128)S(1)}, f32[4,392,128]{2,1,0:T(8,128)S(1)}, u32[]{:S(2)}, u32[]{:S(2)}) collective-permute-start(f32[4,392,128]{2,1,0:T(8,128)S(1)} %get-tuple-element.110), channel_id=1, source_target_pairs={{0,8},{1,9},{2,10},{3,11},{4,12},{5,13},{6,14},{7,15},{8,0},{9,1},... | collective-permute-start | bytes 2408456 | tf_op jit(solution)/shard_map/ppermute | solution.py:543
  81.5 3.4 %collective-permute-start.18 = (f32[4,192,128]{2,1,0:T(8,128)S(1)}, f32[4,192,128]{2,1,0:T(8,128)S(1)}, u32[]{:S(2)}, u32[]{:S(2)}) collective-permute-start(f32[4,192,128]{2,1,0:T(8,128)S(1)} %get-tuple-element.90), channel_id=1, source_target_pairs={{0,8},{1,9},{2,10},{3,11},{4,12},{5,13},{6,14},{7,15},{8,0},{9,1},... | collective-permute-start | bytes 1179656 | tf_op jit(solution)/shard_map/ppermute | solution.py:543
  84.4 9.6 %collective-permute-start.30 = (f32[224,128]{1,0:T(8,128)S(1)}, f32[224,128]{1,0:T(8,128)S(1)}, u32[]{:S(2)}, u32[]{:S(2)}) collective-permute-start(f32[224,128]{1,0:T(8,128)S(1)} %get-tuple-element.118), channel_id=1, source_target_pairs={{0,1},{1,0},{2,3},{3,2},{4,5},{5,4},{6,7},{7,6},{8,9},{9,8},{10,11... | collective-permute-start | bytes 344072 | tf_op jit(solution)/shard_map/ppermute | solution.py:543
  85.0 6.0 %collective-permute-start.19 = (f32[192,128]{1,0:T(8,128)S(1)}, f32[192,128]{1,0:T(8,128)S(1)}, u32[]{:S(2)}, u32[]{:S(2)}) collective-permute-start(f32[192,128]{1,0:T(8,128)S(1)} %get-tuple-element.92), channel_id=1, source_target_pairs={{0,2},{1,3},{2,0},{3,1},{4,6},{5,7},{6,4},{7,5},{8,10},{9,11},{10,... | collective-permute-start | bytes 294920 | tf_op jit(solution)/shard_map/ppermute | solution.py:543
  87.8 7.5 %collective-permute-start.31 = (f32[224,128]{1,0:T(8,128)S(1)}, f32[224,128]{1,0:T(8,128)S(1)}, u32[]{:S(2)}, u32[]{:S(2)}) collective-permute-start(f32[224,128]{1,0:T(8,128)S(1)} %get-tuple-element.119), channel_id=1, source_target_pairs={{0,16},{1,17},{2,18},{3,19},{4,20},{5,21},{6,22},{7,23},{8,24},{9,... | collective-permute-start | bytes 344072 | tf_op jit(solution)/shard_map/ppermute | solution.py:543
  88.3 7.4 %collective-permute-start.32 = (f32[224,128]{1,0:T(8,128)S(1)}, f32[224,128]{1,0:T(8,128)S(1)}, u32[]{:S(2)}, u32[]{:S(2)}) collective-permute-start(f32[224,128]{1,0:T(8,128)S(1)} %get-tuple-element.120), channel_id=1, source_target_pairs={{0,17},{1,16},{2,19},{3,18},{4,21},{5,20},{6,23},{7,22},{8,25},{9,... | collective-permute-start | bytes 344072 | tf_op jit(solution)/shard_map/ppermute | solution.py:543
  90.9 40.1 %collective-permute-start.27 = (f32[392,128]{1,0:T(8,128)S(1)}, f32[392,128]{1,0:T(8,128)S(1)}, u32[]{:S(2)}, u32[]{:S(2)}) collective-permute-start(f32[392,128]{1,0:T(8,128)S(1)} %get-tuple-element.112), channel_id=1, source_target_pairs={{0,2},{1,3},{2,0},{3,1},{4,6},{5,7},{6,4},{7,5},{8,10},{9,11},{10,... | collective-permute-start | bytes 602120 | tf_op jit(solution)/shard_map/ppermute | solution.py:543
  91.0 40.0 %collective-permute-start.28 = (f32[392,128]{1,0:T(8,128)S(1)}, f32[392,128]{1,0:T(8,128)S(1)}, u32[]{:S(2)}, u32[]{:S(2)}) collective-permute-start(f32[392,128]{1,0:T(8,128)S(1)} %get-tuple-element.113), channel_id=1, source_target_pairs={{0,4},{1,5},{2,6},{3,7},{4,0},{5,1},{6,2},{7,3},{8,12},{9,13},{10,... | collective-permute-start | bytes 602120 | tf_op jit(solution)/shard_map/ppermute | solution.py:543
  93.9 37.1 %collective-permute-start.29 = (f32[392,128]{1,0:T(8,128)S(1)}, f32[392,128]{1,0:T(8,128)S(1)}, u32[]{:S(2)}, u32[]{:S(2)}) collective-permute-start(f32[392,128]{1,0:T(8,128)S(1)} %get-tuple-element.114), channel_id=1, source_target_pairs={{0,6},{1,7},{2,4},{3,5},{4,2},{5,3},{6,0},{7,1},{8,14},{9,15},{10,... | collective-permute-start | bytes 602120 | tf_op jit(solution)/shard_map/ppermute | solution.py:543
  95.3 22.8 %collective-permute-start.20 = (f32[192,128]{1,0:T(8,128)S(1)}, f32[192,128]{1,0:T(8,128)S(1)}, u32[]{:S(2)}, u32[]{:S(2)}) collective-permute-start(f32[192,128]{1,0:T(8,128)S(1)} %get-tuple-element.93), channel_id=1, source_target_pairs={{0,4},{1,5},{2,6},{3,7},{4,0},{5,1},{6,2},{7,3},{8,12},{9,13},{10,... | collective-permute-start | bytes 294920 | tf_op jit(solution)/shard_map/ppermute | solution.py:543
  95.7 23.0 %collective-permute-start.21 = (f32[192,128]{1,0:T(8,128)S(1)}, f32[192,128]{1,0:T(8,128)S(1)}, u32[]{:S(2)}, u32[]{:S(2)}) collective-permute-start(f32[192,128]{1,0:T(8,128)S(1)} %get-tuple-element.94), channel_id=1, source_target_pairs={{0,6},{1,7},{2,4},{3,5},{4,2},{5,3},{6,0},{7,1},{8,14},{9,15},{10,... | collective-permute-start | bytes 294920 | tf_op jit(solution)/shard_map/ppermute | solution.py:543
  118.1 1.4 %collective-permute-start.33 = (f32[48,192]{1,0:T(8,128)S(1)}, f32[48,192]{1,0:T(8,128)S(1)}, u32[]{:S(2)}, u32[]{:S(2)}) collective-permute-start(f32[48,192]{1,0:T(8,128)S(1)} %get-tuple-element.122), channel_id=1, source_target_pairs={{0,0},{1,21},{2,13},{3,3},{4,5},{5,27},{6,18},{7,8},{8,22},{9,12},... | collective-permute-start | bytes 110600 | tf_op jit(solution)/shard_map/ppermute | solution.py:543
  118.8 10.6 %collective-permute-start.34 = (f32[48,192]{1,0:T(8,128)S(1)}, f32[48,192]{1,0:T(8,128)S(1)}, u32[]{:S(2)}, u32[]{:S(2)}) collective-permute-start(f32[48,192]{1,0:T(8,128)S(1)} %get-tuple-element.123), channel_id=1, source_target_pairs={{0,10},{1,0},{2,24},{3,13},{4,26},{5,16},{6,29},{7,19},{8,1},{9,23... | collective-permute-start | bytes 110600 | tf_op jit(solution)/shard_map/ppermute | solution.py:543
  119.5 10.7 %collective-permute-start.35 = (f32[48,192]{1,0:T(8,128)S(1)}, f32[48,192]{1,0:T(8,128)S(1)}, u32[]{:S(2)}, u32[]{:S(2)}) collective-permute-start(f32[48,192]{1,0:T(8,128)S(1)} %get-tuple-element.124), channel_id=1, source_target_pairs={{0,21},{1,11},{2,2},{3,24},{4,16},{5,5},{6,8},{7,29},{8,12},{9,1},... | collective-permute-start | bytes 110600 | tf_op jit(solution)/shard_map/ppermute | solution.py:543

commit v2 on v1

--- a/solution.py
+++ b/solution.py
@@ -30,9 +30,11 @@
         self.packed = (
             head_dim == LANES + LANES // 2
             and rows % (2 * SUBLANES) == 0
-            and (3 * self.half) % (4 * SUBLANES) == 0
+            and (3 * self.half) % (2 * SUBLANES) == 0
             and self.pow2
             and self.plane > 1
+            and self.cores == 2
+            and heads > 2
         )
 
     def place(self, device):
@@ -174,16 +176,21 @@
     return cat([payload[:rows], tail], 1), payload[rows + rows // 2 : rows + rows // 2 + 1, :1]
 
 
-def pack_halves(lay, grads, extra):
-    body = cat(grads, 0)
-    rows = body.shape[0] // 2
+def wide_rows(lay):
+    step = 2 * SUBLANES
+    total = 3 * lay.half
+    return total - total * 5 // 12 // step * step
+
+
+def pack_parts(lay, grads, extra):
+    body, rows = cat(grads, 0), wide_rows(lay)
     return [pack(lay, body[:rows], extra), pack(lay, body[rows:], extra)]
 
 
-def unpack_halves(lay, first, first_in, second, second_in):
-    rows = 3 * lay.half // 2
+def unpack_parts(lay, first, first_in, second, second_in):
+    rows = wide_rows(lay)
     top, extra = unpack(lay, first + first_in, rows)
-    bottom, _ = unpack(lay, second + second_in, rows)
+    bottom, _ = unpack(lay, second + second_in, 3 * lay.half - rows)
     return cat([top, bottom], 0), extra
 
 
@@ -295,7 +302,7 @@
 def update_rest_fn(lay, weights, before, total_before, *slabs):
     grads, total = update_math(lay, slabs, weights)
     grads = [g + b for g, b in zip(grads, in_three(lay, before))]
-    return pack_halves(lay, grads, total + total_before[0:1, 0:1])
+    return pack_parts(lay, grads, total + total_before[0:1, 0:1])
 
 
 def norms(initial, moved):
@@ -319,16 +326,12 @@
 
 
 def renorm_all_fn(lay, coefficient, *args):
-    body, total = unpack_halves(lay, *args[:4])
+    body, total = unpack_parts(lay, *args[:4])
     new, grad, moved = renormed(coefficient, body, total, args[4])
     return [new, grad, moved, jnp.broadcast_to(total, (SUBLANES, LANES))]
 
 
-def apply_fn(lay, *args):
-    if lay.packed:
-        weights, slabs = in_three(lay, args[0]), args[1:]
-    else:
-        weights, slabs = unpack_all(lay, args[: lay.plane]), args[lay.plane :]
+def apply_math(lay, slabs, weights):
     queries, cotangents = join_rows(lay, slabs)
     gate, up, down = (split(lay, w) for w in weights)
     a, b = dots_left((gate, up), queries, NN)
@@ -337,18 +340,32 @@
     da = split(lay, u * b * slope)
     db = split(lay, u * silu)
     h = split(lay, silu * b)
-    d_gate, d_up = dots_left((da, db), queries, NT)
-    (d_down,) = dots_left((h,), cotangents, NT)
-    outs = (pack_halves if lay.packed else pack_all)(
-        lay, (d_gate, d_up, d_down), jnp.zeros((1, 1), F32)
-    )
+    grads = dots_left((da, db), queries, NT) + dots_left((h,), cotangents, NT)
     turned = split(lay, cat([weights[0], weights[1]], 0).T)
     both = tuple(cat([x, y], 0) for x, y in zip(da, db))
     d_query = dot_both(turned, both, NN)
     rows = slabs[0].shape[1]
-    cut = [d_query[:, i * rows : (i + 1) * rows] for i in range(len(slabs))]
+    return grads, [d_query[:, i * rows : (i + 1) * rows] for i in range(len(slabs))]
+
+
+def apply_fn(lay, *args):
+    weights, slabs = unpack_all(lay, args[: lay.plane]), args[lay.plane :]
+    grads, parts = apply_math(lay, slabs, weights)
+    outs = pack_all(lay, grads, jnp.zeros((1, 1), F32))
     heads = lay.heads
-    return outs + cut[:heads] + ([stack(cut[heads:])] if lay.cores > 1 else [])
+    return outs + parts[:heads] + ([stack(parts[heads:])] if lay.cores > 1 else [])
+
+
+def apply_near_fn(lay, count, new, *slabs):
+    grads, parts = apply_math(lay, slabs, in_three(lay, new))
+    return [cat(grads, 0), *parts[:count], stack(parts[count:])]
+
+
+def apply_far_fn(lay, count, new, before, *slabs):
+    grads, parts = apply_math(lay, slabs, in_three(lay, new))
+    grads = [g + b for g, b in zip(grads, in_three(lay, before))]
+    outs = pack_parts(lay, grads, jnp.zeros((1, 1), F32))
+    return outs + [*parts[:count], stack(parts[count:])]
 
 
 def stack(parts):
@@ -375,7 +392,7 @@
 
 
 def renorm_back_all_fn(lay, coefficient, *args):
-    d_new, _ = unpack_halves(lay, *args[:4])
+    d_new, _ = unpack_parts(lay, *args[:4])
     initial, grad, moved, total, places = args[4:]
     move, d_total, direct = renormed_back(
         coefficient, d_new, total[0:1, 0:1], initial, grad, moved
@@ -429,23 +446,29 @@
     return outs + parts[:heads] + ([stack(parts[heads:])] if lay.cores > 1 else [])
 
 
-def pull_other_fn(lay, *args):
-    moves, d_total, weights, slabs = args[0], args[1], args[2], args[3:]
+def pull_other_fn(lay, moves, d_total, weights, *slabs):
     grads, parts = pull_math(
         lay, slabs, in_three(lay, weights), in_three(lay, moves), d_total[0:1, 0:1]
     )
     return [stack(parts), cat(grads, 0)]
 
 
-def pull_own_fn(lay, *args):
-    moves, d_total, weights, before, places, slabs = *args[:5], args[5:]
+def pull_own_fn(lay, moves, d_total, weights, before, *slabs):
+    grads, parts = pull_math(
+        lay, slabs, in_three(lay, weights), in_three(lay, moves), d_total[0:1, 0:1]
+    )
+    return [cat(grads, 0) + before, *parts]
+
+
+def pull_last_fn(lay, count, moves, d_total, weights, before, places, *slabs):
     grads, parts = pull_math(
         lay, slabs, in_three(lay, weights), in_three(lay, moves), d_total[0:1, 0:1]
     )
     grads = [g + b for g, b in zip(grads, in_three(lay, before))]
     slots, member = in_slots(lay, grads), member_id(places)
     zero = jnp.zeros((1, 1), F32)
-    return [pack(lay, choose(slots, member ^ r), zero) for r in range(lay.plane)] + parts
+    outs = [pack(lay, choose(slots, member ^ r), zero) for r in range(lay.plane)]
+    return outs + [*parts[:count], stack(parts[count:])]
 
 
 def add_two_fn(first, first_in, second, second_in):
@@ -558,8 +581,13 @@
             return parts
         return run(lay, add_fn, (*parts[:heads], send(parts[heads], lay.core_perm())))
 
+    def add_home(parts, away):
+        return list(run(lay, add_fn, (*parts, send(away, lay.core_perm()))))
+
     def back_home(slabs):
-        return [slabs[0]] + [send(slabs[t], lay.head_perm(t)) for t in range(1, heads)]
+        away = [send(slabs[t], lay.head_perm(t)) for t in range(2, heads)]
+        close = [send(slabs[t], lay.head_perm(t)) for t in range(1, min(2, heads))]
+        return [slabs[0]] + close + away
 
     def scatter(payloads):
         moved = [send(payloads[r], lay.scatter_perm(r)) for r in range(1, plane)]
@@ -609,13 +637,16 @@
         before = run(lay, fn(update_near_fn, lay), (weights, *kv[:near]), deps=(places,))
         rest = run(lay, fn(update_rest_fn, lay), (weights, *before, *kv[near:]))
         sums = exchange(*rest)
-        qg = tie(lay, qg, (sums[0],))
-        qg = qg + over_cores(qg)
+        close, away = qg[:2], tie(lay, qg[2:], (sums[0],))
+        close, away = close + over_cores(close), away + over_cores(away)
         renewed, grad, moved, total = run(
             lay, fn(renorm_all_fn, lay, coefficient), (*sums, weights)
         )
-        applied = run(lay, fn(apply_fn, lay), (renewed, *qg))
-        query_home = total_rows(applied[2:])
+        before, *query_close = run(lay, fn(apply_near_fn, lay, 2), (renewed, *close))
+        applied = run(lay, fn(apply_far_fn, lay, heads - 2), (renewed, before, *away))
+        query_home = add_home(query_close[:-1], query_close[-1]) + add_home(
+            applied[2:-1], applied[-1]
+        )
         sums = exchange(*applied[:2])
         move, d_total, direct = run(
             lay,
@@ -623,14 +654,17 @@
             (*sums, weights, grad, moved, total, places),
         )
         query_home = back_home(query_home)
-        if lay.cores > 1:
-            other, before = run(lay, fn(pull_other_fn, lay), (move, d_total, weights, *kv[heads:]))
-        else:
-            other, before = None, jnp.zeros_like(weights)
+        other, before = run(lay, fn(pull_other_fn, lay), (move, d_total, weights, *kv[heads + 2 :]))
+        before, *key_far = run(
+            lay, fn(pull_own_fn, lay), (move, d_total, weights, before, *kv[2:heads])
+        )
+        key_far = add_home(key_far, other)
         pulled = run(
-            lay, fn(pull_own_fn, lay), (move, d_total, weights, before, places, *kv[:heads])
-        )
-        pulled = [*pulled, other]
+            lay,
+            fn(pull_last_fn, lay, 2),
+            (move, d_total, weights, before, places, *kv[:2], *kv[heads : heads + 2]),
+        )
+        key_home = add_home(pulled[plane : plane + 2], pulled[-1]) + key_far
     else:
         own = jnp.concatenate([t[:slot] for t in turned], 0)
         sums = scatter(run(lay, fn(update_fn, lay), (weights, *kv)))
@@ -643,7 +677,7 @@
             lay, fn(renorm_back_fn, lay, coefficient), (*sums, payload, own, grad, moved)
         )
         pulled = run(lay, fn(pull_fn, lay), (*gather(d_payload), *kv, weights))
-    key_home = total_rows(pulled[plane:])
+        key_home = total_rows(pulled[plane:])
     sums = scatter(pulled[:plane])
     pieces = run(lay, fn(total_fn, lay, scale), (*sums, direct, places), deps=tuple(key_home))
     key_home = back_home(key_home)

time: 134 us -> 129 us (0.963)
  starting transfers between devices: 47.9 us -> 44.4 us
  waiting for transfers between devices: 65.1 us -> 62.4 us
    ppermute x36 -> x38, starting transfers between devices: 47.9 us -> 44.4 us  [send(): return lax.ppermute(x, AXES, perm)]
    ppermute x36 -> x38, waiting for transfers between devices: 65.1 us -> 62.4 us  [send(): return lax.ppermute(x, AXES, perm)]
    pallas_call x17 -> x21, Pallas kernels: 13 us -> 14 us  [run(): pl.pallas_call(kernel, out_shape=[jax.ShapeDtypeStruct(s.shape, s.dtype)...]
  transfers between devices with their start and end apart: 36 -> 38, of which waited for: 16 -> 13; matrix products, arithmetic and copies ran while one was open for 2% -> 2% of each run, Pallas kernels for 4% -> 3%
where the time goes in v2:
time: 129 us; the launch traced here: 127 us
  waiting for transfers between devices  62.4 us (48%)
  starting transfers between devices  44.4 us (34%)
  Pallas kernels  14 us (11%)
  local copies, waits for them, and re-layouts  4.95 us (4%)
    ppermute x38, waiting for transfers between devices, send(): return lax.ppermute(x, AXES, perm)  62.4 us
    ppermute x38, starting transfers between devices, send(): return lax.ppermute(x, AXES, perm)  44.4 us
    pallas_call x21, Pallas kernels, run(): pl.pallas_call(kernel, out_shape=[jax.ShapeDtypeStruct(s.shape, s.dtype)...  14 us
    unnamed x13, local copies, waits for them, and re-layouts  2.88 us
  transfers between devices with their start and end apart: 38, of which 13 were waited for; matrix products, arithmetic and copies ran while one was open for 2% of the time, Pallas kernels for 3%

profile of v2, /device:TPU:0, one launch (start us, length us, event | category | flops | bytes accessed | tf_op | source)
XLA Modules:
  0.0 126.8 jit_solution(2335517701542071512)
XLA Ops:
  0.7 0.9 copy-done
  1.6 0.9 copy-done.1
  2.5 0.7 copy-done.4
  3.4 3.1 %collective-permute-start = (f32[392,128]{1,0:T(8,128)S(1)}, f32[392,128]{1,0:T(8,128)S(1)}, u32[]{:S(2)}, u32[]{:S(2)}) collective-permute-start(f32[392,128]{1,0:T(8,128)S(1)} %get-tuple-element.68), channel_id=1, source_target_pairs={{0,2},{1,3},{2,0},{3,1},{4,6},{5,7},{6,4},{7,5},{8,10},{9,11},{10,... | collective-permute-start | bytes 602120 | tf_op jit(solution)/shard_map/ppermute | solution.py:566
  6.5 2.6 %collective-permute-start.1 = (f32[392,128]{1,0:T(8,128)S(1)}, f32[392,128]{1,0:T(8,128)S(1)}, u32[]{:S(2)}, u32[]{:S(2)}) collective-permute-start(f32[392,128]{1,0:T(8,128)S(1)} %get-tuple-element.71), channel_id=1, source_target_pairs={{0,4},{1,5},{2,6},{3,7},{4,0},{5,1},{6,2},{7,3},{8,12},{9,13},{10,... | collective-permute-start | bytes 602120 | tf_op jit(solution)/shard_map/ppermute | solution.py:566
  9.1 1.4 %constant_dynamic-slice_fusion.3 = (f32[192,192]{1,0:T(8,128)S(1)}, f32[192,192]{1,0:T(8,128)S(1)}, f32[192,192]{1,0:T(8,128)S(1)}) fusion(f32[192,4608]{1,0:T(8,128)} %param.11, s32[]{:T(128)S(6)} %select_n.18, s32[]{:T(128)S(6)} %select_n.19, s32[]{:T(128)S(6)} %select_n.20), kind=kLoop, calls=%fused_computation.4 | loop fusion | bytes 884748 | tf_op jit(solution)/shard_map/dynamic_slice | solution.py:616
  10.9 4.2 %collective-permute-done.refs_2_.refs_6_ = f32[392,128]{1,0:T(8,128)S(1)} collective-permute-done((f32[392,128]{1,0:T(8,128)S(1)}, f32[392,128]{1,0:T(8,128)S(1)}, u32[]{:S(2)}, u32[]{:S(2)}) %collective-permute-start) | collective-permute-done | bytes 200736 | tf_op jit(solution)/shard_map/ppermute | solution.py:566
  15.1 8.8 %collective-permute-done.1.refs_3_.refs_4_ = f32[392,128]{1,0:T(8,128)S(1)} collective-permute-done((f32[392,128]{1,0:T(8,128)S(1)}, f32[392,128]{1,0:T(8,128)S(1)}, u32[]{:S(2)}, u32[]{:S(2)}) %collective-permute-start.1) | collective-permute-done | bytes 200736 | tf_op jit(solution)/shard_map/ppermute | solution.py:566
  24.4 0.7 constant_dynamic-slice_fusion.refs_3_.refs_8_.refs_4_.refs_5_
  25.2 0.7 shard_map.111
  25.9 1.2 shard_map.112
  27.1 1.6 %collective-permute-start.7 = (f32[512,128]{1,0:T(8,128)S(1)}, f32[512,128]{1,0:T(8,128)S(1)}, u32[]{:S(2)}, u32[]{:S(2)}) collective-permute-start(f32[512,128]{1,0:T(8,128)S(1)} %get-tuple-element.73.refs_0_), channel_id=1, source_target_pairs={{0,1},{1,0},{2,3},{3,2},{4,5},{5,4},{6,7},{7,6},{8,9},{9,8},{10,11... | collective-permute-start | bytes 786440 | tf_op jit(solution)/shard_map/ppermute | solution.py:566
  28.7 1.5 %collective-permute-start.8 = (f32[368,128]{1,0:T(8,128)S(1)}, f32[368,128]{1,0:T(8,128)S(1)}, u32[]{:S(2)}, u32[]{:S(2)}) collective-permute-start(f32[368,128]{1,0:T(8,128)S(1)} %get-tuple-element.74.refs_2_), channel_id=1, source_target_pairs={{0,16},{1,17},{2,18},{3,19},{4,20},{5,21},{6,22},{7,23},{8,24},{9,... | collective-permute-start | bytes 565256 | tf_op jit(solution)/shard_map/ppermute | solution.py:566
  30.4 3.1 %collective-permute-start.11 = (f32[384,128]{1,0:T(8,128)S(1)}, f32[384,128]{1,0:T(8,128)S(1)}, u32[]{:S(2)}, u32[]{:S(2)}) collective-permute-start(f32[384,128]{1,0:T(8,128)S(1)} %get-tuple-element.79), channel_id=1, source_target_pairs={{0,2},{1,3},{2,0},{3,1},{4,6},{5,7},{6,4},{7,5},{8,10},{9,11},{10,... | collective-permute-start | bytes 589832 | tf_op jit(solution)/shard_map/ppermute | solution.py:566
  33.4 1.1 collective-permute-start.16
  34.5 1.4 %collective-permute-start.17 = (f32[384,128]{1,0:T(8,128)S(1)}, f32[384,128]{1,0:T(8,128)S(1)}, u32[]{:S(2)}, u32[]{:S(2)}) collective-permute-start(f32[384,128]{1,0:T(8,128)S(1)} %get-tuple-element.89), channel_id=1, source_target_pairs={{0,6},{1,7},{2,4},{3,5},{4,2},{5,3},{6,0},{7,1},{8,14},{9,15},{10,... | collective-permute-start | bytes 589832 | tf_op jit(solution)/shard_map/ppermute | solution.py:566
  36.0 1.0 collective-permute-start.10
  37.0 1.5 %collective-permute-start.9 = (f32[512,128]{1,0:T(8,128)S(1)}, f32[512,128]{1,0:T(8,128)S(1)}, u32[]{:S(2)}, u32[]{:S(2)}) collective-permute-start(f32[512,128]{1,0:T(8,128)S(1)} %get-tuple-element.75.refs_0_), channel_id=1, source_target_pairs={{0,16},{1,17},{2,18},{3,19},{4,20},{5,21},{6,22},{7,23},{8,24},{9,... | collective-permute-start | bytes 786440 | tf_op jit(solution)/shard_map/ppermute | solution.py:566
  38.5 3.5 %collective-permute-done.11.refs_2_ = f32[384,128]{1,0:T(8,128)S(1)} collective-permute-done((f32[384,128]{1,0:T(8,128)S(1)}, f32[384,128]{1,0:T(8,128)S(1)}, u32[]{:S(2)}, u32[]{:S(2)}) %collective-permute-start.11) | collective-permute-done | bytes 196640 | tf_op jit(solution)/shard_map/ppermute | solution.py:566
  42.0 8.6 %collective-permute-done.16.refs_0_ = f32[384,128]{1,0:T(8,128)S(1)} collective-permute-done((f32[384,128]{1,0:T(8,128)S(1)}, f32[384,128]{1,0:T(8,128)S(1)}, u32[]{:S(2)}, u32[]{:S(2)}) %collective-permute-start.16) | collective-permute-done | bytes 196640 | tf_op jit(solution)/shard_map/ppermute | solution.py:566
  52.0 1.2 shard_map.116
  53.2 1.2 shard_map.120
  54.4 0.6 collective-permute-start.23
  55.5 5.9 %collective-permute-done.24.refs_3_ = f32[368,128]{1,0:T(8,128)S(1)} collective-permute-done((f32[368,128]{1,0:T(8,128)S(1)}, f32[368,128]{1,0:T(8,128)S(1)}, u32[]{:S(2)}, u32[]{:S(2)}) %collective-permute-start.24) | collective-permute-done | bytes 188448 | tf_op jit(solution)/shard_map/ppermute | solution.py:566
  61.5 1.4 %collective-permute-done.23.refs_1_ = f32[512,128]{1,0:T(8,128)S(1)} collective-permute-done((f32[512,128]{1,0:T(8,128)S(1)}, f32[512,128]{1,0:T(8,128)S(1)}, u32[]{:S(2)}, u32[]{:S(2)}) %collective-permute-start.23) | collective-permute-done | bytes 262176 | tf_op jit(solution)/shard_map/ppermute | solution.py:566
  62.9 0.6 collective-permute-start.25
  64.0 5.1 %collective-permute-done.26.refs_3_ = f32[368,128]{1,0:T(8,128)S(1)} collective-permute-done((f32[368,128]{1,0:T(8,128)S(1)}, f32[368,128]{1,0:T(8,128)S(1)}, u32[]{:S(2)}, u32[]{:S(2)}) %collective-permute-start.26) | collective-permute-done | bytes 188448 | tf_op jit(solution)/shard_map/ppermute | solution.py:566
  69.1 1.3 %collective-permute-done.25.refs_1_ = f32[512,128]{1,0:T(8,128)S(1)} collective-permute-done((f32[512,128]{1,0:T(8,128)S(1)}, f32[512,128]{1,0:T(8,128)S(1)}, u32[]{:S(2)}, u32[]{:S(2)}) %collective-permute-start.25) | collective-permute-done | bytes 262176 | tf_op jit(solution)/shard_map/ppermute | solution.py:566
  70.5 0.8 shard_map.123
  71.3 1.4 %shard_map.124 = (f32[2,392,128]{2,1,0:T(8,128)S(1)}, f32[576,192]{1,0:T(8,128)S(1)}) custom-call(f32[576,192]{1,0:T(8,128)S(1)} %get-tuple-element.104.refs_0_, f32[8,128]{1,0:T(8,128)S(1)} %get-tuple-element.105.refs_1_, f32[576,192]{1,0:T(8,128)S(1)} %pad_maximum_fusion.refs_0_.refs_4_.refs_2_, f32[392,128]{1,0:T(8,128)S(1)} %collective-permute-done.5.refs_7_.refs_3_, ...), custom_call_target="tpu_custom_call" | custom-call | tf_op jit(solution)/shard_map/pallas_call | solution.py:528
  72.7 1.4 %shard_map.125 = (f32[576,192]{1,0:T(8,128)S(1)}, f32[392,128]{1,0:T(8,128)S(1)}, f32[392,128]{1,0:T(8,128)S(1)}) custom-call(f32[576,192]{1,0:T(8,128)S(1)} %get-tuple-element.104.refs_0_, f32[8,128]{1,0:T(8,128)S(1)} %get-tuple-element.105.refs_1_, f32[576,192]{1,0:T(8,128)S(1)} %pad_maximum_fusion.refs_0_.refs_4_.refs_2_, ...), custom_call_target="tpu_custom_call" | custom-call | tf_op jit(solution)/shard_map/pallas_call | solution.py:528
  74.2 2.3 %shard_map.126 = (f32[224,128]{1,0:T(8,128)S(1)}, f32[224,128]{1,0:T(8,128)S(1)}, f32[224,128]{1,0:T(8,128)S(1)}, f32[224,128]{1,0:T(8,128)S(1)}, f32[392,128]{1...) custom-call(f32[576,192]{1,0:T(8,128)S(1)} %get-tuple-element.104.refs_0_, ...), custom_call_target="tpu_custom_call" | custom-call | tf_op jit(solution)/shard_map/pallas_call | solution.py:528
  78.1 1.1 collective-permute-done.14.refs_2_
  79.2 3.0 %collective-permute-start.15 = (f32[192,128]{1,0:T(8,128)S(1)}, f32[192,128]{1,0:T(8,128)S(1)}, u32[]{:S(2)}, u32[]{:S(2)}) collective-permute-start(f32[192,128]{1,0:T(8,128)S(1)} %get-tuple-element.84), channel_id=1, source_target_pairs={{0,2},{1,3},{2,0},{3,1},{4,6},{5,7},{6,4},{7,5},{8,10},{9,11},{10,... | collective-permute-start | bytes 294920 | tf_op jit(solution)/shard_map/ppermute | solution.py:566
  82.1 0.6 collective-permute-start.33
  82.7 1.4 %collective-permute-start.34 = (f32[224,128]{1,0:T(8,128)S(1)}, f32[224,128]{1,0:T(8,128)S(1)}, u32[]{:S(2)}, u32[]{:S(2)}) collective-permute-start(f32[224,128]{1,0:T(8,128)S(1)} %get-tuple-element.124), channel_id=1, source_target_pairs={{0,17},{1,16},{2,19},{3,18},{4,21},{5,20},{6,23},{7,22},{8,25},{9,... | collective-permute-start | bytes 344072 | tf_op jit(solution)/shard_map/ppermute | solution.py:566
  84.4 0.8 collective-permute-done.15.refs_1_
  85.2 3.2 %collective-permute-start.30 = (f32[392,128]{1,0:T(8,128)S(1)}, f32[392,128]{1,0:T(8,128)S(1)}, u32[]{:S(2)}, u32[]{:S(2)}) collective-permute-start(f32[392,128]{1,0:T(8,128)S(1)} %get-tuple-element.117), channel_id=1, source_target_pairs={{0,4},{1,5},{2,6},{3,7},{4,0},{5,1},{6,2},{7,3},{8,12},{9,13},{10,... | collective-permute-start | bytes 602120 | tf_op jit(solution)/shard_map/ppermute | solution.py:566
  88.4 1.3 %collective-permute-start.31 = (f32[392,128]{1,0:T(8,128)S(1)}, f32[392,128]{1,0:T(8,128)S(1)}, u32[]{:S(2)}, u32[]{:S(2)}) collective-permute-start(f32[392,128]{1,0:T(8,128)S(1)} %get-tuple-element.118), channel_id=1, source_target_pairs={{0,6},{1,7},{2,4},{3,5},{4,2},{5,3},{6,0},{7,1},{8,14},{9,15},{10,... | collective-permute-start | bytes 602120 | tf_op jit(solution)/shard_map/ppermute | solution.py:566
  89.9 2.6 %collective-permute-start.22 = (f32[192,128]{1,0:T(8,128)S(1)}, f32[192,128]{1,0:T(8,128)S(1)}, u32[]{:S(2)}, u32[]{:S(2)}) collective-permute-start(f32[192,128]{1,0:T(8,128)S(1)} %get-tuple-element.96), channel_id=1, source_target_pairs={{0,6},{1,7},{2,4},{3,5},{4,2},{5,3},{6,0},{7,1},{8,14},{9,15},{10,... | collective-permute-start | bytes 294920 | tf_op jit(solution)/shard_map/ppermute | solution.py:566
  92.6 20.3 %collective-permute-done.21.refs_2_ = f32[192,128]{1,0:T(8,128)S(1)} collective-permute-done((f32[192,128]{1,0:T(8,128)S(1)}, f32[192,128]{1,0:T(8,128)S(1)}, u32[]{:S(2)}, u32[]{:S(2)}) %collective-permute-start.21) | collective-permute-done | bytes 98336 | tf_op jit(solution)/shard_map/ppermute | solution.py:566
  112.9 0.7 collective-permute-start.35
  113.6 1.1 collective-permute-start.36
  114.7 8.7 %collective-permute-start.37 = (f32[48,192]{1,0:T(8,128)S(1)}, f32[48,192]{1,0:T(8,128)S(1)}, u32[]{:S(2)}, u32[]{:S(2)}) collective-permute-start(f32[48,192]{1,0:T(8,128)S(1)} %get-tuple-element.128), channel_id=1, source_target_pairs={{0,21},{1,11},{2,2},{3,24},{4,16},{5,5},{6,8},{7,29},{8,12},{9,1},... | collective-permute-start | bytes 110600 | tf_op jit(solution)/shard_map/ppermute | solution.py:566
  123.4 0.8 shard_map.127
  124.2 0.9 collective-permute-done.37.refs_2_
  125.1 0.7 shard_map.132
  125.9 0.9 shard_map.130
  (77 shorter events, 6.0 us)
Async XLA Ops:
  0.7 0.9 copy-start
  1.6 0.9 copy-start.1
  2.5 0.7 copy-start.4
  3.4 26.8 %copy-start.2 = (bf16[128,768]{1,0:T(8,128)(2,1)S(1)}, bf16[128,768]{1,0:T(8,128)(2,1)}, u32[]{:S(2)}) copy-start(bf16[128,768]{1,0:T(8,128)(2,1)} %refs_0_.3) | copy-start | bytes 589828
  3.4 26.7 %copy-start.3 = (bf16[128,768]{1,0:T(8,128)(2,1)S(1)}, bf16[128,768]{1,0:T(8,128)(2,1)}, u32[]{:S(2)}) copy-start(bf16[128,768]{1,0:T(8,128)(2,1)} %refs_1_.3) | copy-start | bytes 589828
  3.4 11.7 %collective-permute-start = (f32[392,128]{1,0:T(8,128)S(1)}, f32[392,128]{1,0:T(8,128)S(1)}, u32[]{:S(2)}, u32[]{:S(2)}) collective-permute-start(f32[392,128]{1,0:T(8,128)S(1)} %get-tuple-element.68), channel_id=1, source_target_pairs={{0,2},{1,3},{2,0},{3,1},{4,6},{5,7},{6,4},{7,5},{8,10},{9,11},{10,... | collective-permute-start | bytes 602120 | tf_op jit(solution)/shard_map/ppermute | solution.py:566
  6.5 17.4 %collective-permute-start.1 = (f32[392,128]{1,0:T(8,128)S(1)}, f32[392,128]{1,0:T(8,128)S(1)}, u32[]{:S(2)}, u32[]{:S(2)}) collective-permute-start(f32[392,128]{1,0:T(8,128)S(1)} %get-tuple-element.71), channel_id=1, source_target_pairs={{0,4},{1,5},{2,6},{3,7},{4,0},{5,1},{6,2},{7,3},{8,12},{9,13},{10,... | collective-permute-start | bytes 602120 | tf_op jit(solution)/shard_map/ppermute | solution.py:566
  9.1 14.8 %collective-permute-start.2 = (f32[392,128]{1,0:T(8,128)S(1)}, f32[392,128]{1,0:T(8,128)S(1)}, u32[]{:S(2)}, u32[]{:S(2)}) collective-permute-start(f32[392,128]{1,0:T(8,128)S(1)} %get-tuple-element.72), channel_id=1, source_target_pairs={{0,6},{1,7},{2,4},{3,5},{4,2},{5,3},{6,0},{7,1},{8,14},{9,15},{10,... | collective-permute-start | bytes 602120 | tf_op jit(solution)/shard_map/ppermute | solution.py:566
  9.1 16.7 %collective-permute-start.3 = (f32[392,128]{1,0:T(8,128)S(1)}, f32[392,128]{1,0:T(8,128)S(1)}, u32[]{:S(2)}, u32[]{:S(2)}) collective-permute-start(f32[392,128]{1,0:T(8,128)S(1)} %get-tuple-element.67.refs_1_.refs_5_), channel_id=1, source_target_pairs={{0,8},{1,9},{2,10},{3,11},{4,12},{5,13},{6,14},{7,15},{8,0},{9,1},... | collective-permute-start | bytes 602120 | tf_op jit(solution)/shard_map/ppermute | solution.py:566
  15.1 10.8 %collective-permute-start.4 = (f32[392,128]{1,0:T(8,128)S(1)}, f32[392,128]{1,0:T(8,128)S(1)}, u32[]{:S(2)}, u32[]{:S(2)}) collective-permute-start(f32[392,128]{1,0:T(8,128)S(1)} %collective-permute-done.refs_2_.refs_6_), channel_id=1, source_target_pairs={{0,8},{1,9},{2,10},{3,11},{4,12},{5,13},{6,14},{7,15},{8,0},{9,1},... | collective-permute-start | bytes 602120 | tf_op jit(solution)/shard_map/ppermute | solution.py:566
  23.9 2.0 %collective-permute-start.5 = (f32[392,128]{1,0:T(8,128)S(1)}, f32[392,128]{1,0:T(8,128)S(1)}, u32[]{:S(2)}, u32[]{:S(2)}) collective-permute-start(f32[392,128]{1,0:T(8,128)S(1)} %collective-permute-done.1.refs_3_.refs_4_), channel_id=1, source_target_pairs={{0,8},{1,9},{2,10},{3,11},{4,12},{5,13},{6,14},{7,15},{8,0},{9,1},... | collective-permute-start | bytes 602120 | tf_op jit(solution)/shard_map/ppermute | solution.py:566
  23.9 2.0 %collective-permute-start.6 = (f32[392,128]{1,0:T(8,128)S(1)}, f32[392,128]{1,0:T(8,128)S(1)}, u32[]{:S(2)}, u32[]{:S(2)}) collective-permute-start(f32[392,128]{1,0:T(8,128)S(1)} %collective-permute-done.2.refs_4_.refs_5_), channel_id=1, source_target_pairs={{0,8},{1,9},{2,10},{3,11},{4,12},{5,13},{6,14},{7,15},{8,0},{9,1},... | collective-permute-start | bytes 602120 | tf_op jit(solution)/shard_map/ppermute | solution.py:566
  27.1 8.9 %collective-permute-start.7 = (f32[512,128]{1,0:T(8,128)S(1)}, f32[512,128]{1,0:T(8,128)S(1)}, u32[]{:S(2)}, u32[]{:S(2)}) collective-permute-start(f32[512,128]{1,0:T(8,128)S(1)} %get-tuple-element.73.refs_0_), channel_id=1, source_target_pairs={{0,1},{1,0},{2,3},{3,2},{4,5},{5,4},{6,7},{7,6},{8,9},{9,8},{10,11... | collective-permute-start | bytes 786440 | tf_op jit(solution)/shard_map/ppermute | solution.py:566
  28.7 7.3 %collective-permute-start.8 = (f32[368,128]{1,0:T(8,128)S(1)}, f32[368,128]{1,0:T(8,128)S(1)}, u32[]{:S(2)}, u32[]{:S(2)}) collective-permute-start(f32[368,128]{1,0:T(8,128)S(1)} %get-tuple-element.74.refs_2_), channel_id=1, source_target_pairs={{0,16},{1,17},{2,18},{3,19},{4,20},{5,21},{6,22},{7,23},{8,24},{9,... | collective-permute-start | bytes 565256 | tf_op jit(solution)/shard_map/ppermute | solution.py:566
  30.4 11.6 %collective-permute-start.11 = (f32[384,128]{1,0:T(8,128)S(1)}, f32[384,128]{1,0:T(8,128)S(1)}, u32[]{:S(2)}, u32[]{:S(2)}) collective-permute-start(f32[384,128]{1,0:T(8,128)S(1)} %get-tuple-element.79), channel_id=1, source_target_pairs={{0,2},{1,3},{2,0},{3,1},{4,6},{5,7},{6,4},{7,5},{8,10},{9,11},{10,... | collective-permute-start | bytes 589832 | tf_op jit(solution)/shard_map/ppermute | solution.py:566
  33.4 17.1 %collective-permute-start.16 = (f32[384,128]{1,0:T(8,128)S(1)}, f32[384,128]{1,0:T(8,128)S(1)}, u32[]{:S(2)}, u32[]{:S(2)}) collective-permute-start(f32[384,128]{1,0:T(8,128)S(1)} %get-tuple-element.88), channel_id=1, source_target_pairs={{0,4},{1,5},{2,6},{3,7},{4,0},{5,1},{6,2},{7,3},{8,12},{9,13},{10,... | collective-permute-start | bytes 589832 | tf_op jit(solution)/shard_map/ppermute | solution.py:566
  34.5 16.0 %collective-permute-start.17 = (f32[384,128]{1,0:T(8,128)S(1)}, f32[384,128]{1,0:T(8,128)S(1)}, u32[]{:S(2)}, u32[]{:S(2)}) collective-permute-start(f32[384,128]{1,0:T(8,128)S(1)} %get-tuple-element.89), channel_id=1, source_target_pairs={{0,6},{1,7},{2,4},{3,5},{4,2},{5,3},{6,0},{7,1},{8,14},{9,15},{10,... | collective-permute-start | bytes 589832 | tf_op jit(solution)/shard_map/ppermute | solution.py:566
  36.0 15.0 %collective-permute-start.10 = (f32[368,128]{1,0:T(8,128)S(1)}, f32[368,128]{1,0:T(8,128)S(1)}, u32[]{:S(2)}, u32[]{:S(2)}) collective-permute-start(f32[368,128]{1,0:T(8,128)S(1)} %get-tuple-element.76.refs_2_), channel_id=1, source_target_pairs={{0,1},{1,0},{2,3},{3,2},{4,5},{5,4},{6,7},{7,6},{8,9},{9,8},{10,11... | collective-permute-start | bytes 565256 | tf_op jit(solution)/shard_map/ppermute | solution.py:566
  37.0 14.1 %collective-permute-start.9 = (f32[512,128]{1,0:T(8,128)S(1)}, f32[512,128]{1,0:T(8,128)S(1)}, u32[]{:S(2)}, u32[]{:S(2)}) collective-permute-start(f32[512,128]{1,0:T(8,128)S(1)} %get-tuple-element.75.refs_0_), channel_id=1, source_target_pairs={{0,16},{1,17},{2,18},{3,19},{4,20},{5,21},{6,22},{7,23},{8,24},{9,... | collective-permute-start | bytes 786440 | tf_op jit(solution)/shard_map/ppermute | solution.py:566
  42.0 9.6 %collective-permute-start.12 = (f32[384,128]{1,0:T(8,128)S(1)}, f32[384,128]{1,0:T(8,128)S(1)}, u32[]{:S(2)}, u32[]{:S(2)}) collective-permute-start(f32[384,128]{1,0:T(8,128)S(1)} %get-tuple-element.78.refs_1_), channel_id=1, source_target_pairs={{0,8},{1,9},{2,10},{3,11},{4,12},{5,13},{6,14},{7,15},{8,0},{9,1},... | collective-permute-start | bytes 589832 | tf_op jit(solution)/shard_map/ppermute | solution.py:566
  50.5 1.4 %collective-permute-start.13 = (f32[384,128]{1,0:T(8,128)S(1)}, f32[384,128]{1,0:T(8,128)S(1)}, u32[]{:S(2)}, u32[]{:S(2)}) collective-permute-start(f32[384,128]{1,0:T(8,128)S(1)} %collective-permute-done.11.refs_2_), channel_id=1, source_target_pairs={{0,8},{1,9},{2,10},{3,11},{4,12},{5,13},{6,14},{7,15},{8,0},{9,1},... | collective-permute-start | bytes 589832 | tf_op jit(solution)/shard_map/ppermute | solution.py:566
  50.5 2.7 %collective-permute-start.18 = (f32[384,128]{1,0:T(8,128)S(1)}, f32[384,128]{1,0:T(8,128)S(1)}, u32[]{:S(2)}, u32[]{:S(2)}) collective-permute-start(f32[384,128]{1,0:T(8,128)S(1)} %get-tuple-element.90.refs_2_), channel_id=1, source_target_pairs={{0,8},{1,9},{2,10},{3,11},{4,12},{5,13},{6,14},{7,15},{8,0},{9,1},... | collective-permute-start | bytes 589832 | tf_op jit(solution)/shard_map/ppermute | solution.py:566
  51.1 2.2 %collective-permute-start.19 = (f32[384,128]{1,0:T(8,128)S(1)}, f32[384,128]{1,0:T(8,128)S(1)}, u32[]{:S(2)}, u32[]{:S(2)}) collective-permute-start(f32[384,128]{1,0:T(8,128)S(1)} %get-tuple-element.91.refs_3_), channel_id=1, source_target_pairs={{0,8},{1,9},{2,10},{3,11},{4,12},{5,13},{6,14},{7,15},{8,0},{9,1},... | collective-permute-start | bytes 589832 | tf_op jit(solution)/shard_map/ppermute | solution.py:566
  54.4 8.4 %collective-permute-start.23 = (f32[512,128]{1,0:T(8,128)S(1)}, f32[512,128]{1,0:T(8,128)S(1)}, u32[]{:S(2)}, u32[]{:S(2)}) collective-permute-start(f32[512,128]{1,0:T(8,128)S(1)} %get-tuple-element.97.refs_0_), channel_id=1, source_target_pairs={{0,1},{1,0},{2,3},{3,2},{4,5},{5,4},{6,7},{7,6},{8,9},{9,8},{10,11... | collective-permute-start | bytes 786440 | tf_op jit(solution)/shard_map/ppermute | solution.py:566
  55.0 6.5 %collective-permute-start.24 = (f32[368,128]{1,0:T(8,128)S(1)}, f32[368,128]{1,0:T(8,128)S(1)}, u32[]{:S(2)}, u32[]{:S(2)}) collective-permute-start(f32[368,128]{1,0:T(8,128)S(1)} %get-tuple-element.98.refs_2_), channel_id=1, source_target_pairs={{0,16},{1,17},{2,18},{3,19},{4,20},{5,21},{6,22},{7,23},{8,24},{9,... | collective-permute-start | bytes 565256 | tf_op jit(solution)/shard_map/ppermute | solution.py:566
  62.9 7.5 %collective-permute-start.25 = (f32[512,128]{1,0:T(8,128)S(1)}, f32[512,128]{1,0:T(8,128)S(1)}, u32[]{:S(2)}, u32[]{:S(2)}) collective-permute-start(f32[512,128]{1,0:T(8,128)S(1)} %get-tuple-element.99.refs_0_), channel_id=1, source_target_pairs={{0,16},{1,17},{2,18},{3,19},{4,20},{5,21},{6,22},{7,23},{8,24},{9,... | collective-permute-start | bytes 786440 | tf_op jit(solution)/shard_map/ppermute | solution.py:566
  63.5 5.6 %collective-permute-start.26 = (f32[368,128]{1,0:T(8,128)S(1)}, f32[368,128]{1,0:T(8,128)S(1)}, u32[]{:S(2)}, u32[]{:S(2)}) collective-permute-start(f32[368,128]{1,0:T(8,128)S(1)} %get-tuple-element.100.refs_2_), channel_id=1, source_target_pairs={{0,1},{1,0},{2,3},{3,2},{4,5},{5,4},{6,7},{7,6},{8,9},{9,8},{10,11... | collective-permute-start | bytes 565256 | tf_op jit(solution)/shard_map/ppermute | solution.py:566
  76.5 5.6 %collective-permute-start.27 = (f32[2,392,128]{2,1,0:T(8,128)S(1)}, f32[2,392,128]{2,1,0:T(8,128)S(1)}, u32[]{:S(2)}, u32[]{:S(2)}) collective-permute-start(f32[2,392,128]{2,1,0:T(8,128)S(1)} %get-tuple-element.111), channel_id=1, source_target_pairs={{0,8},{1,9},{2,10},{3,11},{4,12},{5,13},{6,14},{7,15},{8,0},{9,1},... | collective-permute-start | bytes 1204232 | tf_op jit(solution)/shard_map/ppermute | solution.py:566
  76.6 6.1 %collective-permute-start.29 = (f32[2,392,128]{2,1,0:T(8,128)S(1)}, f32[2,392,128]{2,1,0:T(8,128)S(1)}, u32[]{:S(2)}, u32[]{:S(2)}) collective-permute-start(f32[2,392,128]{2,1,0:T(8,128)S(1)} %get-tuple-element.116), channel_id=1, source_target_pairs={{0,8},{1,9},{2,10},{3,11},{4,12},{5,13},{6,14},{7,15},{8,0},{9,1},... | collective-permute-start | bytes 1204232 | tf_op jit(solution)/shard_map/ppermute | solution.py:566
  77.1 2.1 %collective-permute-start.14 = (f32[2,192,128]{2,1,0:T(8,128)S(1)}, f32[2,192,128]{2,1,0:T(8,128)S(1)}, u32[]{:S(2)}, u32[]{:S(2)}) collective-permute-start(f32[2,192,128]{2,1,0:T(8,128)S(1)} %get-tuple-element.82), channel_id=1, source_target_pairs={{0,8},{1,9},{2,10},{3,11},{4,12},{5,13},{6,14},{7,15},{8,0},{9,1},... | collective-permute-start | bytes 589832 | tf_op jit(solution)/shard_map/ppermute | solution.py:566
  77.1 7.1 %collective-permute-start.20 = (f32[2,192,128]{2,1,0:T(8,128)S(1)}, f32[2,192,128]{2,1,0:T(8,128)S(1)}, u32[]{:S(2)}, u32[]{:S(2)}) collective-permute-start(f32[2,192,128]{2,1,0:T(8,128)S(1)} %get-tuple-element.94), channel_id=1, source_target_pairs={{0,8},{1,9},{2,10},{3,11},{4,12},{5,13},{6,14},{7,15},{8,0},{9,1},... | collective-permute-start | bytes 589832 | tf_op jit(solution)/shard_map/ppermute | solution.py:566
  77.6 10.8 %collective-permute-start.32 = (f32[224,128]{1,0:T(8,128)S(1)}, f32[224,128]{1,0:T(8,128)S(1)}, u32[]{:S(2)}, u32[]{:S(2)}) collective-permute-start(f32[224,128]{1,0:T(8,128)S(1)} %get-tuple-element.122), channel_id=1, source_target_pairs={{0,1},{1,0},{2,3},{3,2},{4,5},{5,4},{6,7},{7,6},{8,9},{9,8},{10,11... | collective-permute-start | bytes 344072 | tf_op jit(solution)/shard_map/ppermute | solution.py:566
  79.2 6.1 %collective-permute-start.15 = (f32[192,128]{1,0:T(8,128)S(1)}, f32[192,128]{1,0:T(8,128)S(1)}, u32[]{:S(2)}, u32[]{:S(2)}) collective-permute-start(f32[192,128]{1,0:T(8,128)S(1)} %get-tuple-element.84), channel_id=1, source_target_pairs={{0,2},{1,3},{2,0},{3,1},{4,6},{5,7},{6,4},{7,5},{8,10},{9,11},{10,... | collective-permute-start | bytes 294920 | tf_op jit(solution)/shard_map/ppermute | solution.py:566
  82.1 7.6 %collective-permute-start.33 = (f32[224,128]{1,0:T(8,128)S(1)}, f32[224,128]{1,0:T(8,128)S(1)}, u32[]{:S(2)}, u32[]{:S(2)}) collective-permute-start(f32[224,128]{1,0:T(8,128)S(1)} %get-tuple-element.123), channel_id=1, source_target_pairs={{0,16},{1,17},{2,18},{3,19},{4,20},{5,21},{6,22},{7,23},{8,24},{9,... | collective-permute-start | bytes 344072 | tf_op jit(solution)/shard_map/ppermute | solution.py:566
  82.7 7.2 %collective-permute-start.34 = (f32[224,128]{1,0:T(8,128)S(1)}, f32[224,128]{1,0:T(8,128)S(1)}, u32[]{:S(2)}, u32[]{:S(2)}) collective-permute-start(f32[224,128]{1,0:T(8,128)S(1)} %get-tuple-element.124), channel_id=1, source_target_pairs={{0,17},{1,16},{2,19},{3,18},{4,21},{5,20},{6,23},{7,22},{8,25},{9,... | collective-permute-start | bytes 344072 | tf_op jit(solution)/shard_map/ppermute | solution.py:566
  84.2 41.6 %collective-permute-start.28 = (f32[392,128]{1,0:T(8,128)S(1)}, f32[392,128]{1,0:T(8,128)S(1)}, u32[]{:S(2)}, u32[]{:S(2)}) collective-permute-start(f32[392,128]{1,0:T(8,128)S(1)} %get-tuple-element.113), channel_id=1, source_target_pairs={{0,2},{1,3},{2,0},{3,1},{4,6},{5,7},{6,4},{7,5},{8,10},{9,11},{10,... | collective-permute-start | bytes 602120 | tf_op jit(solution)/shard_map/ppermute | solution.py:566
  85.2 40.6 %collective-permute-start.30 = (f32[392,128]{1,0:T(8,128)S(1)}, f32[392,128]{1,0:T(8,128)S(1)}, u32[]{:S(2)}, u32[]{:S(2)}) collective-permute-start(f32[392,128]{1,0:T(8,128)S(1)} %get-tuple-element.117), channel_id=1, source_target_pairs={{0,4},{1,5},{2,6},{3,7},{4,0},{5,1},{6,2},{7,3},{8,12},{9,13},{10,... | collective-permute-start | bytes 602120 | tf_op jit(solution)/shard_map/ppermute | solution.py:566
  88.4 37.4 %collective-permute-start.31 = (f32[392,128]{1,0:T(8,128)S(1)}, f32[392,128]{1,0:T(8,128)S(1)}, u32[]{:S(2)}, u32[]{:S(2)}) collective-permute-start(f32[392,128]{1,0:T(8,128)S(1)} %get-tuple-element.118), channel_id=1, source_target_pairs={{0,6},{1,7},{2,4},{3,5},{4,2},{5,3},{6,0},{7,1},{8,14},{9,15},{10,... | collective-permute-start | bytes 602120 | tf_op jit(solution)/shard_map/ppermute | solution.py:566
  89.8 23.1 %collective-permute-start.21 = (f32[192,128]{1,0:T(8,128)S(1)}, f32[192,128]{1,0:T(8,128)S(1)}, u32[]{:S(2)}, u32[]{:S(2)}) collective-permute-start(f32[192,128]{1,0:T(8,128)S(1)} %get-tuple-element.95), channel_id=1, source_target_pairs={{0,4},{1,5},{2,6},{3,7},{4,0},{5,1},{6,2},{7,3},{8,12},{9,13},{10,... | collective-permute-start | bytes 294920 | tf_op jit(solution)/shard_map/ppermute | solution.py:566
  89.9 23.7 %collective-permute-start.22 = (f32[192,128]{1,0:T(8,128)S(1)}, f32[192,128]{1,0:T(8,128)S(1)}, u32[]{:S(2)}, u32[]{:S(2)}) collective-permute-start(f32[192,128]{1,0:T(8,128)S(1)} %get-tuple-element.96), channel_id=1, source_target_pairs={{0,6},{1,7},{2,4},{3,5},{4,2},{5,3},{6,0},{7,1},{8,14},{9,15},{10,... | collective-permute-start | bytes 294920 | tf_op jit(solution)/shard_map/ppermute | solution.py:566
  112.9 1.8 %collective-permute-start.35 = (f32[48,192]{1,0:T(8,128)S(1)}, f32[48,192]{1,0:T(8,128)S(1)}, u32[]{:S(2)}, u32[]{:S(2)}) collective-permute-start(f32[48,192]{1,0:T(8,128)S(1)} %get-tuple-element.126), channel_id=1, source_target_pairs={{0,0},{1,21},{2,13},{3,3},{4,5},{5,27},{6,18},{7,8},{8,22},{9,12},... | collective-permute-start | bytes 110600 | tf_op jit(solution)/shard_map/ppermute | solution.py:566
  113.6 10.6 %collective-permute-start.36 = (f32[48,192]{1,0:T(8,128)S(1)}, f32[48,192]{1,0:T(8,128)S(1)}, u32[]{:S(2)}, u32[]{:S(2)}) collective-permute-start(f32[48,192]{1,0:T(8,128)S(1)} %get-tuple-element.127), channel_id=1, source_target_pairs={{0,10},{1,0},{2,24},{3,13},{4,26},{5,16},{6,29},{7,19},{8,1},{9,23... | collective-permute-start | bytes 110600 | tf_op jit(solution)/shard_map/ppermute | solution.py:566
  114.7 10.4 %collective-permute-start.37 = (f32[48,192]{1,0:T(8,128)S(1)}, f32[48,192]{1,0:T(8,128)S(1)}, u32[]{:S(2)}, u32[]{:S(2)}) collective-permute-start(f32[48,192]{1,0:T(8,128)S(1)} %get-tuple-element.128), channel_id=1, source_target_pairs={{0,21},{1,11},{2,2},{3,24},{4,16},{5,5},{6,8},{7,29},{8,12},{9,1},... | collective-permute-start | bytes 110600 | tf_op jit(solution)/shard_map/ppermute | solution.py:566

commit v3 on v2

--- a/solution.py
+++ b/solution.py
@@ -1,4 +1,5 @@
 import functools
+import itertools
 import math
 
 import jax
@@ -32,7 +33,7 @@
             and rows % (2 * SUBLANES) == 0
             and (3 * self.half) % (2 * SUBLANES) == 0
             and self.pow2
-            and self.plane > 1
+            and self.plane == 4
             and self.cores == 2
             and heads > 2
         )
@@ -107,6 +108,57 @@
         return rounds
 
 
+def direct_plan(lay):
+    table = [[0] * LANES for _ in range(lay.devices)]
+    first, second = [], []
+    spots = {}
+    for head in range(lay.heads):
+        for core in range(lay.cores):
+            runs = {}
+            for m in range(3):
+                for j in range(lay.plane):
+                    base = (m * lay.heads + head) * lay.cores * lay.plane + core * lay.plane
+                    runs.setdefault((m, (base + j) // 3), []).append((m * lay.plane + j, (base + j) % 3))
+            runs = sorted(runs.items(), key=lambda item: -len(item[1]))
+            long_runs, singles = runs[: lay.plane], runs[lay.plane :]
+
+            def hops(member, owner):
+                other, _, there = lay.place(owner)
+                here, away = divmod(member, lay.sub), divmod(other, lay.sub)
+                return abs(here[0] - away[0]) + abs(here[1] - away[1]) + 2 * abs(head - there)
+
+            best = None
+            for order in itertools.permutations(range(lay.plane)):
+                for swap in (singles, singles[::-1]):
+                    roles = [[long_runs[k]] for k in range(lay.plane)]
+                    short = [k for k in range(lay.plane) if len(long_runs[k][1]) == 2]
+                    for k, single in zip(short, swap):
+                        roles[k].append(single)
+                    cost = sum(
+                        len(run[1]) * hops(order[k], run[0][1]) ** 2
+                        for k in range(lay.plane)
+                        for run in roles[k]
+                    )
+                    if best is None or cost < best[0]:
+                        best = cost, order, roles
+            _, order, roles = best
+            held = {}
+            for member, role in zip(order, roles):
+                source = lay.device(member, core, head)
+                held[member] = [piece for run in role for piece, _ in run[1]]
+                for n, ((_, owner), run) in enumerate(role):
+                    (second if n else first).append((source, owner))
+                    for t, (_, spot) in enumerate(run):
+                        spots[owner, spot] = 3 if n else t
+            for member in range(lay.plane):
+                row = table[lay.device(member, core, head)]
+                for r in range(lay.plane):
+                    row[8 + 3 * r : 11 + 3 * r] = held[lay.target(member, r)]
+    for (owner, spot), index in spots.items():
+        table[owner][3 + spot] = index
+    return (first, second), table
+
+
 def split(lay, x):
     if not lay.packed:
         return (x,)
@@ -194,13 +246,14 @@
     return cat([top, bottom], 0), extra
 
 
-def in_slots(lay, parts):
+def in_pieces(lay, parts):
     slot = lay.slot
-    return [cat([p[k * slot : (k + 1) * slot] for p in parts], 0) for k in range(lay.plane)]
-
-
-def member_id(places):
-    return places[0:1, 6:7]
+    return [p[j * slot : (j + 1) * slot] for p in parts for j in range(lay.plane)]
+
+
+def held_pieces(places, pieces, step):
+    first = 8 + 3 * step
+    return cat([choose(pieces, places[0:1, t : t + 1]) for t in range(first, first + 3)], 0)
 
 
 def choose(pieces, index):
@@ -397,7 +450,7 @@
     move, d_total, direct = renormed_back(
         coefficient, d_new, total[0:1, 0:1], initial, grad, moved
     )
-    own = choose(in_slots(lay, in_three(lay, direct)), member_id(places))
+    own = held_pieces(places, in_pieces(lay, in_three(lay, direct)), 0)
     return [move, jnp.broadcast_to(d_total, (SUBLANES, LANES)), own]
 
 
@@ -465,9 +518,9 @@
         lay, slabs, in_three(lay, weights), in_three(lay, moves), d_total[0:1, 0:1]
     )
     grads = [g + b for g, b in zip(grads, in_three(lay, before))]
-    slots, member = in_slots(lay, grads), member_id(places)
+    pieces = in_pieces(lay, grads)
     zero = jnp.zeros((1, 1), F32)
-    outs = [pack(lay, choose(slots, member ^ r), zero) for r in range(lay.plane)]
+    outs = [pack(lay, held_pieces(places, pieces, r), zero) for r in range(lay.plane)]
     return outs + [*parts[:count], stack(parts[count:])]
 
 
@@ -509,6 +562,21 @@
     return [cat([choose(pieces, places[0:1, 3 + q : 4 + q]) for q in range(3)], 0)]
 
 
+def total_two_fn(lay, scale, *args):
+    payloads, direct = args[: lay.plane], args[-1]
+    body, extra = unpack(lay, functools.reduce(jnp.add, payloads))
+    final = (body + direct) / scale
+    return [pack(lay, final, extra), final[2 * lay.slot :]]
+
+
+def finish_all_fn(lay, *args):
+    first, second, places, slabs = args[0], args[1], args[2], args[3:]
+    body, _ = unpack(lay, first)
+    pieces = [body[t * lay.slot : (t + 1) * lay.slot] for t in range(3)] + [second]
+    placed = cat([choose(pieces, places[0:1, t : t + 1]) for t in range(3, 6)], 0)
+    return [placed, *finish_fn(lay, 2, *slabs)]
+
+
 VMEM_LIMIT = 24 * 1024 * 1024
 
 
@@ -608,7 +676,7 @@
     qg = over_heads(qg, tuple(kv[2:]))
     kv = kv + over_cores(kv)
 
-    owner_perms, table = owner_plan(lay)
+    owner_perms, table = (direct_plan if lay.packed else owner_plan)(lay)
     places = lax.dynamic_slice_in_dim(jnp.array(table, jnp.int32), me, 1, 0)
     first = head * lay.hidden + core * lay.half
     turned = []
@@ -679,16 +747,23 @@
         pulled = run(lay, fn(pull_fn, lay), (*gather(d_payload), *kv, weights))
         key_home = total_rows(pulled[plane:])
     sums = scatter(pulled[:plane])
-    pieces = run(lay, fn(total_fn, lay, scale), (*sums, direct, places), deps=tuple(key_home))
-    key_home = back_home(key_home)
+    key_slabs = back_home(key_home)
     (query_grad,) = run(
         lay, fn(finish_fn, lay, 1), (*query_home, head_ids), always=True, deps=tuple(pulled[:1])
     )
-    arrived = [send(x, perm) for x, perm in zip(pieces, owner_perms)]
-    (fast_grad,) = run(lay, place_fn, (*arrived, places))
-    key_grad, value_grad, rate_grad = run(
-        lay, fn(finish_fn, lay, 2), (*key_home, head_ids), always=True
-    )
+    if lay.packed:
+        ready = run(lay, fn(total_two_fn, lay, scale), (*sums, direct), deps=tuple(key_home))
+        arrived = [send(x, perm) for x, perm in zip(ready, owner_perms)]
+        fast_grad, key_grad, value_grad, rate_grad = run(
+            lay, fn(finish_all_fn, lay), (*arrived, places, *key_slabs, head_ids)
+        )
+    else:
+        pieces = run(lay, fn(total_fn, lay, scale), (*sums, direct, places))
+        arrived = [send(x, perm) for x, perm in zip(pieces, owner_perms)]
+        (fast_grad,) = run(lay, place_fn, (*arrived, places))
+        key_grad, value_grad, rate_grad = run(
+            lay, fn(finish_fn, lay, 2), (*key_slabs, head_ids), always=True
+        )
     return query_grad, key_grad, value_grad, rate_grad.T, fast_grad.T
 
 
@@ -699,7 +774,6 @@
         for source, owner, m, spot in chosen:
             table[source][t] = m
             table[owner][3 + spot] = t
-            table[source][6] = lay.place(source)[0]
     return [[(i, o) for i, o, _, _ in chosen] for chosen in rounds], table
 
 

time: 129 us -> 120 us (0.930)
  the two profiles are of different devices: /device:TPU:0 before, /device:TPU:9 now
where the time goes in v3:
time: 120 us
  waiting for transfers between devices  50.4 us (42%)
  starting transfers between devices  49.6 us (41%)
  Pallas kernels  13.8 us (12%)
  local copies, waits for them, and re-layouts  4.95 us (4%)
    ppermute x37, waiting for transfers between devices, send(): return lax.ppermute(x, AXES, perm)  50.4 us
    ppermute x37, starting transfers between devices, send(): return lax.ppermute(x, AXES, perm)  49.6 us
    pallas_call x20, Pallas kernels, run(): pl.pallas_call(kernel, out_shape=[jax.ShapeDtypeStruct(s.shape, s.dtype)...  13.8 us
    unnamed x13, local copies, waits for them, and re-layouts  2.88 us
  transfers between devices with their start and end apart: 37, of which 14 were waited for; matrix products, arithmetic and copies ran while one was open for 2% of the time, Pallas kernels for 3%

profile of v3, /device:TPU:9, one launch (start us, length us, event | category | flops | bytes accessed | tf_op | source)
XLA Modules:
  0.0 119.7 jit_solution(2202103450546525687)
XLA Ops:
  0.7 0.9 copy-done
  1.6 0.9 copy-done.1
  2.5 0.7 copy-done.4
  3.5 2.5 %collective-permute-start.1 = (f32[392,128]{1,0:T(8,128)S(1)}, f32[392,128]{1,0:T(8,128)S(1)}, u32[]{:S(2)}, u32[]{:S(2)}) collective-permute-start(f32[392,128]{1,0:T(8,128)S(1)} %get-tuple-element.71), channel_id=1, source_target_pairs={{0,4},{1,5},{2,6},{3,7},{4,0},{5,1},{6,2},{7,3},{8,12},{9,13},{10,... | collective-permute-start | bytes 602120 | tf_op jit(solution)/shard_map/ppermute | solution.py:634
  6.1 1.5 %collective-permute-start.3 = (f32[392,128]{1,0:T(8,128)S(1)}, f32[392,128]{1,0:T(8,128)S(1)}, u32[]{:S(2)}, u32[]{:S(2)}) collective-permute-start(f32[392,128]{1,0:T(8,128)S(1)} %get-tuple-element.67.refs_1_.refs_5_), channel_id=1, source_target_pairs={{0,8},{1,9},{2,10},{3,11},{4,12},{5,13},{6,14},{7,15},{8,0},{9,1},... | collective-permute-start | bytes 602120 | tf_op jit(solution)/shard_map/ppermute | solution.py:634
  7.7 1.4 %constant_dynamic-slice_fusion.3 = (f32[192,192]{1,0:T(8,128)S(1)}, f32[192,192]{1,0:T(8,128)S(1)}, f32[192,192]{1,0:T(8,128)S(1)}) fusion(f32[192,4608]{1,0:T(8,128)} %param.11, s32[]{:T(128)S(6)} %select_n.18, s32[]{:T(128)S(6)} %select_n.19, s32[]{:T(128)S(6)} %select_n.20), kind=kLoop, calls=%fused_computation.4 | loop fusion | bytes 884748 | tf_op jit(solution)/shard_map/dynamic_slice | solution.py:684
  9.4 1.1 collective-permute-done.refs_2_.refs_6_
  10.5 1.8 %collective-permute-start.4 = (f32[392,128]{1,0:T(8,128)S(1)}, f32[392,128]{1,0:T(8,128)S(1)}, u32[]{:S(2)}, u32[]{:S(2)}) collective-permute-start(f32[392,128]{1,0:T(8,128)S(1)} %collective-permute-done.refs_2_.refs_6_), channel_id=1, source_target_pairs={{0,8},{1,9},{2,10},{3,11},{4,12},{5,13},{6,14},{7,15},{8,0},{9,1},... | collective-permute-start | bytes 602120 | tf_op jit(solution)/shard_map/ppermute | solution.py:634
  12.2 2.5 %collective-permute-done.1.refs_3_.refs_4_ = f32[392,128]{1,0:T(8,128)S(1)} collective-permute-done((f32[392,128]{1,0:T(8,128)S(1)}, f32[392,128]{1,0:T(8,128)S(1)}, u32[]{:S(2)}, u32[]{:S(2)}) %collective-permute-start.1) | collective-permute-done | bytes 200736 | tf_op jit(solution)/shard_map/ppermute | solution.py:634
  14.7 6.5 %collective-permute-start.5 = (f32[392,128]{1,0:T(8,128)S(1)}, f32[392,128]{1,0:T(8,128)S(1)}, u32[]{:S(2)}, u32[]{:S(2)}) collective-permute-start(f32[392,128]{1,0:T(8,128)S(1)} %collective-permute-done.1.refs_3_.refs_4_), channel_id=1, source_target_pairs={{0,8},{1,9},{2,10},{3,11},{4,12},{5,13},{6,14},{7,15},{8,0},{9,1},... | collective-permute-start | bytes 602120 | tf_op jit(solution)/shard_map/ppermute | solution.py:634
  21.2 2.1 %collective-permute-done.2.refs_4_.refs_5_ = f32[392,128]{1,0:T(8,128)S(1)} collective-permute-done((f32[392,128]{1,0:T(8,128)S(1)}, f32[392,128]{1,0:T(8,128)S(1)}, u32[]{:S(2)}, u32[]{:S(2)}) %collective-permute-start.2) | collective-permute-done | bytes 200736 | tf_op jit(solution)/shard_map/ppermute | solution.py:634
  23.3 1.8 %collective-permute-start.6 = (f32[392,128]{1,0:T(8,128)S(1)}, f32[392,128]{1,0:T(8,128)S(1)}, u32[]{:S(2)}, u32[]{:S(2)}) collective-permute-start(f32[392,128]{1,0:T(8,128)S(1)} %collective-permute-done.2.refs_4_.refs_5_), channel_id=1, source_target_pairs={{0,8},{1,9},{2,10},{3,11},{4,12},{5,13},{6,14},{7,15},{8,0},{9,1},... | collective-permute-start | bytes 602120 | tf_op jit(solution)/shard_map/ppermute | solution.py:634
  25.0 0.7 constant_dynamic-slice_fusion.refs_3_.refs_8_.refs_4_.refs_2_
  25.8 0.7 shard_map.111
  26.5 1.2 shard_map.112
  27.7 1.3 %collective-permute-start.7 = (f32[512,128]{1,0:T(8,128)S(1)}, f32[512,128]{1,0:T(8,128)S(1)}, u32[]{:S(2)}, u32[]{:S(2)}) collective-permute-start(f32[512,128]{1,0:T(8,128)S(1)} %get-tuple-element.73.refs_0_), channel_id=1, source_target_pairs={{0,1},{1,0},{2,3},{3,2},{4,5},{5,4},{6,7},{7,6},{8,9},{9,8},{10,11... | collective-permute-start | bytes 786440 | tf_op jit(solution)/shard_map/ppermute | solution.py:634
  29.0 1.2 %collective-permute-start.8 = (f32[368,128]{1,0:T(8,128)S(1)}, f32[368,128]{1,0:T(8,128)S(1)}, u32[]{:S(2)}, u32[]{:S(2)}) collective-permute-start(f32[368,128]{1,0:T(8,128)S(1)} %get-tuple-element.74.refs_2_), channel_id=1, source_target_pairs={{0,16},{1,17},{2,18},{3,19},{4,20},{5,21},{6,22},{7,23},{8,24},{9,... | collective-permute-start | bytes 565256 | tf_op jit(solution)/shard_map/ppermute | solution.py:634
  30.5 2.4 %collective-permute-start.16 = (f32[384,128]{1,0:T(8,128)S(1)}, f32[384,128]{1,0:T(8,128)S(1)}, u32[]{:S(2)}, u32[]{:S(2)}) collective-permute-start(f32[384,128]{1,0:T(8,128)S(1)} %get-tuple-element.88), channel_id=1, source_target_pairs={{0,4},{1,5},{2,6},{3,7},{4,0},{5,1},{6,2},{7,3},{8,12},{9,13},{10,... | collective-permute-start | bytes 589832 | tf_op jit(solution)/shard_map/ppermute | solution.py:634
  33.1 1.8 %collective-permute-done.8.refs_3_ = f32[368,128]{1,0:T(8,128)S(1)} collective-permute-done((f32[368,128]{1,0:T(8,128)S(1)}, f32[368,128]{1,0:T(8,128)S(1)}, u32[]{:S(2)}, u32[]{:S(2)}) %collective-permute-start.8) | collective-permute-done | bytes 188448 | tf_op jit(solution)/shard_map/ppermute | solution.py:634
  35.7 1.3 %collective-permute-start.10 = (f32[368,128]{1,0:T(8,128)S(1)}, f32[368,128]{1,0:T(8,128)S(1)}, u32[]{:S(2)}, u32[]{:S(2)}) collective-permute-start(f32[368,128]{1,0:T(8,128)S(1)} %get-tuple-element.76.refs_2_), channel_id=1, source_target_pairs={{0,1},{1,0},{2,3},{3,2},{4,5},{5,4},{6,7},{7,6},{8,9},{9,8},{10,11... | collective-permute-start | bytes 565256 | tf_op jit(solution)/shard_map/ppermute | solution.py:634
  37.0 1.2 %collective-permute-start.9 = (f32[512,128]{1,0:T(8,128)S(1)}, f32[512,128]{1,0:T(8,128)S(1)}, u32[]{:S(2)}, u32[]{:S(2)}) collective-permute-start(f32[512,128]{1,0:T(8,128)S(1)} %get-tuple-element.75.refs_0_), channel_id=1, source_target_pairs={{0,16},{1,17},{2,18},{3,19},{4,20},{5,21},{6,22},{7,23},{8,24},{9,... | collective-permute-start | bytes 786440 | tf_op jit(solution)/shard_map/ppermute | solution.py:634
  38.2 1.4 %collective-permute-start.12 = (f32[384,128]{1,0:T(8,128)S(1)}, f32[384,128]{1,0:T(8,128)S(1)}, u32[]{:S(2)}, u32[]{:S(2)}) collective-permute-start(f32[384,128]{1,0:T(8,128)S(1)} %get-tuple-element.78.refs_1_), channel_id=1, source_target_pairs={{0,8},{1,9},{2,10},{3,11},{4,12},{5,13},{6,14},{7,15},{8,0},{9,1},... | collective-permute-start | bytes 589832 | tf_op jit(solution)/shard_map/ppermute | solution.py:634
  39.6 2.0 %collective-permute-done.16.refs_0_ = f32[384,128]{1,0:T(8,128)S(1)} collective-permute-done((f32[384,128]{1,0:T(8,128)S(1)}, f32[384,128]{1,0:T(8,128)S(1)}, u32[]{:S(2)}, u32[]{:S(2)}) %collective-permute-start.16) | collective-permute-done | bytes 196640 | tf_op jit(solution)/shard_map/ppermute | solution.py:634
  41.7 6.1 %collective-permute-start.13 = (f32[384,128]{1,0:T(8,128)S(1)}, f32[384,128]{1,0:T(8,128)S(1)}, u32[]{:S(2)}, u32[]{:S(2)}) collective-permute-start(f32[384,128]{1,0:T(8,128)S(1)} %collective-permute-done.11.refs_2_), channel_id=1, source_target_pairs={{0,8},{1,9},{2,10},{3,11},{4,12},{5,13},{6,14},{7,15},{8,0},{9,1},... | collective-permute-start | bytes 589832 | tf_op jit(solution)/shard_map/ppermute | solution.py:634
  47.8 2.2 %collective-permute-done.17.refs_1_ = f32[384,128]{1,0:T(8,128)S(1)} collective-permute-done((f32[384,128]{1,0:T(8,128)S(1)}, f32[384,128]{1,0:T(8,128)S(1)}, u32[]{:S(2)}, u32[]{:S(2)}) %collective-permute-start.17) | collective-permute-done | bytes 196640 | tf_op jit(solution)/shard_map/ppermute | solution.py:634
  50.0 1.7 %collective-permute-start.18 = (f32[384,128]{1,0:T(8,128)S(1)}, f32[384,128]{1,0:T(8,128)S(1)}, u32[]{:S(2)}, u32[]{:S(2)}) collective-permute-start(f32[384,128]{1,0:T(8,128)S(1)} %get-tuple-element.90.refs_2_), channel_id=1, source_target_pairs={{0,8},{1,9},{2,10},{3,11},{4,12},{5,13},{6,14},{7,15},{8,0},{9,1},... | collective-permute-start | bytes 589832 | tf_op jit(solution)/shard_map/ppermute | solution.py:634
  52.2 1.2 %shard_map.116 = (f32[576,192]{1,0:T(8,128)S(1)}, f32[192,128]{1,0:T(8,128)S(1)}, f32[192,128]{1,0:T(8,128)S(1)}, f32[2,192,128]{2,1,0:T(8,128)S(1)}) custom-call(f32[576,192]{1,0:T(8,128)S(1)} %get-tuple-element.77.refs_0_, f32[384,128]{1,0:T(8,128)S(1)} %get-tuple-element.78.refs_1_, f32[384,128]{1,0:T(8,128)S(1)} %collective-permute-done.11.refs_2_, ...), custom_call_target="tpu_custom_call" | custom-call | tf_op jit(solution)/shard_map/pallas_call | solution.py:596
  53.5 1.2 %shard_map.120 = (f32[512,128]{1,0:T(8,128)S(1)}, f32[368,128]{1,0:T(8,128)S(1)}, f32[192,128]{1,0:T(8,128)S(1)}, f32[192,128]{1,0:T(8,128)S(1)}, f32[2,192,128]{2,1,0:T(8,128)S(1)}) custom-call(f32[576,192]{1,0:T(8,128)S(1)} %get-tuple-element.77.refs_0_, f32[576,192]{1,0:T(8,128)S(1)} %get-tuple-element.85.refs_1_, ...), custom_call_target="tpu_custom_call" | custom-call | tf_op jit(solution)/shard_map/pallas_call | solution.py:596
  55.3 5.3 %collective-permute-done.24.refs_3_ = f32[368,128]{1,0:T(8,128)S(1)} collective-permute-done((f32[368,128]{1,0:T(8,128)S(1)}, f32[368,128]{1,0:T(8,128)S(1)}, u32[]{:S(2)}, u32[]{:S(2)}) %collective-permute-start.24) | collective-permute-done | bytes 188448 | tf_op jit(solution)/shard_map/ppermute | solution.py:634
  60.6 1.6 %collective-permute-done.23.refs_1_ = f32[512,128]{1,0:T(8,128)S(1)} collective-permute-done((f32[512,128]{1,0:T(8,128)S(1)}, f32[512,128]{1,0:T(8,128)S(1)}, u32[]{:S(2)}, u32[]{:S(2)}) %collective-permute-start.23) | collective-permute-done | bytes 262176 | tf_op jit(solution)/shard_map/ppermute | solution.py:634
  62.8 4.5 %collective-permute-done.26.refs_3_ = f32[368,128]{1,0:T(8,128)S(1)} collective-permute-done((f32[368,128]{1,0:T(8,128)S(1)}, f32[368,128]{1,0:T(8,128)S(1)}, u32[]{:S(2)}, u32[]{:S(2)}) %collective-permute-start.26) | collective-permute-done | bytes 188448 | tf_op jit(solution)/shard_map/ppermute | solution.py:634
  67.3 1.6 %collective-permute-done.25.refs_1_ = f32[512,128]{1,0:T(8,128)S(1)} collective-permute-done((f32[512,128]{1,0:T(8,128)S(1)}, f32[512,128]{1,0:T(8,128)S(1)}, u32[]{:S(2)}, u32[]{:S(2)}) %collective-permute-start.25) | collective-permute-done | bytes 262176 | tf_op jit(solution)/shard_map/ppermute | solution.py:634
  68.9 0.9 shard_map.123
  69.8 1.5 %shard_map.124 = (f32[2,392,128]{2,1,0:T(8,128)S(1)}, f32[576,192]{1,0:T(8,128)S(1)}) custom-call(f32[576,192]{1,0:T(8,128)S(1)} %get-tuple-element.104.refs_0_, f32[8,128]{1,0:T(8,128)S(1)} %get-tuple-element.105.refs_1_, f32[576,192]{1,0:T(8,128)S(1)} %pad_maximum_fusion.refs_0_.refs_4_.refs_2_, f32[392,128]{1,0:T(8,128)S(1)} %collective-permute-done.5.refs_7_.refs_3_, ...), custom_call_target="tpu_custom_call" | custom-call | tf_op jit(solution)/shard_map/pallas_call | solution.py:596
  71.2 1.5 %shard_map.125 = (f32[576,192]{1,0:T(8,128)S(1)}, f32[392,128]{1,0:T(8,128)S(1)}, f32[392,128]{1,0:T(8,128)S(1)}) custom-call(f32[576,192]{1,0:T(8,128)S(1)} %get-tuple-element.104.refs_0_, f32[8,128]{1,0:T(8,128)S(1)} %get-tuple-element.105.refs_1_, f32[576,192]{1,0:T(8,128)S(1)} %pad_maximum_fusion.refs_0_.refs_4_.refs_2_, ...), custom_call_target="tpu_custom_call" | custom-call | tf_op jit(solution)/shard_map/pallas_call | solution.py:596
  72.7 2.6 %shard_map.126 = (f32[224,128]{1,0:T(8,128)S(1)}, f32[224,128]{1,0:T(8,128)S(1)}, f32[224,128]{1,0:T(8,128)S(1)}, f32[224,128]{1,0:T(8,128)S(1)}, f32[392,128]{1...) custom-call(f32[576,192]{1,0:T(8,128)S(1)} %get-tuple-element.104.refs_0_, ...), custom_call_target="tpu_custom_call" | custom-call | tf_op jit(solution)/shard_map/pallas_call | solution.py:596
  75.2 2.2 %collective-permute-start.30 = (f32[2,392,128]{2,1,0:T(8,128)S(1)}, f32[2,392,128]{2,1,0:T(8,128)S(1)}, u32[]{:S(2)}, u32[]{:S(2)}) collective-permute-start(f32[2,392,128]{2,1,0:T(8,128)S(1)} %get-tuple-element.115), channel_id=1, source_target_pairs={{0,8},{1,9},{2,10},{3,11},{4,12},{5,13},{6,14},{7,15},{8,0},{9,1},... | collective-permute-start | bytes 1204232 | tf_op jit(solution)/shard_map/ppermute | solution.py:634
  78.3 1.4 %collective-permute-done.14.refs_2_ = f32[2,192,128]{2,1,0:T(8,128)S(1)} collective-permute-done((f32[2,192,128]{2,1,0:T(8,128)S(1)}, f32[2,192,128]{2,1,0:T(8,128)S(1)}, u32[]{:S(2)}, u32[]{:S(2)}) %collective-permute-start.14) | collective-permute-done | bytes 196640 | tf_op jit(solution)/shard_map/ppermute | solution.py:634
  80.1 1.2 %collective-permute-start.29 = (f32[224,128]{1,0:T(8,128)S(1)}, f32[224,128]{1,0:T(8,128)S(1)}, u32[]{:S(2)}, u32[]{:S(2)}) collective-permute-start(f32[224,128]{1,0:T(8,128)S(1)} %get-tuple-element.111), channel_id=1, source_target_pairs={{0,17},{1,16},{2,19},{3,18},{4,21},{5,20},{6,23},{7,22},{8,25},{9,... | collective-permute-start | bytes 344072 | tf_op jit(solution)/shard_map/ppermute | solution.py:634
  81.3 2.5 %collective-permute-start.21 = (f32[192,128]{1,0:T(8,128)S(1)}, f32[192,128]{1,0:T(8,128)S(1)}, u32[]{:S(2)}, u32[]{:S(2)}) collective-permute-start(f32[192,128]{1,0:T(8,128)S(1)} %get-tuple-element.95), channel_id=1, source_target_pairs={{0,4},{1,5},{2,6},{3,7},{4,0},{5,1},{6,2},{7,3},{8,12},{9,13},{10,... | collective-permute-start | bytes 294920 | tf_op jit(solution)/shard_map/ppermute | solution.py:634
  84.1 2.2 %collective-permute-start.35 = (f32[392,128]{1,0:T(8,128)S(1)}, f32[392,128]{1,0:T(8,128)S(1)}, u32[]{:S(2)}, u32[]{:S(2)}) collective-permute-start(f32[392,128]{1,0:T(8,128)S(1)} %get-tuple-element.121), channel_id=1, source_target_pairs={{0,4},{1,5},{2,6},{3,7},{4,0},{5,1},{6,2},{7,3},{8,12},{9,13},{10,... | collective-permute-start | bytes 602120 | tf_op jit(solution)/shard_map/ppermute | solution.py:634
  86.6 1.1 collective-permute-start.22
  88.0 5.1 %collective-permute-start.32 = (f32[224,128]{1,0:T(8,128)S(1)}, f32[224,128]{1,0:T(8,128)S(1)}, u32[]{:S(2)}, u32[]{:S(2)}) collective-permute-start(f32[224,128]{1,0:T(8,128)S(1)} %get-tuple-element.123), channel_id=1, source_target_pairs={{0,0},{1,11},{17,21},{16,22},{8,12},{25,23},{9,1},{24,2},{19,3},{1... | collective-permute-start | bytes 344072 | tf_op jit(solution)/shard_map/ppermute | solution.py:634
  93.1 19.3 %collective-permute-done.22.refs_3_ = f32[192,128]{1,0:T(8,128)S(1)} collective-permute-done((f32[192,128]{1,0:T(8,128)S(1)}, f32[192,128]{1,0:T(8,128)S(1)}, u32[]{:S(2)}, u32[]{:S(2)}) %collective-permute-start.22) | collective-permute-done | bytes 98336 | tf_op jit(solution)/shard_map/ppermute | solution.py:634
  112.4 1.3 %collective-permute-start.33 = (f32[48,192]{1,0:T(8,128)S(1)}, f32[48,192]{1,0:T(8,128)S(1)}, u32[]{:S(2)}, u32[]{:S(2)}) collective-permute-start(f32[48,192]{1,0:T(8,128)S(1)} %get-tuple-element.124), channel_id=1, source_target_pairs={{17,1},{16,10},{9,13},{24,22},{3,25},{2,2},{27,5},{26,14},{5,17},{... | collective-permute-start | bytes 110600 | tf_op jit(solution)/shard_map/ppermute | solution.py:634
  113.7 0.8 shard_map.127
  114.5 4.2 %collective-permute-done.33.refs_1_ = f32[48,192]{1,0:T(8,128)S(1)} collective-permute-done((f32[48,192]{1,0:T(8,128)S(1)}, f32[48,192]{1,0:T(8,128)S(1)}, u32[]{:S(2)}, u32[]{:S(2)}) %collective-permute-start.33) | collective-permute-done | bytes 36896 | tf_op jit(solution)/shard_map/ppermute | solution.py:634
  118.7 1.0 shard_map.131
  (74 shorter events, 5.6 us)
Async XLA Ops:
  0.7 0.9 copy-start
  1.6 0.9 copy-start.1
  2.5 0.7 copy-start.4
  3.4 26.8 %copy-start.2 = (bf16[128,768]{1,0:T(8,128)(2,1)S(1)}, bf16[128,768]{1,0:T(8,128)(2,1)}, u32[]{:S(2)}) copy-start(bf16[128,768]{1,0:T(8,128)(2,1)} %refs_0_.3) | copy-start | bytes 589828
  3.4 26.8 %copy-start.3 = (bf16[128,768]{1,0:T(8,128)(2,1)S(1)}, bf16[128,768]{1,0:T(8,128)(2,1)}, u32[]{:S(2)}) copy-start(bf16[128,768]{1,0:T(8,128)(2,1)} %refs_1_.3) | copy-start | bytes 589828
  3.4 7.0 %collective-permute-start = (f32[392,128]{1,0:T(8,128)S(1)}, f32[392,128]{1,0:T(8,128)S(1)}, u32[]{:S(2)}, u32[]{:S(2)}) collective-permute-start(f32[392,128]{1,0:T(8,128)S(1)} %get-tuple-element.68), channel_id=1, source_target_pairs={{0,2},{1,3},{2,0},{3,1},{4,6},{5,7},{6,4},{7,5},{8,10},{9,11},{10,... | collective-permute-start | bytes 602120 | tf_op jit(solution)/shard_map/ppermute | solution.py:634
  3.5 11.2 %collective-permute-start.1 = (f32[392,128]{1,0:T(8,128)S(1)}, f32[392,128]{1,0:T(8,128)S(1)}, u32[]{:S(2)}, u32[]{:S(2)}) collective-permute-start(f32[392,128]{1,0:T(8,128)S(1)} %get-tuple-element.71), channel_id=1, source_target_pairs={{0,4},{1,5},{2,6},{3,7},{4,0},{5,1},{6,2},{7,3},{8,12},{9,13},{10,... | collective-permute-start | bytes 602120 | tf_op jit(solution)/shard_map/ppermute | solution.py:634
  6.0 17.3 %collective-permute-start.2 = (f32[392,128]{1,0:T(8,128)S(1)}, f32[392,128]{1,0:T(8,128)S(1)}, u32[]{:S(2)}, u32[]{:S(2)}) collective-permute-start(f32[392,128]{1,0:T(8,128)S(1)} %get-tuple-element.72), channel_id=1, source_target_pairs={{0,6},{1,7},{2,4},{3,5},{4,2},{5,3},{6,0},{7,1},{8,14},{9,15},{10,... | collective-permute-start | bytes 602120 | tf_op jit(solution)/shard_map/ppermute | solution.py:634
  6.1 20.3 %collective-permute-start.3 = (f32[392,128]{1,0:T(8,128)S(1)}, f32[392,128]{1,0:T(8,128)S(1)}, u32[]{:S(2)}, u32[]{:S(2)}) collective-permute-start(f32[392,128]{1,0:T(8,128)S(1)} %get-tuple-element.67.refs_1_.refs_5_), channel_id=1, source_target_pairs={{0,8},{1,9},{2,10},{3,11},{4,12},{5,13},{6,14},{7,15},{8,0},{9,1},... | collective-permute-start | bytes 602120 | tf_op jit(solution)/shard_map/ppermute | solution.py:634
  10.5 16.0 %collective-permute-start.4 = (f32[392,128]{1,0:T(8,128)S(1)}, f32[392,128]{1,0:T(8,128)S(1)}, u32[]{:S(2)}, u32[]{:S(2)}) collective-permute-start(f32[392,128]{1,0:T(8,128)S(1)} %collective-permute-done.refs_2_.refs_6_), channel_id=1, source_target_pairs={{0,8},{1,9},{2,10},{3,11},{4,12},{5,13},{6,14},{7,15},{8,0},{9,1},... | collective-permute-start | bytes 602120 | tf_op jit(solution)/shard_map/ppermute | solution.py:634
  14.7 11.7 %collective-permute-start.5 = (f32[392,128]{1,0:T(8,128)S(1)}, f32[392,128]{1,0:T(8,128)S(1)}, u32[]{:S(2)}, u32[]{:S(2)}) collective-permute-start(f32[392,128]{1,0:T(8,128)S(1)} %collective-permute-done.1.refs_3_.refs_4_), channel_id=1, source_target_pairs={{0,8},{1,9},{2,10},{3,11},{4,12},{5,13},{6,14},{7,15},{8,0},{9,1},... | collective-permute-start | bytes 602120 | tf_op jit(solution)/shard_map/ppermute | solution.py:634
  23.3 3.2 %collective-permute-start.6 = (f32[392,128]{1,0:T(8,128)S(1)}, f32[392,128]{1,0:T(8,128)S(1)}, u32[]{:S(2)}, u32[]{:S(2)}) collective-permute-start(f32[392,128]{1,0:T(8,128)S(1)} %collective-permute-done.2.refs_4_.refs_5_), channel_id=1, source_target_pairs={{0,8},{1,9},{2,10},{3,11},{4,12},{5,13},{6,14},{7,15},{8,0},{9,1},... | collective-permute-start | bytes 602120 | tf_op jit(solution)/shard_map/ppermute | solution.py:634
  27.7 7.9 %collective-permute-start.7 = (f32[512,128]{1,0:T(8,128)S(1)}, f32[512,128]{1,0:T(8,128)S(1)}, u32[]{:S(2)}, u32[]{:S(2)}) collective-permute-start(f32[512,128]{1,0:T(8,128)S(1)} %get-tuple-element.73.refs_0_), channel_id=1, source_target_pairs={{0,1},{1,0},{2,3},{3,2},{4,5},{5,4},{6,7},{7,6},{8,9},{9,8},{10,11... | collective-permute-start | bytes 786440 | tf_op jit(solution)/shard_map/ppermute | solution.py:634
  29.0 6.0 %collective-permute-start.8 = (f32[368,128]{1,0:T(8,128)S(1)}, f32[368,128]{1,0:T(8,128)S(1)}, u32[]{:S(2)}, u32[]{:S(2)}) collective-permute-start(f32[368,128]{1,0:T(8,128)S(1)} %get-tuple-element.74.refs_2_), channel_id=1, source_target_pairs={{0,16},{1,17},{2,18},{3,19},{4,20},{5,21},{6,22},{7,23},{8,24},{9,... | collective-permute-start | bytes 565256 | tf_op jit(solution)/shard_map/ppermute | solution.py:634
  30.4 7.8 %collective-permute-start.11 = (f32[384,128]{1,0:T(8,128)S(1)}, f32[384,128]{1,0:T(8,128)S(1)}, u32[]{:S(2)}, u32[]{:S(2)}) collective-permute-start(f32[384,128]{1,0:T(8,128)S(1)} %get-tuple-element.79), channel_id=1, source_target_pairs={{0,2},{1,3},{2,0},{3,1},{4,6},{5,7},{6,4},{7,5},{8,10},{9,11},{10,... | collective-permute-start | bytes 589832 | tf_op jit(solution)/shard_map/ppermute | solution.py:634
  30.5 11.1 %collective-permute-start.16 = (f32[384,128]{1,0:T(8,128)S(1)}, f32[384,128]{1,0:T(8,128)S(1)}, u32[]{:S(2)}, u32[]{:S(2)}) collective-permute-start(f32[384,128]{1,0:T(8,128)S(1)} %get-tuple-element.88), channel_id=1, source_target_pairs={{0,4},{1,5},{2,6},{3,7},{4,0},{5,1},{6,2},{7,3},{8,12},{9,13},{10,... | collective-permute-start | bytes 589832 | tf_op jit(solution)/shard_map/ppermute | solution.py:634
  33.0 17.1 %collective-permute-start.17 = (f32[384,128]{1,0:T(8,128)S(1)}, f32[384,128]{1,0:T(8,128)S(1)}, u32[]{:S(2)}, u32[]{:S(2)}) collective-permute-start(f32[384,128]{1,0:T(8,128)S(1)} %get-tuple-element.89), channel_id=1, source_target_pairs={{0,6},{1,7},{2,4},{3,5},{4,2},{5,3},{6,0},{7,1},{8,14},{9,15},{10,... | collective-permute-start | bytes 589832 | tf_op jit(solution)/shard_map/ppermute | solution.py:634
  35.7 16.0 %collective-permute-start.10 = (f32[368,128]{1,0:T(8,128)S(1)}, f32[368,128]{1,0:T(8,128)S(1)}, u32[]{:S(2)}, u32[]{:S(2)}) collective-permute-start(f32[368,128]{1,0:T(8,128)S(1)} %get-tuple-element.76.refs_2_), channel_id=1, source_target_pairs={{0,1},{1,0},{2,3},{3,2},{4,5},{5,4},{6,7},{7,6},{8,9},{9,8},{10,11... | collective-permute-start | bytes 565256 | tf_op jit(solution)/shard_map/ppermute | solution.py:634
  37.0 14.8 %collective-permute-start.9 = (f32[512,128]{1,0:T(8,128)S(1)}, f32[512,128]{1,0:T(8,128)S(1)}, u32[]{:S(2)}, u32[]{:S(2)}) collective-permute-start(f32[512,128]{1,0:T(8,128)S(1)} %get-tuple-element.75.refs_0_), channel_id=1, source_target_pairs={{0,16},{1,17},{2,18},{3,19},{4,20},{5,21},{6,22},{7,23},{8,24},{9,... | collective-permute-start | bytes 786440 | tf_op jit(solution)/shard_map/ppermute | solution.py:634
  38.2 14.0 %collective-permute-start.12 = (f32[384,128]{1,0:T(8,128)S(1)}, f32[384,128]{1,0:T(8,128)S(1)}, u32[]{:S(2)}, u32[]{:S(2)}) collective-permute-start(f32[384,128]{1,0:T(8,128)S(1)} %get-tuple-element.78.refs_1_), channel_id=1, source_target_pairs={{0,8},{1,9},{2,10},{3,11},{4,12},{5,13},{6,14},{7,15},{8,0},{9,1},... | collective-permute-start | bytes 589832 | tf_op jit(solution)/shard_map/ppermute | solution.py:634
  41.7 10.5 %collective-permute-start.13 = (f32[384,128]{1,0:T(8,128)S(1)}, f32[384,128]{1,0:T(8,128)S(1)}, u32[]{:S(2)}, u32[]{:S(2)}) collective-permute-start(f32[384,128]{1,0:T(8,128)S(1)} %collective-permute-done.11.refs_2_), channel_id=1, source_target_pairs={{0,8},{1,9},{2,10},{3,11},{4,12},{5,13},{6,14},{7,15},{8,0},{9,1},... | collective-permute-start | bytes 589832 | tf_op jit(solution)/shard_map/ppermute | solution.py:634
  50.0 3.4 %collective-permute-start.18 = (f32[384,128]{1,0:T(8,128)S(1)}, f32[384,128]{1,0:T(8,128)S(1)}, u32[]{:S(2)}, u32[]{:S(2)}) collective-permute-start(f32[384,128]{1,0:T(8,128)S(1)} %get-tuple-element.90.refs_2_), channel_id=1, source_target_pairs={{0,8},{1,9},{2,10},{3,11},{4,12},{5,13},{6,14},{7,15},{8,0},{9,1},... | collective-permute-start | bytes 589832 | tf_op jit(solution)/shard_map/ppermute | solution.py:634
  51.7 1.8 %collective-permute-start.19 = (f32[384,128]{1,0:T(8,128)S(1)}, f32[384,128]{1,0:T(8,128)S(1)}, u32[]{:S(2)}, u32[]{:S(2)}) collective-permute-start(f32[384,128]{1,0:T(8,128)S(1)} %get-tuple-element.91.refs_3_), channel_id=1, source_target_pairs={{0,8},{1,9},{2,10},{3,11},{4,12},{5,13},{6,14},{7,15},{8,0},{9,1},... | collective-permute-start | bytes 589832 | tf_op jit(solution)/shard_map/ppermute | solution.py:634
  54.7 7.5 %collective-permute-start.23 = (f32[512,128]{1,0:T(8,128)S(1)}, f32[512,128]{1,0:T(8,128)S(1)}, u32[]{:S(2)}, u32[]{:S(2)}) collective-permute-start(f32[512,128]{1,0:T(8,128)S(1)} %get-tuple-element.97.refs_0_), channel_id=1, source_target_pairs={{0,1},{1,0},{2,3},{3,2},{4,5},{5,4},{6,7},{7,6},{8,9},{9,8},{10,11... | collective-permute-start | bytes 786440 | tf_op jit(solution)/shard_map/ppermute | solution.py:634
  55.0 5.6 %collective-permute-start.24 = (f32[368,128]{1,0:T(8,128)S(1)}, f32[368,128]{1,0:T(8,128)S(1)}, u32[]{:S(2)}, u32[]{:S(2)}) collective-permute-start(f32[368,128]{1,0:T(8,128)S(1)} %get-tuple-element.98.refs_2_), channel_id=1, source_target_pairs={{0,16},{1,17},{2,18},{3,19},{4,20},{5,21},{6,22},{7,23},{8,24},{9,... | collective-permute-start | bytes 565256 | tf_op jit(solution)/shard_map/ppermute | solution.py:634
  62.3 6.6 %collective-permute-start.25 = (f32[512,128]{1,0:T(8,128)S(1)}, f32[512,128]{1,0:T(8,128)S(1)}, u32[]{:S(2)}, u32[]{:S(2)}) collective-permute-start(f32[512,128]{1,0:T(8,128)S(1)} %get-tuple-element.99.refs_0_), channel_id=1, source_target_pairs={{0,16},{1,17},{2,18},{3,19},{4,20},{5,21},{6,22},{7,23},{8,24},{9,... | collective-permute-start | bytes 786440 | tf_op jit(solution)/shard_map/ppermute | solution.py:634
  62.6 4.7 %collective-permute-start.26 = (f32[368,128]{1,0:T(8,128)S(1)}, f32[368,128]{1,0:T(8,128)S(1)}, u32[]{:S(2)}, u32[]{:S(2)}) collective-permute-start(f32[368,128]{1,0:T(8,128)S(1)} %get-tuple-element.100.refs_2_), channel_id=1, source_target_pairs={{0,1},{1,0},{2,3},{3,2},{4,5},{5,4},{6,7},{7,6},{8,9},{9,8},{10,11... | collective-permute-start | bytes 565256 | tf_op jit(solution)/shard_map/ppermute | solution.py:634
  75.2 4.8 %collective-permute-start.30 = (f32[2,392,128]{2,1,0:T(8,128)S(1)}, f32[2,392,128]{2,1,0:T(8,128)S(1)}, u32[]{:S(2)}, u32[]{:S(2)}) collective-permute-start(f32[2,392,128]{2,1,0:T(8,128)S(1)} %get-tuple-element.115), channel_id=1, source_target_pairs={{0,8},{1,9},{2,10},{3,11},{4,12},{5,13},{6,14},{7,15},{8,0},{9,1},... | collective-permute-start | bytes 1204232 | tf_op jit(solution)/shard_map/ppermute | solution.py:634
  77.5 3.8 %collective-permute-start.31 = (f32[2,392,128]{2,1,0:T(8,128)S(1)}, f32[2,392,128]{2,1,0:T(8,128)S(1)}, u32[]{:S(2)}, u32[]{:S(2)}) collective-permute-start(f32[2,392,128]{2,1,0:T(8,128)S(1)} %get-tuple-element.120), channel_id=1, source_target_pairs={{0,8},{1,9},{2,10},{3,11},{4,12},{5,13},{6,14},{7,15},{8,0},{9,1},... | collective-permute-start | bytes 1204232 | tf_op jit(solution)/shard_map/ppermute | solution.py:634
  77.6 2.1 %collective-permute-start.14 = (f32[2,192,128]{2,1,0:T(8,128)S(1)}, f32[2,192,128]{2,1,0:T(8,128)S(1)}, u32[]{:S(2)}, u32[]{:S(2)}) collective-permute-start(f32[2,192,128]{2,1,0:T(8,128)S(1)} %get-tuple-element.82), channel_id=1, source_target_pairs={{0,8},{1,9},{2,10},{3,11},{4,12},{5,13},{6,14},{7,15},{8,0},{9,1},... | collective-permute-start | bytes 589832 | tf_op jit(solution)/shard_map/ppermute | solution.py:634
  78.0 2.0 %collective-permute-start.20 = (f32[2,192,128]{2,1,0:T(8,128)S(1)}, f32[2,192,128]{2,1,0:T(8,128)S(1)}, u32[]{:S(2)}, u32[]{:S(2)}) collective-permute-start(f32[2,192,128]{2,1,0:T(8,128)S(1)} %get-tuple-element.94), channel_id=1, source_target_pairs={{0,8},{1,9},{2,10},{3,11},{4,12},{5,13},{6,14},{7,15},{8,0},{9,1},... | collective-permute-start | bytes 589832 | tf_op jit(solution)/shard_map/ppermute | solution.py:634
  78.1 6.0 %collective-permute-start.27 = (f32[224,128]{1,0:T(8,128)S(1)}, f32[224,128]{1,0:T(8,128)S(1)}, u32[]{:S(2)}, u32[]{:S(2)}) collective-permute-start(f32[224,128]{1,0:T(8,128)S(1)} %get-tuple-element.109), channel_id=1, source_target_pairs={{0,1},{1,0},{2,3},{3,2},{4,5},{5,4},{6,7},{7,6},{8,9},{9,8},{10,11... | collective-permute-start | bytes 344072 | tf_op jit(solution)/shard_map/ppermute | solution.py:634
  79.7 6.6 %collective-permute-start.28 = (f32[224,128]{1,0:T(8,128)S(1)}, f32[224,128]{1,0:T(8,128)S(1)}, u32[]{:S(2)}, u32[]{:S(2)}) collective-permute-start(f32[224,128]{1,0:T(8,128)S(1)} %get-tuple-element.110), channel_id=1, source_target_pairs={{0,16},{1,17},{2,18},{3,19},{4,20},{5,21},{6,22},{7,23},{8,24},{9,... | collective-permute-start | bytes 344072 | tf_op jit(solution)/shard_map/ppermute | solution.py:634
  80.0 3.9 %collective-permute-start.15 = (f32[192,128]{1,0:T(8,128)S(1)}, f32[192,128]{1,0:T(8,128)S(1)}, u32[]{:S(2)}, u32[]{:S(2)}) collective-permute-start(f32[192,128]{1,0:T(8,128)S(1)} %get-tuple-element.84), channel_id=1, source_target_pairs={{0,2},{1,3},{2,0},{3,1},{4,6},{5,7},{6,4},{7,5},{8,10},{9,11},{10,... | collective-permute-start | bytes 294920 | tf_op jit(solution)/shard_map/ppermute | solution.py:634
  80.1 6.6 %collective-permute-start.29 = (f32[224,128]{1,0:T(8,128)S(1)}, f32[224,128]{1,0:T(8,128)S(1)}, u32[]{:S(2)}, u32[]{:S(2)}) collective-permute-start(f32[224,128]{1,0:T(8,128)S(1)} %get-tuple-element.111), channel_id=1, source_target_pairs={{0,17},{1,16},{2,19},{3,18},{4,21},{5,20},{6,23},{7,22},{8,25},{9,... | collective-permute-start | bytes 344072 | tf_op jit(solution)/shard_map/ppermute | solution.py:634
  81.3 6.6 %collective-permute-start.21 = (f32[192,128]{1,0:T(8,128)S(1)}, f32[192,128]{1,0:T(8,128)S(1)}, u32[]{:S(2)}, u32[]{:S(2)}) collective-permute-start(f32[192,128]{1,0:T(8,128)S(1)} %get-tuple-element.95), channel_id=1, source_target_pairs={{0,4},{1,5},{2,6},{3,7},{4,0},{5,1},{6,2},{7,3},{8,12},{9,13},{10,... | collective-permute-start | bytes 294920 | tf_op jit(solution)/shard_map/ppermute | solution.py:634
  83.9 34.8 %collective-permute-start.34 = (f32[392,128]{1,0:T(8,128)S(1)}, f32[392,128]{1,0:T(8,128)S(1)}, u32[]{:S(2)}, u32[]{:S(2)}) collective-permute-start(f32[392,128]{1,0:T(8,128)S(1)} %get-tuple-element.117), channel_id=1, source_target_pairs={{0,2},{1,3},{2,0},{3,1},{4,6},{5,7},{6,4},{7,5},{8,10},{9,11},{10,... | collective-permute-start | bytes 602120 | tf_op jit(solution)/shard_map/ppermute | solution.py:634
  84.1 34.6 %collective-permute-start.35 = (f32[392,128]{1,0:T(8,128)S(1)}, f32[392,128]{1,0:T(8,128)S(1)}, u32[]{:S(2)}, u32[]{:S(2)}) collective-permute-start(f32[392,128]{1,0:T(8,128)S(1)} %get-tuple-element.121), channel_id=1, source_target_pairs={{0,4},{1,5},{2,6},{3,7},{4,0},{5,1},{6,2},{7,3},{8,12},{9,13},{10,... | collective-permute-start | bytes 602120 | tf_op jit(solution)/shard_map/ppermute | solution.py:634
  86.3 32.4 %collective-permute-start.36 = (f32[392,128]{1,0:T(8,128)S(1)}, f32[392,128]{1,0:T(8,128)S(1)}, u32[]{:S(2)}, u32[]{:S(2)}) collective-permute-start(f32[392,128]{1,0:T(8,128)S(1)} %get-tuple-element.122), channel_id=1, source_target_pairs={{0,6},{1,7},{2,4},{3,5},{4,2},{5,3},{6,0},{7,1},{8,14},{9,15},{10,... | collective-permute-start | bytes 602120 | tf_op jit(solution)/shard_map/ppermute | solution.py:634
  86.6 25.8 %collective-permute-start.22 = (f32[192,128]{1,0:T(8,128)S(1)}, f32[192,128]{1,0:T(8,128)S(1)}, u32[]{:S(2)}, u32[]{:S(2)}) collective-permute-start(f32[192,128]{1,0:T(8,128)S(1)} %get-tuple-element.96), channel_id=1, source_target_pairs={{0,6},{1,7},{2,4},{3,5},{4,2},{5,3},{6,0},{7,1},{8,14},{9,15},{10,... | collective-permute-start | bytes 294920 | tf_op jit(solution)/shard_map/ppermute | solution.py:634
  88.0 30.7 %collective-permute-start.32 = (f32[224,128]{1,0:T(8,128)S(1)}, f32[224,128]{1,0:T(8,128)S(1)}, u32[]{:S(2)}, u32[]{:S(2)}) collective-permute-start(f32[224,128]{1,0:T(8,128)S(1)} %get-tuple-element.123), channel_id=1, source_target_pairs={{0,0},{1,11},{17,21},{16,22},{8,12},{25,23},{9,1},{24,2},{19,3},{1... | collective-permute-start | bytes 344072 | tf_op jit(solution)/shard_map/ppermute | solution.py:634
  112.4 6.3 %collective-permute-start.33 = (f32[48,192]{1,0:T(8,128)S(1)}, f32[48,192]{1,0:T(8,128)S(1)}, u32[]{:S(2)}, u32[]{:S(2)}) collective-permute-start(f32[48,192]{1,0:T(8,128)S(1)} %get-tuple-element.124), channel_id=1, source_target_pairs={{17,1},{16,10},{9,13},{24,22},{3,25},{2,2},{27,5},{26,14},{5,17},{... | collective-permute-start | bytes 110600 | tf_op jit(solution)/shard_map/ppermute | solution.py:634

commit v4 on v3

--- a/solution.py
+++ b/solution.py
@@ -231,7 +231,7 @@
 def wide_rows(lay):
     step = 2 * SUBLANES
     total = 3 * lay.half
-    return total - total * 5 // 12 // step * step
+    return total - total * 17 // 36 // step * step
 
 
 def pack_parts(lay, grads, extra):
@@ -446,12 +446,18 @@
 
 def renorm_back_all_fn(lay, coefficient, *args):
     d_new, _ = unpack_parts(lay, *args[:4])
+    initial, grad, moved, total = args[4:]
+    move, d_total, _ = renormed_back(
+        coefficient, d_new, total[0:1, 0:1], initial, grad, moved
+    )
+    return [move, jnp.broadcast_to(d_total, (SUBLANES, LANES))]
+
+
+def direct_fn(lay, coefficient, *args):
+    d_new, _ = unpack_parts(lay, *args[:4])
     initial, grad, moved, total, places = args[4:]
-    move, d_total, direct = renormed_back(
-        coefficient, d_new, total[0:1, 0:1], initial, grad, moved
-    )
-    own = held_pieces(places, in_pieces(lay, in_three(lay, direct)), 0)
-    return [move, jnp.broadcast_to(d_total, (SUBLANES, LANES)), own]
+    direct = renormed_back(coefficient, d_new, total[0:1, 0:1], initial, grad, moved)[2]
+    return [held_pieces(places, in_pieces(lay, in_three(lay, direct)), 0)]
 
 
 def pull_math(lay, slabs, weights, moves, d_total):
@@ -499,23 +505,64 @@
     return outs + parts[:heads] + ([stack(parts[heads:])] if lay.cores > 1 else [])
 
 
-def pull_other_fn(lay, moves, d_total, weights, *slabs):
-    grads, parts = pull_math(
-        lay, slabs, in_three(lay, weights), in_three(lay, moves), d_total[0:1, 0:1]
+def ready_fn(lay, weights, *slabs):
+    keys, values = join_rows(lay, slabs)
+    gate, up, down = (split(lay, w) for w in in_three(lay, weights))
+    a, b = dots_left((gate, up), keys, NN)
+    (u,) = dots_left((down,), values, NN)
+    sig, silu, rest, slope = gates(a)
+    mu = -join_rates(lay, slabs)
+    hidden, um = silu * b, mu * u
+    steep = slope * b
+    bent = um * (sig * rest * (2.0 + a * (rest - sig))) * b
+    wide = jnp.broadcast_to(mu, (SUBLANES, mu.shape[1]))
+    outs = [keys, values, wide, steep, silu, hidden, u, bent, um * slope]
+    return outs + [*split(lay, um * steep), *split(lay, um * silu), *split(lay, mu * hidden)]
+
+
+def pull_ready(lay, ready, weights, moves, d_total):
+    keys, values, mu, steep, silu, hidden, u, bent, ums = ready[:9]
+    gta, gtb, mh = ready[9:11], ready[11:13], ready[13:15]
+    mu = mu[0:1]
+    gate_move, up_move, down_move = (split(lay, w) for w in moves)
+    ta, tb = dots_left((gate_move, up_move), keys, NN)
+    (w,) = dots_left((down_move,), values, NN)
+    hidden_dot = steep * ta + silu * tb
+    rate_part = -jnp.sum(w * hidden + u * hidden_dot, 0, keepdims=True) + d_total
+    wm = mu * w
+    ga = split(lay, wm * steep + bent * ta + ums * tb)
+    gb = split(lay, wm * silu + ums * ta)
+    md = split(lay, mu * hidden_dot)
+    grads = dots_left((ga, gb), keys, NT) + dots_left((md,), values, NT)
+    turned = split(lay, cat([weights[0], weights[1], moves[0], moves[1]], 0).T)
+    d_key = dot_both(turned, tuple(cat(x, 0) for x in zip(ga, gb, gta, gtb)), NN)
+    turned = split(lay, cat([moves[2], weights[2]], 0).T)
+    d_value = dot_both(turned, tuple(cat(x, 0) for x in zip(mh, md)), NN)
+    parts = []
+    for i in range(keys.shape[1] // LANES):
+        take = slice(i * LANES, (i + 1) * LANES)
+        rate_rows = jnp.broadcast_to(rate_part[:, take], (SUBLANES, LANES))
+        parts.append(cat([d_key[:, take], d_value[:, take], rate_rows], 0))
+    return grads, parts
+
+
+def pull_other_fn(lay, moves, d_total, weights, *ready):
+    grads, parts = pull_ready(
+        lay, ready, in_three(lay, weights), in_three(lay, moves), d_total[0:1, 0:1]
     )
     return [stack(parts), cat(grads, 0)]
 
 
-def pull_own_fn(lay, moves, d_total, weights, before, *slabs):
-    grads, parts = pull_math(
-        lay, slabs, in_three(lay, weights), in_three(lay, moves), d_total[0:1, 0:1]
+def pull_own_fn(lay, moves, d_total, weights, before, *ready):
+    grads, parts = pull_ready(
+        lay, ready, in_three(lay, weights), in_three(lay, moves), d_total[0:1, 0:1]
     )
     return [cat(grads, 0) + before, *parts]
 
 
-def pull_last_fn(lay, count, moves, d_total, weights, before, places, *slabs):
-    grads, parts = pull_math(
-        lay, slabs, in_three(lay, weights), in_three(lay, moves), d_total[0:1, 0:1]
+def pull_last_fn(lay, count, moves, d_total, weights, before, places, *ready):
+    grads, parts = pull_ready(
+        lay, ready, in_three(lay, weights), in_three(lay, moves), d_total[0:1, 0:1]
     )
     grads = [g + b for g, b in zip(grads, in_three(lay, before))]
     pieces = in_pieces(lay, grads)
@@ -716,21 +763,21 @@
             applied[2:-1], applied[-1]
         )
         sums = exchange(*applied[:2])
-        move, d_total, direct = run(
-            lay,
-            fn(renorm_back_all_fn, lay, coefficient),
-            (*sums, weights, grad, moved, total, places),
-        )
+        groups = (kv[heads + 2 :], kv[2:heads], kv[:2] + kv[heads : heads + 2])
+        ready = [run(lay, fn(ready_fn, lay), (weights, *rows)) for rows in groups]
+        state = (*sums, weights, grad, moved, total)
+        move, d_total = run(lay, fn(renorm_back_all_fn, lay, coefficient), state)
         query_home = back_home(query_home)
-        other, before = run(lay, fn(pull_other_fn, lay), (move, d_total, weights, *kv[heads + 2 :]))
+        other, before = run(lay, fn(pull_other_fn, lay), (move, d_total, weights, *ready[0]))
         before, *key_far = run(
-            lay, fn(pull_own_fn, lay), (move, d_total, weights, before, *kv[2:heads])
+            lay, fn(pull_own_fn, lay), (move, d_total, weights, before, *ready[1])
         )
         key_far = add_home(key_far, other)
         pulled = run(
-            lay,
-            fn(pull_last_fn, lay, 2),
-            (move, d_total, weights, before, places, *kv[:2], *kv[heads : heads + 2]),
+            lay, fn(pull_last_fn, lay, 2), (move, d_total, weights, before, places, *ready[2])
+        )
+        (direct,) = run(
+            lay, fn(direct_fn, lay, coefficient), (*state, places), deps=tuple(pulled[:1])
         )
         key_home = add_home(pulled[plane : plane + 2], pulled[-1]) + key_far
     else:

time: 120 us -> 127 us (1.058)
  starting transfers between devices: 49.6 us -> 56.6 us
  waiting for transfers between devices: 50.4 us -> 48.5 us
  Pallas kernels: 13.8 us -> 15.2 us
    ppermute x37, starting transfers between devices: 49.6 us -> 56.6 us  [send(): return lax.ppermute(x, AXES, perm)]
    ppermute x37, waiting for transfers between devices: 50.4 us -> 48.5 us  [send(): return lax.ppermute(x, AXES, perm)]
    pallas_call x20 -> x24, Pallas kernels: 13.8 us -> 15.2 us  [run(): pl.pallas_call(kernel, out_shape=[jax.ShapeDtypeStruct(s.shape, s.dtype)...]
  transfers between devices with their start and end apart: 37 -> 37, of which waited for: 14 -> 14; matrix products, arithmetic and copies ran while one was open for 2% -> 2% of each run, Pallas kernels for 3% -> 8%
where the time goes in v4:
time: 127 us; the launch traced here: 126 us
  starting transfers between devices  56.6 us (45%)
  waiting for transfers between devices  48.5 us (38%)
  Pallas kernels  15.2 us (12%)
  local copies, waits for them, and re-layouts  4.95 us (4%)
    ppermute x37, starting transfers between devices, send(): return lax.ppermute(x, AXES, perm)  56.6 us
    ppermute x37, waiting for transfers between devices, send(): return lax.ppermute(x, AXES, perm)  48.5 us
    pallas_call x24, Pallas kernels, run(): pl.pallas_call(kernel, out_shape=[jax.ShapeDtypeStruct(s.shape, s.dtype)...  15.2 us
    unnamed x13, local copies, waits for them, and re-layouts  2.88 us
  transfers between devices with their start and end apart: 37, of which 14 were waited for; matrix products, arithmetic and copies ran while one was open for 2% of the time, Pallas kernels for 8%

profile of v4, /device:TPU:9, one launch (start us, length us, event | category | flops | bytes accessed | tf_op | source)
XLA Modules:
  0.0 126.4 jit_solution(5162433943989882809)
XLA Ops:
  0.7 0.9 copy-done
  1.6 0.9 copy-done.1
  3.5 2.5 %collective-permute-start.1 = (f32[392,128]{1,0:T(8,128)S(1)}, f32[392,128]{1,0:T(8,128)S(1)}, u32[]{:S(2)}, u32[]{:S(2)}) collective-permute-start(f32[392,128]{1,0:T(8,128)S(1)} %get-tuple-element.115), channel_id=1, source_target_pairs={{0,4},{1,5},{2,6},{3,7},{4,0},{5,1},{6,2},{7,3},{8,12},{9,13},{10,... | collective-permute-start | bytes 602120 | tf_op jit(solution)/shard_map/ppermute | solution.py:681
  6.1 1.5 %collective-permute-start.3 = (f32[392,128]{1,0:T(8,128)S(1)}, f32[392,128]{1,0:T(8,128)S(1)}, u32[]{:S(2)}, u32[]{:S(2)}) collective-permute-start(f32[392,128]{1,0:T(8,128)S(1)} %get-tuple-element.111.refs_1_), channel_id=1, source_target_pairs={{0,8},{1,9},{2,10},{3,11},{4,12},{5,13},{6,14},{7,15},{8,0},{9,1},... | collective-permute-start | bytes 602120 | tf_op jit(solution)/shard_map/ppermute | solution.py:681
  7.6 1.4 %constant_dynamic-slice_fusion.3 = (f32[192,192]{1,0:T(8,128)S(1)}, f32[192,192]{1,0:T(8,128)S(1)}, f32[192,192]{1,0:T(8,128)S(1)}) fusion(f32[192,4608]{1,0:T(8,128)} %param.11, s32[]{:T(128)S(6)} %select_n.18, s32[]{:T(128)S(6)} %select_n.19, s32[]{:T(128)S(6)} %select_n.20), kind=kLoop, calls=%fused_computation.4 | loop fusion | bytes 884748 | tf_op jit(solution)/shard_map/dynamic_slice | solution.py:731
  9.4 1.1 collective-permute-done.refs_2_
  10.5 1.8 %collective-permute-start.4 = (f32[392,128]{1,0:T(8,128)S(1)}, f32[392,128]{1,0:T(8,128)S(1)}, u32[]{:S(2)}, u32[]{:S(2)}) collective-permute-start(f32[392,128]{1,0:T(8,128)S(1)} %collective-permute-done.refs_2_), channel_id=1, source_target_pairs={{0,8},{1,9},{2,10},{3,11},{4,12},{5,13},{6,14},{7,15},{8,0},{9,1},... | collective-permute-start | bytes 602120 | tf_op jit(solution)/shard_map/ppermute | solution.py:681
  12.2 2.5 %collective-permute-done.1.refs_3_.refs_1_ = f32[392,128]{1,0:T(8,128)S(1)} collective-permute-done((f32[392,128]{1,0:T(8,128)S(1)}, f32[392,128]{1,0:T(8,128)S(1)}, u32[]{:S(2)}, u32[]{:S(2)}) %collective-permute-start.1) | collective-permute-done | bytes 200736 | tf_op jit(solution)/shard_map/ppermute | solution.py:681
  14.7 6.5 %collective-permute-start.5 = (f32[392,128]{1,0:T(8,128)S(1)}, f32[392,128]{1,0:T(8,128)S(1)}, u32[]{:S(2)}, u32[]{:S(2)}) collective-permute-start(f32[392,128]{1,0:T(8,128)S(1)} %collective-permute-done.1.refs_3_.refs_1_), channel_id=1, source_target_pairs={{0,8},{1,9},{2,10},{3,11},{4,12},{5,13},{6,14},{7,15},{8,0},{9,1},... | collective-permute-start | bytes 602120 | tf_op jit(solution)/shard_map/ppermute | solution.py:681
  21.2 2.1 %collective-permute-done.2.refs_4_.refs_2_ = f32[392,128]{1,0:T(8,128)S(1)} collective-permute-done((f32[392,128]{1,0:T(8,128)S(1)}, f32[392,128]{1,0:T(8,128)S(1)}, u32[]{:S(2)}, u32[]{:S(2)}) %collective-permute-start.2) | collective-permute-done | bytes 200736 | tf_op jit(solution)/shard_map/ppermute | solution.py:681
  23.2 1.8 %collective-permute-start.6 = (f32[392,128]{1,0:T(8,128)S(1)}, f32[392,128]{1,0:T(8,128)S(1)}, u32[]{:S(2)}, u32[]{:S(2)}) collective-permute-start(f32[392,128]{1,0:T(8,128)S(1)} %collective-permute-done.2.refs_4_.refs_2_), channel_id=1, source_target_pairs={{0,8},{1,9},{2,10},{3,11},{4,12},{5,13},{6,14},{7,15},{8,0},{9,1},... | collective-permute-start | bytes 602120 | tf_op jit(solution)/shard_map/ppermute | solution.py:681
  26.5 1.2 shard_map.112
  27.7 1.3 %collective-permute-start.7 = (f32[464,128]{1,0:T(8,128)S(1)}, f32[464,128]{1,0:T(8,128)S(1)}, u32[]{:S(2)}, u32[]{:S(2)}) collective-permute-start(f32[464,128]{1,0:T(8,128)S(1)} %get-tuple-element.117.refs_0_), channel_id=1, source_target_pairs={{0,1},{1,0},{2,3},{3,2},{4,5},{5,4},{6,7},{7,6},{8,9},{9,8},{10,11... | collective-permute-start | bytes 712712 | tf_op jit(solution)/shard_map/ppermute | solution.py:681
  29.0 1.2 collective-permute-start.8
  30.2 5.3 %collective-permute-done.8.refs_3_ = f32[416,128]{1,0:T(8,128)S(1)} collective-permute-done((f32[416,128]{1,0:T(8,128)S(1)}, f32[416,128]{1,0:T(8,128)S(1)}, u32[]{:S(2)}, u32[]{:S(2)}) %collective-permute-start.8) | collective-permute-done | bytes 213024 | tf_op jit(solution)/shard_map/ppermute | solution.py:681
  35.6 0.9 collective-permute-start.10
  36.8 2.4 %collective-permute-start.16 = (f32[384,128]{1,0:T(8,128)S(1)}, f32[384,128]{1,0:T(8,128)S(1)}, u32[]{:S(2)}, u32[]{:S(2)}) collective-permute-start(f32[384,128]{1,0:T(8,128)S(1)} %get-tuple-element.132), channel_id=1, source_target_pairs={{0,4},{1,5},{2,6},{3,7},{4,0},{5,1},{6,2},{7,3},{8,12},{9,13},{10,... | collective-permute-start | bytes 589832 | tf_op jit(solution)/shard_map/ppermute | solution.py:681
  39.4 1.2 collective-permute-start.9
  40.6 1.8 %collective-permute-done.11.refs_2_ = f32[384,128]{1,0:T(8,128)S(1)} collective-permute-done((f32[384,128]{1,0:T(8,128)S(1)}, f32[384,128]{1,0:T(8,128)S(1)}, u32[]{:S(2)}, u32[]{:S(2)}) %collective-permute-start.11) | collective-permute-done | bytes 196640 | tf_op jit(solution)/shard_map/ppermute | solution.py:681
  42.4 3.2 %collective-permute-start.12 = (f32[384,128]{1,0:T(8,128)S(1)}, f32[384,128]{1,0:T(8,128)S(1)}, u32[]{:S(2)}, u32[]{:S(2)}) collective-permute-start(f32[384,128]{1,0:T(8,128)S(1)} %get-tuple-element.122.refs_1_), channel_id=1, source_target_pairs={{0,8},{1,9},{2,10},{3,11},{4,12},{5,13},{6,14},{7,15},{8,0},{9,1},... | collective-permute-start | bytes 589832 | tf_op jit(solution)/shard_map/ppermute | solution.py:681
  45.6 1.7 %collective-permute-done.16.refs_0_ = f32[384,128]{1,0:T(8,128)S(1)} collective-permute-done((f32[384,128]{1,0:T(8,128)S(1)}, f32[384,128]{1,0:T(8,128)S(1)}, u32[]{:S(2)}, u32[]{:S(2)}) %collective-permute-start.16) | collective-permute-done | bytes 196640 | tf_op jit(solution)/shard_map/ppermute | solution.py:681
  47.3 7.1 %collective-permute-start.13 = (f32[384,128]{1,0:T(8,128)S(1)}, f32[384,128]{1,0:T(8,128)S(1)}, u32[]{:S(2)}, u32[]{:S(2)}) collective-permute-start(f32[384,128]{1,0:T(8,128)S(1)} %collective-permute-done.11.refs_2_), channel_id=1, source_target_pairs={{0,8},{1,9},{2,10},{3,11},{4,12},{5,13},{6,14},{7,15},{8,0},{9,1},... | collective-permute-start | bytes 589832 | tf_op jit(solution)/shard_map/ppermute | solution.py:681
  54.3 1.3 %collective-permute-done.17.refs_1_ = f32[384,128]{1,0:T(8,128)S(1)} collective-permute-done((f32[384,128]{1,0:T(8,128)S(1)}, f32[384,128]{1,0:T(8,128)S(1)}, u32[]{:S(2)}, u32[]{:S(2)}) %collective-permute-start.17) | collective-permute-done | bytes 196640 | tf_op jit(solution)/shard_map/ppermute | solution.py:681
  55.7 2.2 %collective-permute-start.18 = (f32[384,128]{1,0:T(8,128)S(1)}, f32[384,128]{1,0:T(8,128)S(1)}, u32[]{:S(2)}, u32[]{:S(2)}) collective-permute-start(f32[384,128]{1,0:T(8,128)S(1)} %get-tuple-element.134.refs_2_), channel_id=1, source_target_pairs={{0,8},{1,9},{2,10},{3,11},{4,12},{5,13},{6,14},{7,15},{8,0},{9,1},... | collective-permute-start | bytes 589832 | tf_op jit(solution)/shard_map/ppermute | solution.py:681
  58.4 1.2 shard_map.116
  59.7 1.2 shard_map.120
  60.9 0.7 collective-permute-start.23
  61.7 1.2 collective-permute-start.24
  62.9 4.9 %collective-permute-done.24.refs_3_ = f32[416,128]{1,0:T(8,128)S(1)} collective-permute-done((f32[416,128]{1,0:T(8,128)S(1)}, f32[416,128]{1,0:T(8,128)S(1)}, u32[]{:S(2)}, u32[]{:S(2)}) %collective-permute-start.24) | collective-permute-done | bytes 213024 | tf_op jit(solution)/shard_map/ppermute | solution.py:681
  67.9 1.2 collective-permute-start.25
  70.4 3.9 %collective-permute-done.26.refs_3_ = f32[416,128]{1,0:T(8,128)S(1)} collective-permute-done((f32[416,128]{1,0:T(8,128)S(1)}, f32[416,128]{1,0:T(8,128)S(1)}, u32[]{:S(2)}, u32[]{:S(2)}) %collective-permute-start.26) | collective-permute-done | bytes 213024 | tf_op jit(solution)/shard_map/ppermute | solution.py:681
  75.0 1.1 shard_map.125
  76.1 2.7 %collective-permute-start.31 = (f32[2,392,128]{2,1,0:T(8,128)S(1)}, f32[2,392,128]{2,1,0:T(8,128)S(1)}, u32[]{:S(2)}, u32[]{:S(2)}) collective-permute-start(f32[2,392,128]{2,1,0:T(8,128)S(1)} %get-tuple-element.208), channel_id=1, source_target_pairs={{0,8},{1,9},{2,10},{3,11},{4,12},{5,13},{6,14},{7,15},{8,0},{9,1},... | collective-permute-start | bytes 1204232 | tf_op jit(solution)/shard_map/ppermute | solution.py:681
  79.2 0.8 shard_map.128
  80.1 1.1 shard_map.127
  81.2 2.4 %shard_map.129 = (f32[224,128]{1,0:T(8,128)S(1)}, f32[224,128]{1,0:T(8,128)S(1)}, f32[224,128]{1,0:T(8,128)S(1)}, f32[224,128]{1,0:T(8,128)S(1)}, f32[392,128]{1...) custom-call(f32[576,192]{1,0:T(8,128)S(1)} %get-tuple-element.148.refs_0_, ...), custom_call_target="tpu_custom_call" | custom-call | tf_op jit(solution)/shard_map/pallas_call | solution.py:643
  86.3 1.4 %collective-permute-start.29 = (f32[224,128]{1,0:T(8,128)S(1)}, f32[224,128]{1,0:T(8,128)S(1)}, u32[]{:S(2)}, u32[]{:S(2)}) collective-permute-start(f32[224,128]{1,0:T(8,128)S(1)} %get-tuple-element.200), channel_id=1, source_target_pairs={{0,17},{1,16},{2,19},{3,18},{4,21},{5,20},{6,23},{7,22},{8,25},{9,... | collective-permute-start | bytes 344072 | tf_op jit(solution)/shard_map/ppermute | solution.py:681
  87.8 2.5 %collective-permute-start.21 = (f32[192,128]{1,0:T(8,128)S(1)}, f32[192,128]{1,0:T(8,128)S(1)}, u32[]{:S(2)}, u32[]{:S(2)}) collective-permute-start(f32[192,128]{1,0:T(8,128)S(1)} %get-tuple-element.139), channel_id=1, source_target_pairs={{0,4},{1,5},{2,6},{3,7},{4,0},{5,1},{6,2},{7,3},{8,12},{9,13},{10,... | collective-permute-start | bytes 294920 | tf_op jit(solution)/shard_map/ppermute | solution.py:681
  90.4 1.2 collective-permute-start.35
  91.7 2.3 %collective-permute-start.34 = (f32[392,128]{1,0:T(8,128)S(1)}, f32[392,128]{1,0:T(8,128)S(1)}, u32[]{:S(2)}, u32[]{:S(2)}) collective-permute-start(f32[392,128]{1,0:T(8,128)S(1)} %get-tuple-element.205), channel_id=1, source_target_pairs={{0,2},{1,3},{2,0},{3,1},{4,6},{5,7},{6,4},{7,5},{8,10},{9,11},{10,... | collective-permute-start | bytes 602120 | tf_op jit(solution)/shard_map/ppermute | solution.py:681
  94.0 1.1 collective-permute-start.22
  96.0 6.1 %collective-permute-done.21.refs_2_ = f32[192,128]{1,0:T(8,128)S(1)} collective-permute-done((f32[192,128]{1,0:T(8,128)S(1)}, f32[192,128]{1,0:T(8,128)S(1)}, u32[]{:S(2)}, u32[]{:S(2)}) %collective-permute-start.21) | collective-permute-done | bytes 98336 | tf_op jit(solution)/shard_map/ppermute | solution.py:681
  102.2 4.2 %collective-permute-start.32 = (f32[224,128]{1,0:T(8,128)S(1)}, f32[224,128]{1,0:T(8,128)S(1)}, u32[]{:S(2)}, u32[]{:S(2)}) collective-permute-start(f32[224,128]{1,0:T(8,128)S(1)} %get-tuple-element.211), channel_id=1, source_target_pairs={{0,0},{1,11},{17,21},{16,22},{8,12},{25,23},{9,1},{24,2},{19,3},{1... | collective-permute-start | bytes 344072 | tf_op jit(solution)/shard_map/ppermute | solution.py:681
  106.4 12.7 %collective-permute-done.22.refs_3_ = f32[192,128]{1,0:T(8,128)S(1)} collective-permute-done((f32[192,128]{1,0:T(8,128)S(1)}, f32[192,128]{1,0:T(8,128)S(1)}, u32[]{:S(2)}, u32[]{:S(2)}) %collective-permute-start.22) | collective-permute-done | bytes 98336 | tf_op jit(solution)/shard_map/ppermute | solution.py:681
  119.1 1.3 %collective-permute-start.33 = (f32[48,192]{1,0:T(8,128)S(1)}, f32[48,192]{1,0:T(8,128)S(1)}, u32[]{:S(2)}, u32[]{:S(2)}) collective-permute-start(f32[48,192]{1,0:T(8,128)S(1)} %get-tuple-element.212), channel_id=1, source_target_pairs={{17,1},{16,10},{9,13},{24,22},{3,25},{2,2},{27,5},{26,14},{5,17},{... | collective-permute-start | bytes 110600 | tf_op jit(solution)/shard_map/ppermute | solution.py:681
  120.4 0.8 shard_map.130
  121.2 4.2 %collective-permute-done.33.refs_1_ = f32[48,192]{1,0:T(8,128)S(1)} collective-permute-done((f32[48,192]{1,0:T(8,128)S(1)}, f32[48,192]{1,0:T(8,128)S(1)}, u32[]{:S(2)}, u32[]{:S(2)}) %collective-permute-start.33) | collective-permute-done | bytes 36896 | tf_op jit(solution)/shard_map/ppermute | solution.py:681
  125.4 1.0 shard_map.135
  (78 shorter events, 10.4 us)
Async XLA Ops:
  0.7 0.9 copy-start
  1.6 0.9 copy-start.1
  2.5 0.7 copy-start.4
  3.4 7.0 %collective-permute-start = (f32[392,128]{1,0:T(8,128)S(1)}, f32[392,128]{1,0:T(8,128)S(1)}, u32[]{:S(2)}, u32[]{:S(2)}) collective-permute-start(f32[392,128]{1,0:T(8,128)S(1)} %get-tuple-element.112), channel_id=1, source_target_pairs={{0,2},{1,3},{2,0},{3,1},{4,6},{5,7},{6,4},{7,5},{8,10},{9,11},{10,... | collective-permute-start | bytes 602120 | tf_op jit(solution)/shard_map/ppermute | solution.py:681
  3.5 11.2 %collective-permute-start.1 = (f32[392,128]{1,0:T(8,128)S(1)}, f32[392,128]{1,0:T(8,128)S(1)}, u32[]{:S(2)}, u32[]{:S(2)}) collective-permute-start(f32[392,128]{1,0:T(8,128)S(1)} %get-tuple-element.115), channel_id=1, source_target_pairs={{0,4},{1,5},{2,6},{3,7},{4,0},{5,1},{6,2},{7,3},{8,12},{9,13},{10,... | collective-permute-start | bytes 602120 | tf_op jit(solution)/shard_map/ppermute | solution.py:681
  5.9 17.3 %collective-permute-start.2 = (f32[392,128]{1,0:T(8,128)S(1)}, f32[392,128]{1,0:T(8,128)S(1)}, u32[]{:S(2)}, u32[]{:S(2)}) collective-permute-start(f32[392,128]{1,0:T(8,128)S(1)} %get-tuple-element.116), channel_id=1, source_target_pairs={{0,6},{1,7},{2,4},{3,5},{4,2},{5,3},{6,0},{7,1},{8,14},{9,15},{10,... | collective-permute-start | bytes 602120 | tf_op jit(solution)/shard_map/ppermute | solution.py:681
  6.1 20.3 %collective-permute-start.3 = (f32[392,128]{1,0:T(8,128)S(1)}, f32[392,128]{1,0:T(8,128)S(1)}, u32[]{:S(2)}, u32[]{:S(2)}) collective-permute-start(f32[392,128]{1,0:T(8,128)S(1)} %get-tuple-element.111.refs_1_), channel_id=1, source_target_pairs={{0,8},{1,9},{2,10},{3,11},{4,12},{5,13},{6,14},{7,15},{8,0},{9,1},... | collective-permute-start | bytes 602120 | tf_op jit(solution)/shard_map/ppermute | solution.py:681
  9.0 27.4 %copy-start.2 = (bf16[128,768]{1,0:T(8,128)(2,1)S(1)}, bf16[128,768]{1,0:T(8,128)(2,1)}, u32[]{:S(2)}) copy-start(bf16[128,768]{1,0:T(8,128)(2,1)} %refs_0_.3) | copy-start | bytes 589828
  9.0 27.4 %copy-start.3 = (bf16[128,768]{1,0:T(8,128)(2,1)S(1)}, bf16[128,768]{1,0:T(8,128)(2,1)}, u32[]{:S(2)}) copy-start(bf16[128,768]{1,0:T(8,128)(2,1)} %refs_1_.3) | copy-start | bytes 589828
  10.5 16.0 %collective-permute-start.4 = (f32[392,128]{1,0:T(8,128)S(1)}, f32[392,128]{1,0:T(8,128)S(1)}, u32[]{:S(2)}, u32[]{:S(2)}) collective-permute-start(f32[392,128]{1,0:T(8,128)S(1)} %collective-permute-done.refs_2_), channel_id=1, source_target_pairs={{0,8},{1,9},{2,10},{3,11},{4,12},{5,13},{6,14},{7,15},{8,0},{9,1},... | collective-permute-start | bytes 602120 | tf_op jit(solution)/shard_map/ppermute | solution.py:681
  14.7 11.8 %collective-permute-start.5 = (f32[392,128]{1,0:T(8,128)S(1)}, f32[392,128]{1,0:T(8,128)S(1)}, u32[]{:S(2)}, u32[]{:S(2)}) collective-permute-start(f32[392,128]{1,0:T(8,128)S(1)} %collective-permute-done.1.refs_3_.refs_1_), channel_id=1, source_target_pairs={{0,8},{1,9},{2,10},{3,11},{4,12},{5,13},{6,14},{7,15},{8,0},{9,1},... | collective-permute-start | bytes 602120 | tf_op jit(solution)/shard_map/ppermute | solution.py:681
  23.2 3.2 %collective-permute-start.6 = (f32[392,128]{1,0:T(8,128)S(1)}, f32[392,128]{1,0:T(8,128)S(1)}, u32[]{:S(2)}, u32[]{:S(2)}) collective-permute-start(f32[392,128]{1,0:T(8,128)S(1)} %collective-permute-done.2.refs_4_.refs_2_), channel_id=1, source_target_pairs={{0,8},{1,9},{2,10},{3,11},{4,12},{5,13},{6,14},{7,15},{8,0},{9,1},... | collective-permute-start | bytes 602120 | tf_op jit(solution)/shard_map/ppermute | solution.py:681
  27.7 7.8 %collective-permute-start.7 = (f32[464,128]{1,0:T(8,128)S(1)}, f32[464,128]{1,0:T(8,128)S(1)}, u32[]{:S(2)}, u32[]{:S(2)}) collective-permute-start(f32[464,128]{1,0:T(8,128)S(1)} %get-tuple-element.117.refs_0_), channel_id=1, source_target_pairs={{0,1},{1,0},{2,3},{3,2},{4,5},{5,4},{6,7},{7,6},{8,9},{9,8},{10,11... | collective-permute-start | bytes 712712 | tf_op jit(solution)/shard_map/ppermute | solution.py:681
  29.0 6.5 %collective-permute-start.8 = (f32[416,128]{1,0:T(8,128)S(1)}, f32[416,128]{1,0:T(8,128)S(1)}, u32[]{:S(2)}, u32[]{:S(2)}) collective-permute-start(f32[416,128]{1,0:T(8,128)S(1)} %get-tuple-element.118.refs_2_), channel_id=1, source_target_pairs={{0,16},{1,17},{2,18},{3,19},{4,20},{5,21},{6,22},{7,23},{8,24},{9,... | collective-permute-start | bytes 638984 | tf_op jit(solution)/shard_map/ppermute | solution.py:681
  35.6 22.3 %collective-permute-start.10 = (f32[416,128]{1,0:T(8,128)S(1)}, f32[416,128]{1,0:T(8,128)S(1)}, u32[]{:S(2)}, u32[]{:S(2)}) collective-permute-start(f32[416,128]{1,0:T(8,128)S(1)} %get-tuple-element.120.refs_2_), channel_id=1, source_target_pairs={{0,1},{1,0},{2,3},{3,2},{4,5},{5,4},{6,7},{7,6},{8,9},{9,8},{10,11... | collective-permute-start | bytes 638984 | tf_op jit(solution)/shard_map/ppermute | solution.py:681
  36.6 5.8 %collective-permute-start.11 = (f32[384,128]{1,0:T(8,128)S(1)}, f32[384,128]{1,0:T(8,128)S(1)}, u32[]{:S(2)}, u32[]{:S(2)}) collective-permute-start(f32[384,128]{1,0:T(8,128)S(1)} %get-tuple-element.123), channel_id=1, source_target_pairs={{0,2},{1,3},{2,0},{3,1},{4,6},{5,7},{6,4},{7,5},{8,10},{9,11},{10,... | collective-permute-start | bytes 589832 | tf_op jit(solution)/shard_map/ppermute | solution.py:681
  36.8 10.5 %collective-permute-start.16 = (f32[384,128]{1,0:T(8,128)S(1)}, f32[384,128]{1,0:T(8,128)S(1)}, u32[]{:S(2)}, u32[]{:S(2)}) collective-permute-start(f32[384,128]{1,0:T(8,128)S(1)} %get-tuple-element.132), channel_id=1, source_target_pairs={{0,4},{1,5},{2,6},{3,7},{4,0},{5,1},{6,2},{7,3},{8,12},{9,13},{10,... | collective-permute-start | bytes 589832 | tf_op jit(solution)/shard_map/ppermute | solution.py:681
  39.2 16.5 %collective-permute-start.17 = (f32[384,128]{1,0:T(8,128)S(1)}, f32[384,128]{1,0:T(8,128)S(1)}, u32[]{:S(2)}, u32[]{:S(2)}) collective-permute-start(f32[384,128]{1,0:T(8,128)S(1)} %get-tuple-element.133), channel_id=1, source_target_pairs={{0,6},{1,7},{2,4},{3,5},{4,2},{5,3},{6,0},{7,1},{8,14},{9,15},{10,... | collective-permute-start | bytes 589832 | tf_op jit(solution)/shard_map/ppermute | solution.py:681
  39.4 18.6 %collective-permute-start.9 = (f32[464,128]{1,0:T(8,128)S(1)}, f32[464,128]{1,0:T(8,128)S(1)}, u32[]{:S(2)}, u32[]{:S(2)}) collective-permute-start(f32[464,128]{1,0:T(8,128)S(1)} %get-tuple-element.119.refs_0_), channel_id=1, source_target_pairs={{0,16},{1,17},{2,18},{3,19},{4,20},{5,21},{6,22},{7,23},{8,24},{9,... | collective-permute-start | bytes 712712 | tf_op jit(solution)/shard_map/ppermute | solution.py:681
  42.4 16.0 %collective-permute-start.12 = (f32[384,128]{1,0:T(8,128)S(1)}, f32[384,128]{1,0:T(8,128)S(1)}, u32[]{:S(2)}, u32[]{:S(2)}) collective-permute-start(f32[384,128]{1,0:T(8,128)S(1)} %get-tuple-element.122.refs_1_), channel_id=1, source_target_pairs={{0,8},{1,9},{2,10},{3,11},{4,12},{5,13},{6,14},{7,15},{8,0},{9,1},... | collective-permute-start | bytes 589832 | tf_op jit(solution)/shard_map/ppermute | solution.py:681
  47.3 11.2 %collective-permute-start.13 = (f32[384,128]{1,0:T(8,128)S(1)}, f32[384,128]{1,0:T(8,128)S(1)}, u32[]{:S(2)}, u32[]{:S(2)}) collective-permute-start(f32[384,128]{1,0:T(8,128)S(1)} %collective-permute-done.11.refs_2_), channel_id=1, source_target_pairs={{0,8},{1,9},{2,10},{3,11},{4,12},{5,13},{6,14},{7,15},{8,0},{9,1},... | collective-permute-start | bytes 589832 | tf_op jit(solution)/shard_map/ppermute | solution.py:681
  55.7 4.0 %collective-permute-start.18 = (f32[384,128]{1,0:T(8,128)S(1)}, f32[384,128]{1,0:T(8,128)S(1)}, u32[]{:S(2)}, u32[]{:S(2)}) collective-permute-start(f32[384,128]{1,0:T(8,128)S(1)} %get-tuple-element.134.refs_2_), channel_id=1, source_target_pairs={{0,8},{1,9},{2,10},{3,11},{4,12},{5,13},{6,14},{7,15},{8,0},{9,1},... | collective-permute-start | bytes 589832 | tf_op jit(solution)/shard_map/ppermute | solution.py:681
  57.9 1.8 %collective-permute-start.19 = (f32[384,128]{1,0:T(8,128)S(1)}, f32[384,128]{1,0:T(8,128)S(1)}, u32[]{:S(2)}, u32[]{:S(2)}) collective-permute-start(f32[384,128]{1,0:T(8,128)S(1)} %get-tuple-element.135.refs_3_), channel_id=1, source_target_pairs={{0,8},{1,9},{2,10},{3,11},{4,12},{5,13},{6,14},{7,15},{8,0},{9,1},... | collective-permute-start | bytes 589832 | tf_op jit(solution)/shard_map/ppermute | solution.py:681
  60.9 7.0 %collective-permute-start.23 = (f32[464,128]{1,0:T(8,128)S(1)}, f32[464,128]{1,0:T(8,128)S(1)}, u32[]{:S(2)}, u32[]{:S(2)}) collective-permute-start(f32[464,128]{1,0:T(8,128)S(1)} %get-tuple-element.141.refs_0_), channel_id=1, source_target_pairs={{0,1},{1,0},{2,3},{3,2},{4,5},{5,4},{6,7},{7,6},{8,9},{9,8},{10,11... | collective-permute-start | bytes 712712 | tf_op jit(solution)/shard_map/ppermute | solution.py:681
  61.7 6.1 %collective-permute-start.24 = (f32[416,128]{1,0:T(8,128)S(1)}, f32[416,128]{1,0:T(8,128)S(1)}, u32[]{:S(2)}, u32[]{:S(2)}) collective-permute-start(f32[416,128]{1,0:T(8,128)S(1)} %get-tuple-element.142.refs_2_), channel_id=1, source_target_pairs={{0,16},{1,17},{2,18},{3,19},{4,20},{5,21},{6,22},{7,23},{8,24},{9,... | collective-permute-start | bytes 638984 | tf_op jit(solution)/shard_map/ppermute | solution.py:681
  67.9 6.3 %collective-permute-start.25 = (f32[464,128]{1,0:T(8,128)S(1)}, f32[464,128]{1,0:T(8,128)S(1)}, u32[]{:S(2)}, u32[]{:S(2)}) collective-permute-start(f32[464,128]{1,0:T(8,128)S(1)} %get-tuple-element.143.refs_0_), channel_id=1, source_target_pairs={{0,16},{1,17},{2,18},{3,19},{4,20},{5,21},{6,22},{7,23},{8,24},{9,... | collective-permute-start | bytes 712712 | tf_op jit(solution)/shard_map/ppermute | solution.py:681
  69.2 5.1 %collective-permute-start.26 = (f32[416,128]{1,0:T(8,128)S(1)}, f32[416,128]{1,0:T(8,128)S(1)}, u32[]{:S(2)}, u32[]{:S(2)}) collective-permute-start(f32[416,128]{1,0:T(8,128)S(1)} %get-tuple-element.144.refs_2_), channel_id=1, source_target_pairs={{0,1},{1,0},{2,3},{3,2},{4,5},{5,4},{6,7},{7,6},{8,9},{9,8},{10,11... | collective-permute-start | bytes 638984 | tf_op jit(solution)/shard_map/ppermute | solution.py:681
  76.1 10.2 %collective-permute-start.31 = (f32[2,392,128]{2,1,0:T(8,128)S(1)}, f32[2,392,128]{2,1,0:T(8,128)S(1)}, u32[]{:S(2)}, u32[]{:S(2)}) collective-permute-start(f32[2,392,128]{2,1,0:T(8,128)S(1)} %get-tuple-element.208), channel_id=1, source_target_pairs={{0,8},{1,9},{2,10},{3,11},{4,12},{5,13},{6,14},{7,15},{8,0},{9,1},... | collective-permute-start | bytes 1204232 | tf_op jit(solution)/shard_map/ppermute | solution.py:681
  83.6 4.2 %collective-permute-start.30 = (f32[2,392,128]{2,1,0:T(8,128)S(1)}, f32[2,392,128]{2,1,0:T(8,128)S(1)}, u32[]{:S(2)}, u32[]{:S(2)}) collective-permute-start(f32[2,392,128]{2,1,0:T(8,128)S(1)} %get-tuple-element.203), channel_id=1, source_target_pairs={{0,8},{1,9},{2,10},{3,11},{4,12},{5,13},{6,14},{7,15},{8,0},{9,1},... | collective-permute-start | bytes 1204232 | tf_op jit(solution)/shard_map/ppermute | solution.py:681
  83.7 2.0 %collective-permute-start.14 = (f32[2,192,128]{2,1,0:T(8,128)S(1)}, f32[2,192,128]{2,1,0:T(8,128)S(1)}, u32[]{:S(2)}, u32[]{:S(2)}) collective-permute-start(f32[2,192,128]{2,1,0:T(8,128)S(1)} %get-tuple-element.126), channel_id=1, source_target_pairs={{0,8},{1,9},{2,10},{3,11},{4,12},{5,13},{6,14},{7,15},{8,0},{9,1},... | collective-permute-start | bytes 589832 | tf_op jit(solution)/shard_map/ppermute | solution.py:681
  84.2 2.1 %collective-permute-start.20 = (f32[2,192,128]{2,1,0:T(8,128)S(1)}, f32[2,192,128]{2,1,0:T(8,128)S(1)}, u32[]{:S(2)}, u32[]{:S(2)}) collective-permute-start(f32[2,192,128]{2,1,0:T(8,128)S(1)} %get-tuple-element.138), channel_id=1, source_target_pairs={{0,8},{1,9},{2,10},{3,11},{4,12},{5,13},{6,14},{7,15},{8,0},{9,1},... | collective-permute-start | bytes 589832 | tf_op jit(solution)/shard_map/ppermute | solution.py:681
  84.2 7.3 %collective-permute-start.27 = (f32[224,128]{1,0:T(8,128)S(1)}, f32[224,128]{1,0:T(8,128)S(1)}, u32[]{:S(2)}, u32[]{:S(2)}) collective-permute-start(f32[224,128]{1,0:T(8,128)S(1)} %get-tuple-element.198), channel_id=1, source_target_pairs={{0,1},{1,0},{2,3},{3,2},{4,5},{5,4},{6,7},{7,6},{8,9},{9,8},{10,11... | collective-permute-start | bytes 344072 | tf_op jit(solution)/shard_map/ppermute | solution.py:681
  85.7 6.1 %collective-permute-start.28 = (f32[224,128]{1,0:T(8,128)S(1)}, f32[224,128]{1,0:T(8,128)S(1)}, u32[]{:S(2)}, u32[]{:S(2)}) collective-permute-start(f32[224,128]{1,0:T(8,128)S(1)} %get-tuple-element.199), channel_id=1, source_target_pairs={{0,16},{1,17},{2,18},{3,19},{4,20},{5,21},{6,22},{7,23},{8,24},{9,... | collective-permute-start | bytes 344072 | tf_op jit(solution)/shard_map/ppermute | solution.py:681
  86.2 4.1 %collective-permute-start.15 = (f32[192,128]{1,0:T(8,128)S(1)}, f32[192,128]{1,0:T(8,128)S(1)}, u32[]{:S(2)}, u32[]{:S(2)}) collective-permute-start(f32[192,128]{1,0:T(8,128)S(1)} %get-tuple-element.128), channel_id=1, source_target_pairs={{0,2},{1,3},{2,0},{3,1},{4,6},{5,7},{6,4},{7,5},{8,10},{9,11},{10,... | collective-permute-start | bytes 294920 | tf_op jit(solution)/shard_map/ppermute | solution.py:681
  86.3 7.7 %collective-permute-start.29 = (f32[224,128]{1,0:T(8,128)S(1)}, f32[224,128]{1,0:T(8,128)S(1)}, u32[]{:S(2)}, u32[]{:S(2)}) collective-permute-start(f32[224,128]{1,0:T(8,128)S(1)} %get-tuple-element.200), channel_id=1, source_target_pairs={{0,17},{1,16},{2,19},{3,18},{4,21},{5,20},{6,23},{7,22},{8,25},{9,... | collective-permute-start | bytes 344072 | tf_op jit(solution)/shard_map/ppermute | solution.py:681
  87.8 14.4 %collective-permute-start.21 = (f32[192,128]{1,0:T(8,128)S(1)}, f32[192,128]{1,0:T(8,128)S(1)}, u32[]{:S(2)}, u32[]{:S(2)}) collective-permute-start(f32[192,128]{1,0:T(8,128)S(1)} %get-tuple-element.139), channel_id=1, source_target_pairs={{0,4},{1,5},{2,6},{3,7},{4,0},{5,1},{6,2},{7,3},{8,12},{9,13},{10,... | collective-permute-start | bytes 294920 | tf_op jit(solution)/shard_map/ppermute | solution.py:681
  90.4 35.0 %collective-permute-start.35 = (f32[392,128]{1,0:T(8,128)S(1)}, f32[392,128]{1,0:T(8,128)S(1)}, u32[]{:S(2)}, u32[]{:S(2)}) collective-permute-start(f32[392,128]{1,0:T(8,128)S(1)} %get-tuple-element.209), channel_id=1, source_target_pairs={{0,4},{1,5},{2,6},{3,7},{4,0},{5,1},{6,2},{7,3},{8,12},{9,13},{10,... | collective-permute-start | bytes 602120 | tf_op jit(solution)/shard_map/ppermute | solution.py:681
  91.6 33.8 %collective-permute-start.36 = (f32[392,128]{1,0:T(8,128)S(1)}, f32[392,128]{1,0:T(8,128)S(1)}, u32[]{:S(2)}, u32[]{:S(2)}) collective-permute-start(f32[392,128]{1,0:T(8,128)S(1)} %get-tuple-element.210), channel_id=1, source_target_pairs={{0,6},{1,7},{2,4},{3,5},{4,2},{5,3},{6,0},{7,1},{8,14},{9,15},{10,... | collective-permute-start | bytes 602120 | tf_op jit(solution)/shard_map/ppermute | solution.py:681
  91.7 33.7 %collective-permute-start.34 = (f32[392,128]{1,0:T(8,128)S(1)}, f32[392,128]{1,0:T(8,128)S(1)}, u32[]{:S(2)}, u32[]{:S(2)}) collective-permute-start(f32[392,128]{1,0:T(8,128)S(1)} %get-tuple-element.205), channel_id=1, source_target_pairs={{0,2},{1,3},{2,0},{3,1},{4,6},{5,7},{6,4},{7,5},{8,10},{9,11},{10,... | collective-permute-start | bytes 602120 | tf_op jit(solution)/shard_map/ppermute | solution.py:681
  94.0 25.1 %collective-permute-start.22 = (f32[192,128]{1,0:T(8,128)S(1)}, f32[192,128]{1,0:T(8,128)S(1)}, u32[]{:S(2)}, u32[]{:S(2)}) collective-permute-start(f32[192,128]{1,0:T(8,128)S(1)} %get-tuple-element.140), channel_id=1, source_target_pairs={{0,6},{1,7},{2,4},{3,5},{4,2},{5,3},{6,0},{7,1},{8,14},{9,15},{10,... | collective-permute-start | bytes 294920 | tf_op jit(solution)/shard_map/ppermute | solution.py:681
  102.2 23.2 %collective-permute-start.32 = (f32[224,128]{1,0:T(8,128)S(1)}, f32[224,128]{1,0:T(8,128)S(1)}, u32[]{:S(2)}, u32[]{:S(2)}) collective-permute-start(f32[224,128]{1,0:T(8,128)S(1)} %get-tuple-element.211), channel_id=1, source_target_pairs={{0,0},{1,11},{17,21},{16,22},{8,12},{25,23},{9,1},{24,2},{19,3},{1... | collective-permute-start | bytes 344072 | tf_op jit(solution)/shard_map/ppermute | solution.py:681
  119.1 6.3 %collective-permute-start.33 = (f32[48,192]{1,0:T(8,128)S(1)}, f32[48,192]{1,0:T(8,128)S(1)}, u32[]{:S(2)}, u32[]{:S(2)}) collective-permute-start(f32[48,192]{1,0:T(8,128)S(1)} %get-tuple-element.212), channel_id=1, source_target_pairs={{17,1},{16,10},{9,13},{24,22},{3,25},{2,2},{27,5},{26,14},{5,17},{... | collective-permute-start | bytes 110600 | tf_op jit(solution)/shard_map/ppermute | solution.py:681

commit v5 on v4

--- a/solution.py
+++ b/solution.py
@@ -231,7 +231,7 @@
 def wide_rows(lay):
     step = 2 * SUBLANES
     total = 3 * lay.half
-    return total - total * 17 // 36 // step * step
+    return total - total * 4 // 9 // step * step
 
 
 def pack_parts(lay, grads, extra):
@@ -297,10 +297,11 @@
     return result
 
 
-def spread_rows(lay, with_rates, first, second, *rest):
+def spread_rows(lay, with_rates, both, *rest):
     dim = lay.head_dim
     head_ids = rest[-1]
-    turned = [x.astype(F32).T for x in (first, second)]
+    count = both.shape[0] // 2
+    turned = [x.astype(F32).T for x in (both[:count], both[count:])]
     pieces = [[t[h * dim : (h + 1) * dim] for h in range(lay.heads)] for t in turned]
     if with_rates:
         rates = rest[0]
@@ -714,11 +715,18 @@
     fn = functools.partial
     scale = math.sqrt(queries.shape[0] * lay.devices)
     kv = run(
-        lay, fn(spread_rows, lay, True), (key_rows, value_rows, step_rates.T, head_ids), always=True
+        lay,
+        fn(spread_rows, lay, True),
+        (jnp.concatenate([key_rows, value_rows], 0), step_rates.T, head_ids),
+        always=True,
     )
     kv = over_heads(kv)
     qg = run(
-        lay, fn(spread_rows, lay, False), (queries, out_grad, head_ids), always=True, deps=(kv[1],)
+        lay,
+        fn(spread_rows, lay, False),
+        (jnp.concatenate([queries, out_grad], 0), head_ids),
+        always=True,
+        deps=(kv[1],),
     )
     qg = over_heads(qg, tuple(kv[2:]))
     kv = kv + over_cores(kv)

time: 127 us -> 125 us (0.984)
  the two profiles are of different devices: /device:TPU:9 before, /device:TPU:22 now
where the time goes in v5:
time: 125 us
  waiting for transfers between devices  74.4 us (60%)
  starting transfers between devices  30.6 us (24%)
  Pallas kernels  14.9 us (12%)
  local copies, waits for them, and re-layouts  3.1 us (2%)
    ppermute x37, waiting for transfers between devices, send(): return lax.ppermute(x, AXES, perm)  74.4 us
    ppermute x37, starting transfers between devices, send(): return lax.ppermute(x, AXES, perm)  30.6 us
    pallas_call x24, Pallas kernels, run(): pl.pallas_call(kernel, out_shape=[jax.ShapeDtypeStruct(s.shape, s.dtype)...  14.9 us
  transfers between devices with their start and end apart: 37, of which 15 were waited for; matrix products, arithmetic and copies ran while one was open for 2% of the time, Pallas kernels for 8%

profile of v5, /device:TPU:22, one launch (start us, length us, event | category | flops | bytes accessed | tf_op | source)
XLA Modules:
  0.0 125.2 jit_solution(15721016280017754577)
XLA Ops:
  0.6 1.0 pad_maximum_fusion.1.refs_0_
  1.7 0.7 copy-done
  2.6 1.6 %collective-permute-start = (f32[392,128]{1,0:T(8,128)S(1)}, f32[392,128]{1,0:T(8,128)S(1)}, u32[]{:S(2)}, u32[]{:S(2)}) collective-permute-start(f32[392,128]{1,0:T(8,128)S(1)} %get-tuple-element.112), channel_id=1, source_target_pairs={{0,2},{1,3},{2,0},{3,1},{4,6},{5,7},{6,4},{7,5},{8,10},{9,11},{10,... | collective-permute-start | bytes 602120 | tf_op jit(solution)/shard_map/ppermute | solution.py:682
  4.6 1.6 %collective-permute-start.2 = (f32[392,128]{1,0:T(8,128)S(1)}, f32[392,128]{1,0:T(8,128)S(1)}, u32[]{:S(2)}, u32[]{:S(2)}) collective-permute-start(f32[392,128]{1,0:T(8,128)S(1)} %get-tuple-element.116), channel_id=1, source_target_pairs={{0,6},{1,7},{2,4},{3,5},{4,2},{5,3},{6,0},{7,1},{8,14},{9,15},{10,... | collective-permute-start | bytes 602120 | tf_op jit(solution)/shard_map/ppermute | solution.py:682
  6.2 1.4 %constant_dynamic-slice_fusion.3 = (f32[192,192]{1,0:T(8,128)S(1)}, f32[192,192]{1,0:T(8,128)S(1)}, f32[192,192]{1,0:T(8,128)S(1)}) fusion(f32[192,4608]{1,0:T(8,128)} %param.11, s32[]{:T(128)S(6)} %select_n.18, s32[]{:T(128)S(6)} %select_n.19, s32[]{:T(128)S(6)} %select_n.20), kind=kLoop, calls=%fused_computation.6 | loop fusion | bytes 884748 | tf_op jit(solution)/shard_map/dynamic_slice | solution.py:739
  7.9 3.6 %collective-permute-done.refs_2_ = f32[392,128]{1,0:T(8,128)S(1)} collective-permute-done((f32[392,128]{1,0:T(8,128)S(1)}, f32[392,128]{1,0:T(8,128)S(1)}, u32[]{:S(2)}, u32[]{:S(2)}) %collective-permute-start) | collective-permute-done | bytes 200736 | tf_op jit(solution)/shard_map/ppermute | solution.py:682
  11.5 7.1 %collective-permute-done.1.refs_3_.refs_1_ = f32[392,128]{1,0:T(8,128)S(1)} collective-permute-done((f32[392,128]{1,0:T(8,128)S(1)}, f32[392,128]{1,0:T(8,128)S(1)}, u32[]{:S(2)}, u32[]{:S(2)}) %collective-permute-start.1) | collective-permute-done | bytes 200736 | tf_op jit(solution)/shard_map/ppermute | solution.py:682
  18.6 5.0 %collective-permute-done.2.refs_4_.refs_2_ = f32[392,128]{1,0:T(8,128)S(1)} collective-permute-done((f32[392,128]{1,0:T(8,128)S(1)}, f32[392,128]{1,0:T(8,128)S(1)}, u32[]{:S(2)}, u32[]{:S(2)}) %collective-permute-start.2) | collective-permute-done | bytes 200736 | tf_op jit(solution)/shard_map/ppermute | solution.py:682
  23.5 0.7 constant_dynamic-slice_fusion.refs_3_.refs_4_.refs_8_.refs_2_
  24.3 0.7 shard_map.111
  25.0 1.2 shard_map.112
  27.3 6.6 %collective-permute-done.8.refs_3_ = f32[392,128]{1,0:T(8,128)S(1)} collective-permute-done((f32[392,128]{1,0:T(8,128)S(1)}, f32[392,128]{1,0:T(8,128)S(1)}, u32[]{:S(2)}, u32[]{:S(2)}) %collective-permute-start.8) | collective-permute-done | bytes 200736 | tf_op jit(solution)/shard_map/ppermute | solution.py:682
  33.9 0.8 collective-permute-done.7.refs_1_
  34.7 0.8 collective-permute-start.10
  35.9 1.9 %collective-permute-start.16 = (f32[384,128]{1,0:T(8,128)S(1)}, f32[384,128]{1,0:T(8,128)S(1)}, u32[]{:S(2)}, u32[]{:S(2)}) collective-permute-start(f32[384,128]{1,0:T(8,128)S(1)} %get-tuple-element.132), channel_id=1, source_target_pairs={{0,4},{1,5},{2,6},{3,7},{4,0},{5,1},{6,2},{7,3},{8,12},{9,13},{10,... | collective-permute-start | bytes 589832 | tf_op jit(solution)/shard_map/ppermute | solution.py:682
  37.8 1.6 %collective-permute-start.17 = (f32[384,128]{1,0:T(8,128)S(1)}, f32[384,128]{1,0:T(8,128)S(1)}, u32[]{:S(2)}, u32[]{:S(2)}) collective-permute-start(f32[384,128]{1,0:T(8,128)S(1)} %get-tuple-element.133), channel_id=1, source_target_pairs={{0,6},{1,7},{2,4},{3,5},{4,2},{5,3},{6,0},{7,1},{8,14},{9,15},{10,... | collective-permute-start | bytes 589832 | tf_op jit(solution)/shard_map/ppermute | solution.py:682
  39.9 3.7 %collective-permute-done.11.refs_2_ = f32[384,128]{1,0:T(8,128)S(1)} collective-permute-done((f32[384,128]{1,0:T(8,128)S(1)}, f32[384,128]{1,0:T(8,128)S(1)}, u32[]{:S(2)}, u32[]{:S(2)}) %collective-permute-start.11) | collective-permute-done | bytes 196640 | tf_op jit(solution)/shard_map/ppermute | solution.py:682
  43.6 7.9 %collective-permute-done.16.refs_0_ = f32[384,128]{1,0:T(8,128)S(1)} collective-permute-done((f32[384,128]{1,0:T(8,128)S(1)}, f32[384,128]{1,0:T(8,128)S(1)}, u32[]{:S(2)}, u32[]{:S(2)}) %collective-permute-start.16) | collective-permute-done | bytes 196640 | tf_op jit(solution)/shard_map/ppermute | solution.py:682
  51.5 4.2 %collective-permute-done.17.refs_1_ = f32[384,128]{1,0:T(8,128)S(1)} collective-permute-done((f32[384,128]{1,0:T(8,128)S(1)}, f32[384,128]{1,0:T(8,128)S(1)}, u32[]{:S(2)}, u32[]{:S(2)}) %collective-permute-start.17) | collective-permute-done | bytes 196640 | tf_op jit(solution)/shard_map/ppermute | solution.py:682
  56.7 1.2 shard_map.116
  57.9 1.2 shard_map.120
  59.1 1.6 %collective-permute-start.23 = (f32[488,128]{1,0:T(8,128)S(1)}, f32[488,128]{1,0:T(8,128)S(1)}, u32[]{:S(2)}, u32[]{:S(2)}) collective-permute-start(f32[488,128]{1,0:T(8,128)S(1)} %get-tuple-element.141.refs_0_), channel_id=1, source_target_pairs={{0,1},{1,0},{2,3},{3,2},{4,5},{5,4},{6,7},{7,6},{8,9},{9,8},{10,11... | collective-permute-start | bytes 749576 | tf_op jit(solution)/shard_map/ppermute | solution.py:682
  61.3 6.1 %collective-permute-done.24.refs_3_ = f32[392,128]{1,0:T(8,128)S(1)} collective-permute-done((f32[392,128]{1,0:T(8,128)S(1)}, f32[392,128]{1,0:T(8,128)S(1)}, u32[]{:S(2)}, u32[]{:S(2)}) %collective-permute-start.24) | collective-permute-done | bytes 200736 | tf_op jit(solution)/shard_map/ppermute | solution.py:682
  67.4 0.6 collective-permute-start.25
  68.1 1.3 %collective-permute-start.26 = (f32[392,128]{1,0:T(8,128)S(1)}, f32[392,128]{1,0:T(8,128)S(1)}, u32[]{:S(2)}, u32[]{:S(2)}) collective-permute-start(f32[392,128]{1,0:T(8,128)S(1)} %get-tuple-element.144.refs_2_), channel_id=1, source_target_pairs={{0,1},{1,0},{2,3},{3,2},{4,5},{5,4},{6,7},{7,6},{8,9},{9,8},{10,11... | collective-permute-start | bytes 602120 | tf_op jit(solution)/shard_map/ppermute | solution.py:682
  69.9 3.9 %collective-permute-done.26.refs_3_ = f32[392,128]{1,0:T(8,128)S(1)} collective-permute-done((f32[392,128]{1,0:T(8,128)S(1)}, f32[392,128]{1,0:T(8,128)S(1)}, u32[]{:S(2)}, u32[]{:S(2)}) %collective-permute-start.26) | collective-permute-done | bytes 200736 | tf_op jit(solution)/shard_map/ppermute | solution.py:682
  73.8 0.7 collective-permute-done.25.refs_1_
  74.5 0.7 shard_map.123
  75.2 1.1 shard_map.125
  76.8 0.8 shard_map.128
  77.6 1.1 shard_map.127
  78.7 2.2 %shard_map.129 = (f32[224,128]{1,0:T(8,128)S(1)}, f32[224,128]{1,0:T(8,128)S(1)}, f32[224,128]{1,0:T(8,128)S(1)}, f32[224,128]{1,0:T(8,128)S(1)}, f32[392,128]{1...) custom-call(f32[576,192]{1,0:T(8,128)S(1)} %get-tuple-element.148.refs_0_, ...), custom_call_target="tpu_custom_call" | custom-call | tf_op jit(solution)/shard_map/pallas_call | solution.py:644
  82.0 1.5 %collective-permute-start.27 = (f32[224,128]{1,0:T(8,128)S(1)}, f32[224,128]{1,0:T(8,128)S(1)}, u32[]{:S(2)}, u32[]{:S(2)}) collective-permute-start(f32[224,128]{1,0:T(8,128)S(1)} %get-tuple-element.198), channel_id=1, source_target_pairs={{0,1},{1,0},{2,3},{3,2},{4,5},{5,4},{6,7},{7,6},{8,9},{9,8},{10,11... | collective-permute-start | bytes 344072 | tf_op jit(solution)/shard_map/ppermute | solution.py:682
  83.5 0.7 collective-permute-start.28
  84.3 2.0 %collective-permute-start.29 = (f32[224,128]{1,0:T(8,128)S(1)}, f32[224,128]{1,0:T(8,128)S(1)}, u32[]{:S(2)}, u32[]{:S(2)}) collective-permute-start(f32[224,128]{1,0:T(8,128)S(1)} %get-tuple-element.200), channel_id=1, source_target_pairs={{0,17},{1,16},{2,19},{3,18},{4,21},{5,20},{6,23},{7,22},{8,25},{9,... | collective-permute-start | bytes 344072 | tf_op jit(solution)/shard_map/ppermute | solution.py:682
  86.3 1.9 %collective-permute-start.21 = (f32[192,128]{1,0:T(8,128)S(1)}, f32[192,128]{1,0:T(8,128)S(1)}, u32[]{:S(2)}, u32[]{:S(2)}) collective-permute-start(f32[192,128]{1,0:T(8,128)S(1)} %get-tuple-element.139), channel_id=1, source_target_pairs={{0,4},{1,5},{2,6},{3,7},{4,0},{5,1},{6,2},{7,3},{8,12},{9,13},{10,... | collective-permute-start | bytes 294920 | tf_op jit(solution)/shard_map/ppermute | solution.py:682
  88.3 0.8 collective-permute-done.15.refs_1_
  89.5 1.1 collective-permute-start.36
  90.6 3.0 %collective-permute-start.34 = (f32[392,128]{1,0:T(8,128)S(1)}, f32[392,128]{1,0:T(8,128)S(1)}, u32[]{:S(2)}, u32[]{:S(2)}) collective-permute-start(f32[392,128]{1,0:T(8,128)S(1)} %get-tuple-element.205), channel_id=1, source_target_pairs={{0,2},{1,3},{2,0},{3,1},{4,6},{5,7},{6,4},{7,5},{8,10},{9,11},{10,... | collective-permute-start | bytes 602120 | tf_op jit(solution)/shard_map/ppermute | solution.py:682
  93.5 0.8 collective-permute-start.22
  94.4 0.7 shard_map.131.refs_4_
  95.3 5.4 %collective-permute-done.21.refs_2_ = f32[192,128]{1,0:T(8,128)S(1)} collective-permute-done((f32[192,128]{1,0:T(8,128)S(1)}, f32[192,128]{1,0:T(8,128)S(1)}, u32[]{:S(2)}, u32[]{:S(2)}) %collective-permute-start.21) | collective-permute-done | bytes 98336 | tf_op jit(solution)/shard_map/ppermute | solution.py:682
  100.7 2.7 %collective-permute-start.32 = (f32[224,128]{1,0:T(8,128)S(1)}, f32[224,128]{1,0:T(8,128)S(1)}, u32[]{:S(2)}, u32[]{:S(2)}) collective-permute-start(f32[224,128]{1,0:T(8,128)S(1)} %get-tuple-element.211), channel_id=1, source_target_pairs={{0,0},{1,11},{17,21},{16,22},{8,12},{25,23},{9,1},{24,2},{19,3},{1... | collective-permute-start | bytes 344072 | tf_op jit(solution)/shard_map/ppermute | solution.py:682
  103.4 14.4 %collective-permute-done.22.refs_3_ = f32[192,128]{1,0:T(8,128)S(1)} collective-permute-done((f32[192,128]{1,0:T(8,128)S(1)}, f32[192,128]{1,0:T(8,128)S(1)}, u32[]{:S(2)}, u32[]{:S(2)}) %collective-permute-start.22) | collective-permute-done | bytes 98336 | tf_op jit(solution)/shard_map/ppermute | solution.py:682
  117.8 1.3 %collective-permute-start.33 = (f32[48,192]{1,0:T(8,128)S(1)}, f32[48,192]{1,0:T(8,128)S(1)}, u32[]{:S(2)}, u32[]{:S(2)}) collective-permute-start(f32[48,192]{1,0:T(8,128)S(1)} %get-tuple-element.212), channel_id=1, source_target_pairs={{17,1},{16,10},{9,13},{24,22},{3,25},{2,2},{27,5},{26,14},{5,17},{... | collective-permute-start | bytes 110600 | tf_op jit(solution)/shard_map/ppermute | solution.py:682
  119.1 0.8 shard_map.130
  119.9 4.2 %collective-permute-done.33.refs_1_ = f32[48,192]{1,0:T(8,128)S(1)} collective-permute-done((f32[48,192]{1,0:T(8,128)S(1)}, f32[48,192]{1,0:T(8,128)S(1)}, u32[]{:S(2)}, u32[]{:S(2)}) %collective-permute-start.33) | collective-permute-done | bytes 36896 | tf_op jit(solution)/shard_map/ppermute | solution.py:682
  124.1 1.0 shard_map.135
  (76 shorter events, 7.4 us)
Async XLA Ops:
  1.7 0.7 copy-start
  2.6 8.9 %collective-permute-start = (f32[392,128]{1,0:T(8,128)S(1)}, f32[392,128]{1,0:T(8,128)S(1)}, u32[]{:S(2)}, u32[]{:S(2)}) collective-permute-start(f32[392,128]{1,0:T(8,128)S(1)} %get-tuple-element.112), channel_id=1, source_target_pairs={{0,2},{1,3},{2,0},{3,1},{4,6},{5,7},{6,4},{7,5},{8,10},{9,11},{10,... | collective-permute-start | bytes 602120 | tf_op jit(solution)/shard_map/ppermute | solution.py:682
  4.2 14.3 %collective-permute-start.1 = (f32[392,128]{1,0:T(8,128)S(1)}, f32[392,128]{1,0:T(8,128)S(1)}, u32[]{:S(2)}, u32[]{:S(2)}) collective-permute-start(f32[392,128]{1,0:T(8,128)S(1)} %get-tuple-element.115), channel_id=1, source_target_pairs={{0,4},{1,5},{2,6},{3,7},{4,0},{5,1},{6,2},{7,3},{8,12},{9,13},{10,... | collective-permute-start | bytes 602120 | tf_op jit(solution)/shard_map/ppermute | solution.py:682
  4.6 18.9 %collective-permute-start.2 = (f32[392,128]{1,0:T(8,128)S(1)}, f32[392,128]{1,0:T(8,128)S(1)}, u32[]{:S(2)}, u32[]{:S(2)}) collective-permute-start(f32[392,128]{1,0:T(8,128)S(1)} %get-tuple-element.116), channel_id=1, source_target_pairs={{0,6},{1,7},{2,4},{3,5},{4,2},{5,3},{6,0},{7,1},{8,14},{9,15},{10,... | collective-permute-start | bytes 602120 | tf_op jit(solution)/shard_map/ppermute | solution.py:682
  6.2 18.8 %collective-permute-start.3 = (f32[392,128]{1,0:T(8,128)S(1)}, f32[392,128]{1,0:T(8,128)S(1)}, u32[]{:S(2)}, u32[]{:S(2)}) collective-permute-start(f32[392,128]{1,0:T(8,128)S(1)} %get-tuple-element.111.refs_1_), channel_id=1, source_target_pairs={{0,8},{1,9},{2,10},{3,11},{4,12},{5,13},{6,14},{7,15},{8,0},{9,1},... | collective-permute-start | bytes 602120 | tf_op jit(solution)/shard_map/ppermute | solution.py:682
  7.5 28.0 %copy-start.1 = (bf16[128,768]{1,0:T(8,128)(2,1)S(1)}, bf16[128,768]{1,0:T(8,128)(2,1)}, u32[]{:S(2)}) copy-start(bf16[128,768]{1,0:T(8,128)(2,1)} %param.12) | copy-start | bytes 589828
  7.5 28.0 %copy-start.2 = (bf16[128,768]{1,0:T(8,128)(2,1)S(1)}, bf16[128,768]{1,0:T(8,128)(2,1)}, u32[]{:S(2)}) copy-start(bf16[128,768]{1,0:T(8,128)(2,1)} %param.7) | copy-start | bytes 589828
  11.5 13.5 %collective-permute-start.4 = (f32[392,128]{1,0:T(8,128)S(1)}, f32[392,128]{1,0:T(8,128)S(1)}, u32[]{:S(2)}, u32[]{:S(2)}) collective-permute-start(f32[392,128]{1,0:T(8,128)S(1)} %collective-permute-done.refs_2_), channel_id=1, source_target_pairs={{0,8},{1,9},{2,10},{3,11},{4,12},{5,13},{6,14},{7,15},{8,0},{9,1},... | collective-permute-start | bytes 602120 | tf_op jit(solution)/shard_map/ppermute | solution.py:682
  18.6 6.4 %collective-permute-start.5 = (f32[392,128]{1,0:T(8,128)S(1)}, f32[392,128]{1,0:T(8,128)S(1)}, u32[]{:S(2)}, u32[]{:S(2)}) collective-permute-start(f32[392,128]{1,0:T(8,128)S(1)} %collective-permute-done.1.refs_3_.refs_1_), channel_id=1, source_target_pairs={{0,8},{1,9},{2,10},{3,11},{4,12},{5,13},{6,14},{7,15},{8,0},{9,1},... | collective-permute-start | bytes 602120 | tf_op jit(solution)/shard_map/ppermute | solution.py:682
  23.5 1.5 %collective-permute-start.6 = (f32[392,128]{1,0:T(8,128)S(1)}, f32[392,128]{1,0:T(8,128)S(1)}, u32[]{:S(2)}, u32[]{:S(2)}) collective-permute-start(f32[392,128]{1,0:T(8,128)S(1)} %collective-permute-done.2.refs_4_.refs_2_), channel_id=1, source_target_pairs={{0,8},{1,9},{2,10},{3,11},{4,12},{5,13},{6,14},{7,15},{8,0},{9,1},... | collective-permute-start | bytes 602120 | tf_op jit(solution)/shard_map/ppermute | solution.py:682
  26.2 8.5 %collective-permute-start.7 = (f32[488,128]{1,0:T(8,128)S(1)}, f32[488,128]{1,0:T(8,128)S(1)}, u32[]{:S(2)}, u32[]{:S(2)}) collective-permute-start(f32[488,128]{1,0:T(8,128)S(1)} %get-tuple-element.117.refs_0_), channel_id=1, source_target_pairs={{0,1},{1,0},{2,3},{3,2},{4,5},{5,4},{6,7},{7,6},{8,9},{9,8},{10,11... | collective-permute-start | bytes 749576 | tf_op jit(solution)/shard_map/ppermute | solution.py:682
  26.8 7.1 %collective-permute-start.8 = (f32[392,128]{1,0:T(8,128)S(1)}, f32[392,128]{1,0:T(8,128)S(1)}, u32[]{:S(2)}, u32[]{:S(2)}) collective-permute-start(f32[392,128]{1,0:T(8,128)S(1)} %get-tuple-element.118.refs_2_), channel_id=1, source_target_pairs={{0,16},{1,17},{2,18},{3,19},{4,20},{5,21},{6,22},{7,23},{8,24},{9,... | collective-permute-start | bytes 602120 | tf_op jit(solution)/shard_map/ppermute | solution.py:682
  34.7 21.0 %collective-permute-start.10 = (f32[392,128]{1,0:T(8,128)S(1)}, f32[392,128]{1,0:T(8,128)S(1)}, u32[]{:S(2)}, u32[]{:S(2)}) collective-permute-start(f32[392,128]{1,0:T(8,128)S(1)} %get-tuple-element.120.refs_2_), channel_id=1, source_target_pairs={{0,1},{1,0},{2,3},{3,2},{4,5},{5,4},{6,7},{7,6},{8,9},{9,8},{10,11... | collective-permute-start | bytes 602120 | tf_op jit(solution)/shard_map/ppermute | solution.py:682
  35.8 7.8 %collective-permute-start.11 = (f32[384,128]{1,0:T(8,128)S(1)}, f32[384,128]{1,0:T(8,128)S(1)}, u32[]{:S(2)}, u32[]{:S(2)}) collective-permute-start(f32[384,128]{1,0:T(8,128)S(1)} %get-tuple-element.123), channel_id=1, source_target_pairs={{0,2},{1,3},{2,0},{3,1},{4,6},{5,7},{6,4},{7,5},{8,10},{9,11},{10,... | collective-permute-start | bytes 589832 | tf_op jit(solution)/shard_map/ppermute | solution.py:682
  35.9 15.6 %collective-permute-start.16 = (f32[384,128]{1,0:T(8,128)S(1)}, f32[384,128]{1,0:T(8,128)S(1)}, u32[]{:S(2)}, u32[]{:S(2)}) collective-permute-start(f32[384,128]{1,0:T(8,128)S(1)} %get-tuple-element.132), channel_id=1, source_target_pairs={{0,4},{1,5},{2,6},{3,7},{4,0},{5,1},{6,2},{7,3},{8,12},{9,13},{10,... | collective-permute-start | bytes 589832 | tf_op jit(solution)/shard_map/ppermute | solution.py:682
  37.8 17.9 %collective-permute-start.17 = (f32[384,128]{1,0:T(8,128)S(1)}, f32[384,128]{1,0:T(8,128)S(1)}, u32[]{:S(2)}, u32[]{:S(2)}) collective-permute-start(f32[384,128]{1,0:T(8,128)S(1)} %get-tuple-element.133), channel_id=1, source_target_pairs={{0,6},{1,7},{2,4},{3,5},{4,2},{5,3},{6,0},{7,1},{8,14},{9,15},{10,... | collective-permute-start | bytes 589832 | tf_op jit(solution)/shard_map/ppermute | solution.py:682
  39.3 16.9 %collective-permute-start.9 = (f32[488,128]{1,0:T(8,128)S(1)}, f32[488,128]{1,0:T(8,128)S(1)}, u32[]{:S(2)}, u32[]{:S(2)}) collective-permute-start(f32[488,128]{1,0:T(8,128)S(1)} %get-tuple-element.119.refs_0_), channel_id=1, source_target_pairs={{0,16},{1,17},{2,18},{3,19},{4,20},{5,21},{6,22},{7,23},{8,24},{9,... | collective-permute-start | bytes 749576 | tf_op jit(solution)/shard_map/ppermute | solution.py:682
  43.6 13.1 %collective-permute-start.12 = (f32[384,128]{1,0:T(8,128)S(1)}, f32[384,128]{1,0:T(8,128)S(1)}, u32[]{:S(2)}, u32[]{:S(2)}) collective-permute-start(f32[384,128]{1,0:T(8,128)S(1)} %get-tuple-element.122.refs_1_), channel_id=1, source_target_pairs={{0,8},{1,9},{2,10},{3,11},{4,12},{5,13},{6,14},{7,15},{8,0},{9,1},... | collective-permute-start | bytes 589832 | tf_op jit(solution)/shard_map/ppermute | solution.py:682
  51.5 5.2 %collective-permute-start.13 = (f32[384,128]{1,0:T(8,128)S(1)}, f32[384,128]{1,0:T(8,128)S(1)}, u32[]{:S(2)}, u32[]{:S(2)}) collective-permute-start(f32[384,128]{1,0:T(8,128)S(1)} %collective-permute-done.11.refs_2_), channel_id=1, source_target_pairs={{0,8},{1,9},{2,10},{3,11},{4,12},{5,13},{6,14},{7,15},{8,0},{9,1},... | collective-permute-start | bytes 589832 | tf_op jit(solution)/shard_map/ppermute | solution.py:682
  55.7 2.2 %collective-permute-start.18 = (f32[384,128]{1,0:T(8,128)S(1)}, f32[384,128]{1,0:T(8,128)S(1)}, u32[]{:S(2)}, u32[]{:S(2)}) collective-permute-start(f32[384,128]{1,0:T(8,128)S(1)} %get-tuple-element.134.refs_2_), channel_id=1, source_target_pairs={{0,8},{1,9},{2,10},{3,11},{4,12},{5,13},{6,14},{7,15},{8,0},{9,1},... | collective-permute-start | bytes 589832 | tf_op jit(solution)/shard_map/ppermute | solution.py:682
  55.7 2.2 %collective-permute-start.19 = (f32[384,128]{1,0:T(8,128)S(1)}, f32[384,128]{1,0:T(8,128)S(1)}, u32[]{:S(2)}, u32[]{:S(2)}) collective-permute-start(f32[384,128]{1,0:T(8,128)S(1)} %get-tuple-element.135.refs_3_), channel_id=1, source_target_pairs={{0,8},{1,9},{2,10},{3,11},{4,12},{5,13},{6,14},{7,15},{8,0},{9,1},... | collective-permute-start | bytes 589832 | tf_op jit(solution)/shard_map/ppermute | solution.py:682
  59.1 8.2 %collective-permute-start.23 = (f32[488,128]{1,0:T(8,128)S(1)}, f32[488,128]{1,0:T(8,128)S(1)}, u32[]{:S(2)}, u32[]{:S(2)}) collective-permute-start(f32[488,128]{1,0:T(8,128)S(1)} %get-tuple-element.141.refs_0_), channel_id=1, source_target_pairs={{0,1},{1,0},{2,3},{3,2},{4,5},{5,4},{6,7},{7,6},{8,9},{9,8},{10,11... | collective-permute-start | bytes 749576 | tf_op jit(solution)/shard_map/ppermute | solution.py:682
  60.7 6.7 %collective-permute-start.24 = (f32[392,128]{1,0:T(8,128)S(1)}, f32[392,128]{1,0:T(8,128)S(1)}, u32[]{:S(2)}, u32[]{:S(2)}) collective-permute-start(f32[392,128]{1,0:T(8,128)S(1)} %get-tuple-element.142.refs_2_), channel_id=1, source_target_pairs={{0,16},{1,17},{2,18},{3,19},{4,20},{5,21},{6,22},{7,23},{8,24},{9,... | collective-permute-start | bytes 602120 | tf_op jit(solution)/shard_map/ppermute | solution.py:682
  67.4 7.0 %collective-permute-start.25 = (f32[488,128]{1,0:T(8,128)S(1)}, f32[488,128]{1,0:T(8,128)S(1)}, u32[]{:S(2)}, u32[]{:S(2)}) collective-permute-start(f32[488,128]{1,0:T(8,128)S(1)} %get-tuple-element.143.refs_0_), channel_id=1, source_target_pairs={{0,16},{1,17},{2,18},{3,19},{4,20},{5,21},{6,22},{7,23},{8,24},{9,... | collective-permute-start | bytes 749576 | tf_op jit(solution)/shard_map/ppermute | solution.py:682
  68.1 5.7 %collective-permute-start.26 = (f32[392,128]{1,0:T(8,128)S(1)}, f32[392,128]{1,0:T(8,128)S(1)}, u32[]{:S(2)}, u32[]{:S(2)}) collective-permute-start(f32[392,128]{1,0:T(8,128)S(1)} %get-tuple-element.144.refs_2_), channel_id=1, source_target_pairs={{0,1},{1,0},{2,3},{3,2},{4,5},{5,4},{6,7},{7,6},{8,9},{9,8},{10,11... | collective-permute-start | bytes 602120 | tf_op jit(solution)/shard_map/ppermute | solution.py:682
  76.2 8.1 %collective-permute-start.31 = (f32[2,392,128]{2,1,0:T(8,128)S(1)}, f32[2,392,128]{2,1,0:T(8,128)S(1)}, u32[]{:S(2)}, u32[]{:S(2)}) collective-permute-start(f32[2,392,128]{2,1,0:T(8,128)S(1)} %get-tuple-element.208), channel_id=1, source_target_pairs={{0,8},{1,9},{2,10},{3,11},{4,12},{5,13},{6,14},{7,15},{8,0},{9,1},... | collective-permute-start | bytes 1204232 | tf_op jit(solution)/shard_map/ppermute | solution.py:682
  80.9 5.4 %collective-permute-start.30 = (f32[2,392,128]{2,1,0:T(8,128)S(1)}, f32[2,392,128]{2,1,0:T(8,128)S(1)}, u32[]{:S(2)}, u32[]{:S(2)}) collective-permute-start(f32[2,392,128]{2,1,0:T(8,128)S(1)} %get-tuple-element.203), channel_id=1, source_target_pairs={{0,8},{1,9},{2,10},{3,11},{4,12},{5,13},{6,14},{7,15},{8,0},{9,1},... | collective-permute-start | bytes 1204232 | tf_op jit(solution)/shard_map/ppermute | solution.py:682
  81.5 2.0 %collective-permute-start.14 = (f32[2,192,128]{2,1,0:T(8,128)S(1)}, f32[2,192,128]{2,1,0:T(8,128)S(1)}, u32[]{:S(2)}, u32[]{:S(2)}) collective-permute-start(f32[2,192,128]{2,1,0:T(8,128)S(1)} %get-tuple-element.126), channel_id=1, source_target_pairs={{0,8},{1,9},{2,10},{3,11},{4,12},{5,13},{6,14},{7,15},{8,0},{9,1},... | collective-permute-start | bytes 589832 | tf_op jit(solution)/shard_map/ppermute | solution.py:682
  81.6 2.7 %collective-permute-start.20 = (f32[2,192,128]{2,1,0:T(8,128)S(1)}, f32[2,192,128]{2,1,0:T(8,128)S(1)}, u32[]{:S(2)}, u32[]{:S(2)}) collective-permute-start(f32[2,192,128]{2,1,0:T(8,128)S(1)} %get-tuple-element.138), channel_id=1, source_target_pairs={{0,8},{1,9},{2,10},{3,11},{4,12},{5,13},{6,14},{7,15},{8,0},{9,1},... | collective-permute-start | bytes 589832 | tf_op jit(solution)/shard_map/ppermute | solution.py:682
  82.0 7.5 %collective-permute-start.27 = (f32[224,128]{1,0:T(8,128)S(1)}, f32[224,128]{1,0:T(8,128)S(1)}, u32[]{:S(2)}, u32[]{:S(2)}) collective-permute-start(f32[224,128]{1,0:T(8,128)S(1)} %get-tuple-element.198), channel_id=1, source_target_pairs={{0,1},{1,0},{2,3},{3,2},{4,5},{5,4},{6,7},{7,6},{8,9},{9,8},{10,11... | collective-permute-start | bytes 344072 | tf_op jit(solution)/shard_map/ppermute | solution.py:682
  83.5 7.1 %collective-permute-start.28 = (f32[224,128]{1,0:T(8,128)S(1)}, f32[224,128]{1,0:T(8,128)S(1)}, u32[]{:S(2)}, u32[]{:S(2)}) collective-permute-start(f32[224,128]{1,0:T(8,128)S(1)} %get-tuple-element.199), channel_id=1, source_target_pairs={{0,16},{1,17},{2,18},{3,19},{4,20},{5,21},{6,22},{7,23},{8,24},{9,... | collective-permute-start | bytes 344072 | tf_op jit(solution)/shard_map/ppermute | solution.py:682
  84.2 4.9 %collective-permute-start.15 = (f32[192,128]{1,0:T(8,128)S(1)}, f32[192,128]{1,0:T(8,128)S(1)}, u32[]{:S(2)}, u32[]{:S(2)}) collective-permute-start(f32[192,128]{1,0:T(8,128)S(1)} %get-tuple-element.128), channel_id=1, source_target_pairs={{0,2},{1,3},{2,0},{3,1},{4,6},{5,7},{6,4},{7,5},{8,10},{9,11},{10,... | collective-permute-start | bytes 294920 | tf_op jit(solution)/shard_map/ppermute | solution.py:682
  84.3 9.2 %collective-permute-start.29 = (f32[224,128]{1,0:T(8,128)S(1)}, f32[224,128]{1,0:T(8,128)S(1)}, u32[]{:S(2)}, u32[]{:S(2)}) collective-permute-start(f32[224,128]{1,0:T(8,128)S(1)} %get-tuple-element.200), channel_id=1, source_target_pairs={{0,17},{1,16},{2,19},{3,18},{4,21},{5,20},{6,23},{7,22},{8,25},{9,... | collective-permute-start | bytes 344072 | tf_op jit(solution)/shard_map/ppermute | solution.py:682
  86.3 14.3 %collective-permute-start.21 = (f32[192,128]{1,0:T(8,128)S(1)}, f32[192,128]{1,0:T(8,128)S(1)}, u32[]{:S(2)}, u32[]{:S(2)}) collective-permute-start(f32[192,128]{1,0:T(8,128)S(1)} %get-tuple-element.139), channel_id=1, source_target_pairs={{0,4},{1,5},{2,6},{3,7},{4,0},{5,1},{6,2},{7,3},{8,12},{9,13},{10,... | collective-permute-start | bytes 294920 | tf_op jit(solution)/shard_map/ppermute | solution.py:682
  89.1 35.0 %collective-permute-start.35 = (f32[392,128]{1,0:T(8,128)S(1)}, f32[392,128]{1,0:T(8,128)S(1)}, u32[]{:S(2)}, u32[]{:S(2)}) collective-permute-start(f32[392,128]{1,0:T(8,128)S(1)} %get-tuple-element.209), channel_id=1, source_target_pairs={{0,4},{1,5},{2,6},{3,7},{4,0},{5,1},{6,2},{7,3},{8,12},{9,13},{10,... | collective-permute-start | bytes 602120 | tf_op jit(solution)/shard_map/ppermute | solution.py:682
  89.5 34.6 %collective-permute-start.36 = (f32[392,128]{1,0:T(8,128)S(1)}, f32[392,128]{1,0:T(8,128)S(1)}, u32[]{:S(2)}, u32[]{:S(2)}) collective-permute-start(f32[392,128]{1,0:T(8,128)S(1)} %get-tuple-element.210), channel_id=1, source_target_pairs={{0,6},{1,7},{2,4},{3,5},{4,2},{5,3},{6,0},{7,1},{8,14},{9,15},{10,... | collective-permute-start | bytes 602120 | tf_op jit(solution)/shard_map/ppermute | solution.py:682
  90.6 33.6 %collective-permute-start.34 = (f32[392,128]{1,0:T(8,128)S(1)}, f32[392,128]{1,0:T(8,128)S(1)}, u32[]{:S(2)}, u32[]{:S(2)}) collective-permute-start(f32[392,128]{1,0:T(8,128)S(1)} %get-tuple-element.205), channel_id=1, source_target_pairs={{0,2},{1,3},{2,0},{3,1},{4,6},{5,7},{6,4},{7,5},{8,10},{9,11},{10,... | collective-permute-start | bytes 602120 | tf_op jit(solution)/shard_map/ppermute | solution.py:682
  93.5 24.3 %collective-permute-start.22 = (f32[192,128]{1,0:T(8,128)S(1)}, f32[192,128]{1,0:T(8,128)S(1)}, u32[]{:S(2)}, u32[]{:S(2)}) collective-permute-start(f32[192,128]{1,0:T(8,128)S(1)} %get-tuple-element.140), channel_id=1, source_target_pairs={{0,6},{1,7},{2,4},{3,5},{4,2},{5,3},{6,0},{7,1},{8,14},{9,15},{10,... | collective-permute-start | bytes 294920 | tf_op jit(solution)/shard_map/ppermute | solution.py:682
  100.7 23.5 %collective-permute-start.32 = (f32[224,128]{1,0:T(8,128)S(1)}, f32[224,128]{1,0:T(8,128)S(1)}, u32[]{:S(2)}, u32[]{:S(2)}) collective-permute-start(f32[224,128]{1,0:T(8,128)S(1)} %get-tuple-element.211), channel_id=1, source_target_pairs={{0,0},{1,11},{17,21},{16,22},{8,12},{25,23},{9,1},{24,2},{19,3},{1... | collective-permute-start | bytes 344072 | tf_op jit(solution)/shard_map/ppermute | solution.py:682
  117.8 6.3 %collective-permute-start.33 = (f32[48,192]{1,0:T(8,128)S(1)}, f32[48,192]{1,0:T(8,128)S(1)}, u32[]{:S(2)}, u32[]{:S(2)}) collective-permute-start(f32[48,192]{1,0:T(8,128)S(1)} %get-tuple-element.212), channel_id=1, source_target_pairs={{17,1},{16,10},{9,13},{24,22},{3,25},{2,2},{27,5},{26,14},{5,17},{... | collective-permute-start | bytes 110600 | tf_op jit(solution)/shard_map/ppermute | solution.py:682
